TPU v7x, 512 devices: a whole 4x8x8 slice. The times are simulated.
512 devices in a mesh: dom: 64 (over x, y, core), head: 8 (over z).
Axes of the slice: x: 4, y: 8, z: 8, core: 2. Of those that a mesh axis runs over, the one named last changes fastest.
Arguments:
- node_feats: bfloat16 [262144, 256], P(('dom', 'head'))
- w_qkv: bfloat16 [3, 256, 256], replicated, may hold values from -0.375 to 0.375
- w_graph: bfloat16 [256, 256], replicated, may hold values from -0.375 to 0.375
- ln_gain: float32 [256], replicated, may hold values from 0.1 to 1.9
- out_grad: bfloat16 [262144, 256], P(('dom', 'head')), may hold values from -6 to 6
- part_counts: int32 [512], P(('dom', 'head')), may hold values from 128 to 512, as said below
- send_rows: int32 [512, 2, 64], P(('dom', 'head')), may hold values from 0 to 511, as said below
- neighbours: int32 [262144, 16], P(('dom', 'head')), may hold values from 0 to 639, as said below
- neighbour_counts: int32 [262144], P(('dom', 'head')), may hold values from 1 to 16
Outputs:
- node_out: bfloat16 [262144, 256], P(('dom', 'head'))
- qkv_grad: float32 [3, 256, 256], replicated
- graph_grad: float32 [256, 256], replicated
Inputs may be any that keep to these rules, and one draw needn't show every extreme that they name: `part_counts`: some partition is full in every draw. `send_rows`: every index is below the sending partition's count. `neighbours`: an index below 512 names a live row of the node's own partition; 512 + j names row j received from the partition before, 576 + j row j from the one after; the first partition never names rows from before, the last never rows from after.
All inputs are finite; a program needn't handle non-finite values.
Results may differ from a plain program's by a relative error of at most 0.0005.
The roundings to bfloat16 on the way count: a program that leaves them out, or rounds other values in their place, can miss the bound.
Values may be sent and summed in bfloat16 or wider, within the bound.
No kernel may reach another device: no remote copies, remote signals or barrier semaphores. Data moves between devices by JAX's collectives and lax.ppermute only.
A program may use at most 64 MiB of HBM per device.

v0:
```python
import jax
import jax.numpy as jnp
from jax import lax
from jax.sharding import PartitionSpec as P

D = 256
DH = 32


highest = lax.Precision.HIGHEST


def extended_2(shard, sides, width):
    for axis, dim in sides:
        size, length = (lax.axis_size(axis), shard.shape[dim])
        up = [(i, (i + 1) % size) for i in range(size - 1)]
        down = [(j, i) for i, j in up]
        last = lax.slice_in_dim(shard, length - width, length, axis=dim)
        initial = lax.slice_in_dim(shard, 0, width, axis=dim)
        before = lax.ppermute(last, axis, up)
        after = lax.ppermute(initial, axis, down)
        shard = jnp.concatenate([before, shard, after], axis=dim)
    return shard


def feature_map(value):
    return jnp.where(value > 0, value + 1.0, jnp.exp(jnp.minimum(value, 0.0)))


def feature_slope(value):
    return jnp.where(value > 0, jnp.ones_like(value), jnp.exp(jnp.minimum(value, 0.0)))


def gather_packs(source, send_rows):
    return source[send_rows.reshape(-1)]


def combine_rows(source, beside_all, neighbours, neighbour_counts):
    total_rows = source.shape[0]
    width = source.shape[1]
    rim = beside_all.shape[0] // 4
    block = min(256, total_rows)
    extended = jnp.concatenate([source, beside_all[:rim], beside_all[3 * rim :]], axis=0)

    def one_block(pieces):
        nbr_block, count_block, own_block = pieces
        picked = extended[nbr_block].astype(jnp.float32)
        slots = jnp.arange(nbr_block.shape[1], dtype=jnp.int32)
        usable = slots[None, :] < count_block[:, None]
        summed = jnp.sum(jnp.where(usable[:, :, None], picked, jnp.zeros_like(picked)), axis=1)
        total = own_block.astype(jnp.float32) + summed
        return (total / (1.0 + count_block.astype(jnp.float32))[:, None]).astype(jnp.bfloat16)

    result = lax.map(
        one_block,
        (
            neighbours.reshape(total_rows // block, block, -1),
            neighbour_counts.reshape(total_rows // block, block),
            source.reshape(total_rows // block, block, width),
        ),
    )
    return result.reshape(total_rows, width)


def local(
    node_feats,
    w_qkv,
    w_graph,
    ln_gain,
    out_grad,
    part_counts,
    send_rows,
    neighbours,
    neighbour_counts,
):
    rows = node_feats.shape[0]
    width = node_feats.shape[1]
    head_count = width // DH
    halo_rows = send_rows.shape[2]
    alive_rows = (jnp.arange(rows, dtype=jnp.int32) < part_counts[0]).astype(jnp.float32)
    own_count = part_counts.astype(jnp.float32)
    live_sum = lax.psum(own_count, ("dom", "head"))
    beside_all = extended_2(gather_packs(node_feats, send_rows), ((("dom", "head"), 0),), halo_rows)
    agg = combine_rows(node_feats, beside_all, neighbours, neighbour_counts)
    projected = jnp.einsum("rd,kdc->krc", node_feats, w_qkv, preferred_element_type=jnp.float32)
    queries, key_rows, value_rows = (projected[0], projected[1], projected[2])
    query_map = feature_map(queries).reshape(rows, head_count, DH)
    key_map = feature_map(key_rows).reshape(rows, head_count, DH) * alive_rows[:, None, None]
    value_heads = value_rows.reshape(rows, head_count, DH)
    kv_part = jnp.einsum("rhi,rhj->hij", key_map, value_heads, precision=highest)
    ks_part = jnp.sum(key_map, axis=0)
    kv_sum, ks_sum = lax.psum((kv_part, ks_part), ("dom", "head"))
    factor = 1.0 / (DH * live_sum[0])
    numer = value_heads + factor * jnp.einsum("rhi,hij->rhj", query_map, kv_sum, precision=highest)
    denom = 1.0 + factor * jnp.sum(query_map * ks_sum[None], axis=-1)
    attn = numer / denom[:, :, None]
    graph = jnp.dot(agg, w_graph, preferred_element_type=jnp.float32)
    mixed = 0.5 * attn.reshape(rows, width) + 0.5 * graph
    mean = jnp.sum(mixed, -1, keepdims=True) / D
    spread = jnp.sum(mixed * mixed, -1, keepdims=True) / D - mean * mean
    rstd = lax.rsqrt(spread + 1e-05)
    normed = (mixed - mean) * rstd
    node_out = (normed * ln_gain[None] * alive_rows[:, None]).astype(jnp.bfloat16)
    dnormed = out_grad.astype(jnp.float32) * alive_rows[:, None] * ln_gain[None]
    dmixed = rstd * (
        dnormed
        - jnp.sum(dnormed, -1, keepdims=True) / D
        - normed * jnp.sum(dnormed * normed, -1, keepdims=True) / D
    )
    dgraph = (0.5 * dmixed).astype(jnp.bfloat16)
    graph_term = jnp.einsum("rd,rc->dc", agg, dgraph, preferred_element_type=jnp.float32)
    dattn = (0.5 * dmixed).reshape(rows, head_count, DH)
    dnum = dattn / denom[:, :, None]
    dden = -jnp.sum(dattn * attn, -1) / denom
    dkv_part = factor * jnp.einsum("rhi,rhj->hij", query_map, dnum, precision=highest)
    dks_part = factor * jnp.sum(query_map * dden[:, :, None], axis=0)
    dkv_sum, dks_sum = lax.psum((dkv_part, dks_part), ("dom", "head"))
    dquery = factor * (
        jnp.einsum("rhj,hij->rhi", dnum, kv_sum, precision=highest)
        + dden[:, :, None] * ks_sum[None]
    )
    dvalue = dnum + jnp.einsum("rhi,hij->rhj", key_map, dkv_sum, precision=highest)
    dkey = (
        jnp.einsum("rhj,hij->rhi", value_heads, dkv_sum, precision=highest) + dks_sum[None]
    ) * alive_rows[:, None, None]
    dprojs = jnp.stack(
        [
            dquery.reshape(rows, width) * feature_slope(queries),
            dkey.reshape(rows, width) * feature_slope(key_rows),
            dvalue.reshape(rows, width),
        ]
    ).astype(jnp.bfloat16)
    qkv_term = jnp.einsum("rd,krc->kdc", node_feats, dprojs, preferred_element_type=jnp.float32)
    qkv_total, graph_total = lax.psum((qkv_term, graph_term), ("dom", "head"))
    loss_scale = lax.rsqrt(live_sum[0])
    return (node_out, qkv_total * loss_scale, graph_total * loss_scale)


def solution(mesh):
    return jax.shard_map(
        local,
        mesh=mesh,
        in_specs=(
            P(("dom", "head"), None),
            P(),
            P(),
            P(),
            P(("dom", "head"), None),
            P(("dom", "head")),
            P(("dom", "head"), None, None),
            P(("dom", "head"), None),
            P(("dom", "head")),
        ),
        out_specs=(P(("dom", "head"), None), P(), P()),
        check_vma=False,
    )
```

profile of v0, /device:TPU:1, one launch (start us, length us, event | category | flops | bytes accessed | tf_op | source)
XLA Modules:
  0.0 556.4 jit_solution(1884374837968277647)
XLA Ops:
  7.2 0.0 copy-start
  7.2 0.0 all-reduce.5.cloned.1.call-start
  7.2 0.8 reshape.216
  8.0 1.7 gather_fusion.1
  9.8 4.8 collective-permute-start
  14.6 9.1 %collective-permute-start.1 = (bf16[64,256]{1,0:T(8,128)(2,1)S(1)}, bf16[64,256]{1,0:T(8,128)(2,1)S(1)}, u32[]{:S(2)}, u32[]{:S(2)}) collective-permute-start(bf16[64,256]{1,0:T(8,128)(2,1)S(1)} %get-tuple-element.86), channel_id=1, source_target_pairs={{1,0},{2,1},{3,2},{4,3},{5,4},{6,5},{7,6},{8,7},{9,8},{10,9},{11,1... | collective-permute-start | bytes 98312 | tf_op jit(solution)/shard_map/ppermute | solution.py:21
  24.4 0.0 copy-done
  24.4 1.4 convolution_bitcast_fusion
  25.8 1.1 copy-done.1
  27.0 1.0 add_select_fusion
  28.0 0.0 copy-start.25
  28.0 0.0 copy-start.19
  28.0 0.1 reduce_sum.86
  28.1 0.6 fusion.23
  28.7 98.5 %all-reduce.1 = (f32[8,32,32]{2,1,0:T(8,128)S(1)}, f32[8,32]{1,0:T(8,128)S(1)}, f32[1]{0:T(128)}) all-reduce(f32[8,32,32]{2,1,0:T(8,128)S(1)} %fusion.23, f32[8,32]{1,0:T(8,128)S(1)} %reduce_sum.86, f32[1]{0:T(128)S(6)} %convert_element_type.42), channel_id=1, replica_groups=mesh['dom'=64,'head'=8] {'dom','head'}, use_global_device_ids=true, to_apply=%region_1.2 | all-reduce | flops 8449 | bytes 67592 | tf_op jit(solution)/shard_map/psum | solution.py:92
  127.8 0.1 multiply_reduce_fusion.3
  128.0 1.4 fusion.11
  129.5 0.0 copy-done.22
  129.5 0.8 copy.21
  130.3 0.1 copy.28
  130.5 0.0 collective-permute-done
  130.5 0.0 collective-permute-done.1
  130.5 0.0 copy-start.20
  130.5 0.0 copy-done.26
  130.5 37.3 %while.10 = (s32[]{:T(128)}, bf16[2,256,256]{2,1,0:T(8,128)(2,1)}, bf16[2,256,256]{2,1,0:T(8,128)(2,1)S(1)}, s32[2,256]{1,0:T(2,128)S(1)}, s32[2,256,16]{2,1,0:T...) while((s32[]{:T(128)}, bf16[2,256,256]{2,1,0:T(8,128)(2,1)}, bf16[2,256,256]{2,1,0:T(8,128)(2,1)S(1)}, ...), condition=%wide.region_7.8_spmd, body=%wide.region_5.7_spmd.sunk | while | flops 3363330 | bytes 9304217 | solution.py:54
  130.6 0.1 iota_compare_fusion.3
  130.7 0.1 reshape.245
  130.8 14.6 %gather_fusion = bf16[4096,256]{1,0:T(8,128)(2,1)S(1)} fusion(bf16[640,256]{1,0:T(8,128)(2,1)S(1)} %get-tuple-element.146, s32[4096]{0:T(1024)S(1)} %broadcast_clamp_fusion.2), kind=kCustom, calls=%fused_computation.clone.1 | custom fusion | bytes 4210688 | tf_op jit(solution)/shard_map/while/body/eval_jaxpr/gather | solution.py:47
  145.5 0.0 copy-start.13
  145.5 2.9 fusion.50
  148.4 0.1 fusion.51
  148.5 0.0 copy-start.14
  148.5 0.7 copy-done.14
  149.2 0.1 iota_compare_fusion.3
  149.3 0.1 reshape.245
  149.5 14.6 %gather_fusion = bf16[4096,256]{1,0:T(8,128)(2,1)S(1)} fusion(bf16[640,256]{1,0:T(8,128)(2,1)S(1)} %get-tuple-element.146, s32[4096]{0:T(1024)S(1)} %broadcast_clamp_fusion.2), kind=kCustom, calls=%fused_computation.clone.1 | custom fusion | bytes 4210688 | tf_op jit(solution)/shard_map/while/body/eval_jaxpr/gather | solution.py:47
  164.1 0.0 copy-start.13
  164.1 2.9 fusion.50
  167.0 0.0 copy-done.13
  167.0 0.1 fusion.51
  167.1 0.0 copy-start.14
  167.1 0.7 copy-done.14
  167.8 0.0 copy-start.15
  167.8 1.5 fusion.34
  169.4 1.2 fusion.21
  170.7 0.3 multiply_reduce_fusion
  171.0 0.0 copy-start.11
  171.0 1.0 fusion.27
  172.0 0.1 fusion.19
  172.1 1.3 convolution_multiply_fusion.1
  173.4 1.4 fusion.6
  174.8 0.1 mul.233
  174.9 94.4 %all-reduce = (f32[8,32,32]{2,1,0:T(8,128)}, f32[8,32]{1,0:T(8,128)S(1)}) all-reduce(f32[8,32,32]{2,1,0:T(8,128)} %convolution_multiply_fusion.1, f32[8,32]{1,0:T(8,128)S(1)} %mul.233), channel_id=1, replica_groups=mesh['dom'=64,'head'=8] {'dom','head'}, use_global_device_ids=true, to_apply=%region_13.14 | all-reduce | flops 8448 | bytes 67584 | tf_op jit(solution)/shard_map/psum | solution.py:117
  269.3 0.0 copy-done.10
  269.3 1.8 fusion.12
  271.1 1.5 fusion.8
  272.6 0.3 fusion.20
  272.9 1.3 convolution_bitcast_fusion.1
  274.2 0.0 all-reduce.5.cloned.1.call-update
  274.9 0.8 copy.23
  275.7 269.8 %all-reduce.5.cloned.1.call-done = (f32[3,256,256]{1,2,0:T(8,128)}, f32[256,256]{1,0:T(8,128)}) async-done(((f32[3,256,256]{1,2,0:T(8,128)}, f32[256,256]{1,0:T(8,128)}), (f32[3,256,256]{1,2,0:T(8,128)}, f32[256,256]{1,0:T(8,128)})) %all-reduce.5.cloned.1.call-update) | async-done | bytes 1048592 | tf_op jit(solution)/shard_map/psum | solution.py:134
  545.6 1.2 broadcast_multiply_fusion
  546.8 1.7 broadcast_multiply_fusion.1
  548.4 1.1 copy.24
  (62 shorter events, 0.3 us)
Async XLA Ops:
  7.2 17.3 %copy-start = (bf16[3,256,256]{2,1,0:T(8,128)(2,1)S(1)}, bf16[3,256,256]{2,1,0:T(8,128)(2,1)}, u32[]{:S(2)}) copy-start(bf16[3,256,256]{2,1,0:T(8,128)(2,1)} %param.12) | copy-start | bytes 1179652
  7.2 538.4 %all-reduce.5.cloned.1.call-start = ((), (), s32[]{:S(2)}) async-start(), calls=%async_computation | async-start | bytes 2097152 | tf_op jit(solution)/shard_map/psum | solution.py:134
  9.8 120.7 %collective-permute-start = (bf16[64,256]{1,0:T(8,128)(2,1)S(1)}, bf16[64,256]{1,0:T(8,128)(2,1)S(1)}, u32[]{:S(2)}, u32[]{:S(2)}) collective-permute-start(bf16[64,256]{1,0:T(8,128)(2,1)S(1)} %get-tuple-element.85), channel_id=1, source_target_pairs={{0,1},{1,2},{2,3},{3,4},{4,5},{5,6},{6,7},{7,8},{8,9},{9,10},{10,1... | collective-permute-start | bytes 98312 | tf_op jit(solution)/shard_map/ppermute | solution.py:20
  14.6 115.9 %collective-permute-start.1 = (bf16[64,256]{1,0:T(8,128)(2,1)S(1)}, bf16[64,256]{1,0:T(8,128)(2,1)S(1)}, u32[]{:S(2)}, u32[]{:S(2)}) collective-permute-start(bf16[64,256]{1,0:T(8,128)(2,1)S(1)} %get-tuple-element.86), channel_id=1, source_target_pairs={{1,0},{2,1},{3,2},{4,3},{5,4},{6,5},{7,6},{8,7},{9,8},{10,9},{11,1... | collective-permute-start | bytes 98312 | tf_op jit(solution)/shard_map/ppermute | solution.py:21
  25.8 1.1 copy-start.1
  28.0 102.3 %copy-start.4 = (f32[1,512,256]{1,2,0:T(8,128)}, f32[1,512,256]{1,2,0:T(8,128)S(1)}, u32[]{:S(2)}) copy-start(f32[1,512,256]{1,2,0:T(8,128)S(1)} %get-tuple-element.83) | copy-start | bytes 1572868
  28.0 102.3 %copy-start.6 = (f32[1,512,256]{1,2,0:T(8,128)}, f32[1,512,256]{1,2,0:T(8,128)S(1)}, u32[]{:S(2)}) copy-start(f32[1,512,256]{1,2,0:T(8,128)S(1)} %get-tuple-element.73) | copy-start | bytes 1572868
  28.0 102.3 %copy-start.9 = (f32[1,512,256]{1,2,0:T(8,128)}, f32[1,512,256]{1,2,0:T(8,128)S(1)}, u32[]{:S(2)}) copy-start(f32[1,512,256]{1,2,0:T(8,128)S(1)} %get-tuple-element.81) | copy-start | bytes 1572868
  28.0 101.5 %copy-start.25 = (s32[512]{0:T(512)S(1)}, s32[512]{0:T(512)}, u32[]{:S(2)}) copy-start(s32[512]{0:T(512)} %param.19) | copy-start | bytes 6148
  28.0 101.5 %copy-start.19 = (bf16[512,256]{1,0:T(8,128)(2,1)S(1)}, bf16[512,256]{1,0:T(8,128)(2,1)}, u32[]{:S(2)}) copy-start(bf16[512,256]{1,0:T(8,128)(2,1)} %param.15) | copy-start | bytes 786436
  28.1 102.2 %copy-start.21 = (s32[512,16]{0,1:T(8,128)S(1)}, s32[512,16]{0,1:T(8,128)}, u32[]{:S(2)}) copy-start(s32[512,16]{0,1:T(8,128)} %param.18) | copy-start | bytes 98308
  28.1 102.4 %copy-start.3 = (bf16[512,256]{1,0:T(8,128)(2,1)S(1)}, bf16[512,256]{1,0:T(8,128)(2,1)}, u32[]{:S(2)}) copy-start(bf16[512,256]{1,0:T(8,128)(2,1)} %param.11) | copy-start | bytes 786436
  127.2 3.4 copy-start.26
  128.0 1.5 copy-start.22
  130.5 37.3 %copy-start.20 = (bf16[256,256]{1,0:T(8,128)(2,1)S(1)}, bf16[256,256]{1,0:T(8,128)(2,1)}, u32[]{:S(2)}) copy-start(bf16[256,256]{1,0:T(8,128)(2,1)} %param.13) | copy-start | bytes 393220
  145.5 2.9 copy-start.13
  148.5 0.7 copy-start.14
  164.1 2.9 copy-start.13
  167.1 0.7 copy-start.14
  167.8 2.8 copy-start.8
  167.8 2.8 copy-start.12
  167.8 2.8 copy-start.24
  167.8 3.2 copy-start.15
  169.4 2.6 copy-start.7
  169.4 2.7 copy-start.23
  171.0 2.5 copy-start.11
  171.0 2.4 copy-start.27
  172.1 97.2 %copy-start.10 = (f32[1,512,256]{1,2,0:T(8,128)S(1)}, f32[1,512,256]{1,2,0:T(8,128)}, u32[]{:S(2)}) copy-start(f32[1,512,256]{1,2,0:T(8,128)} %copy-done.9) | copy-start | bytes 1572868
  173.4 97.7 %copy-start.5 = (f32[1,512,256]{1,2,0:T(8,128)S(1)}, f32[1,512,256]{1,2,0:T(8,128)}, u32[]{:S(2)}) copy-start(f32[1,512,256]{1,2,0:T(8,128)} %copy-done.4) | copy-start | bytes 1572868
  174.8 97.8 %copy-start.2 = (f32[3,512,256]{1,2,0:T(8,128)S(1)}, f32[3,512,256]{1,2,0:T(8,128)}, u32[]{:S(2)}) copy-start(f32[3,512,256]{1,2,0:T(8,128)} %copy-done.1) | copy-start | bytes 4718596
  269.3 3.3 copy-start.16
  269.3 3.3 copy-start.17
  269.3 3.3 copy-start.18
Sparse Core Ops, SparseCore 0:
  274.3 271.1 all-reduce.4
where the time goes:
time: 557 us; the launch traced here: 556 us
  waiting for transfers between devices  270 us (48%)
  blocking collectives  193 us (35%)
  local copies, waits for them, and re-layouts  37.8 us (7%)
  between operations  16.4 us (3%)
  starting transfers between devices  14 us (3%)
  matrix products  13.1 us (2%)
  other arithmetic  12.3 us (2%)
    psum x1, waiting for transfers between devices, local(): qkv_total, graph_total = lax.psum((qkv_term, graph_term), ('dom', 'head'))  270 us
    psum x1, blocking collectives, local(): kv_sum, ks_sum = lax.psum((kv_part, ks_part), ('dom', 'head'))  98.5 us
    psum x1, blocking collectives, local(): dkv_sum, dks_sum = lax.psum((dkv_part, dks_part), ('dom', 'head'))  94.4 us
    gather x2, local copies, waits for them, and re-layouts, one_block(): picked = extended[nbr_block].astype(jnp.float32)  29.2 us
  transfers between devices with their start and end apart: 3, of which 1 were waited for; matrix products, arithmetic and copies ran while one was open for 1% of the time, Pallas kernels for 0%

commit v1 on v0

v1 whole, which is shorter than its diff:
```python
import functools

import jax
import jax.numpy as jnp
from jax import lax
from jax.experimental import pallas as pl
from jax.experimental.pallas import tpu as pltpu
from jax.sharding import Mesh, PartitionSpec as P

D = 256
DH = 32
HEADS = D // DH
TILE = 8
PACK = 5 * D
BLOCK = 128
MESH_FACTORS = {64: (4, 8, 2), 8: (2, 2, 2)}
FINE = ("x", "y", "c", "z")
HIGHEST = lax.Precision.HIGHEST
ROWS_FIRST = (((0,), (0,)), ((), ()))
COLS_LAST = (((1,), (1,)), ((), ()))


def dot(a, b, dims=(((1,), (0,)), ((), ())), precision=None):
    return lax.dot_general(a, b, dims, precision=precision, preferred_element_type=jnp.float32)


def feature_map(value):
    return jnp.where(value > 0, value + 1.0, jnp.exp(jnp.minimum(value, 0.0)))


def feature_slope(value):
    return jnp.where(value > 0, jnp.ones_like(value), jnp.exp(jnp.minimum(value, 0.0)))


def same_head():
    row = lax.broadcasted_iota(jnp.int32, (D, D), 0) // DH
    col = lax.broadcasted_iota(jnp.int32, (D, D), 1) // DH
    return row == col


def alive_of(count, rows, first):
    return (lax.broadcasted_iota(jnp.int32, (rows, 1), 0) + first < count).astype(jnp.float32)


def pack_sums(dense, vectors):
    kept = jnp.where(same_head(), dense, 0.0)
    folded = kept[0:DH]
    for h in range(1, HEADS):
        folded = folded + kept[h * DH : (h + 1) * DH]
    row = lax.broadcasted_iota(jnp.int32, (TILE, D), 0)
    last = jnp.zeros((TILE, D), jnp.float32)
    for i, vector in enumerate(vectors):
        last = jnp.where(row == i, vector, last)
    return [folded[t * TILE : (t + 1) * TILE] for t in range(4)] + [last]


def unpack_sums(packed):
    folded = jnp.concatenate([packed[:, t * D : (t + 1) * D] for t in range(4)], axis=0)
    dense = jnp.where(same_head(), jnp.concatenate([folded] * HEADS, axis=0), 0.0)
    return dense, packed[:, 4 * D : 5 * D]


def key_kernel(count_ref, feats_ref, all_ref, w_ref, send_ref, packed_ref, before_ref, after_ref, kv_ref, ks_ref):
    step = pl.program_id(0)
    rows = feats_ref.shape[0]

    @pl.when(step == 0)
    def _():
        kv_ref[...] = jnp.zeros_like(kv_ref)
        ks_ref[...] = jnp.zeros_like(ks_ref)
        source = all_ref[...]
        slot = lax.broadcasted_iota(jnp.int32, (source.shape[0], send_ref.shape[2]), 0)
        for side, out in ((0, before_ref), (1, after_ref)):
            chosen = (slot == send_ref[0, side : side + 1, :]).astype(jnp.bfloat16)
            out[...] = dot(chosen, source, ROWS_FIRST).astype(jnp.bfloat16)

    feats = feats_ref[...]
    alive = alive_of(count_ref[0], rows, step * rows)
    key_map = feature_map(dot(feats, w_ref[1])) * alive
    value_rows = dot(feats, w_ref[2])
    kv_ref[...] += dot(key_map, value_rows, ROWS_FIRST, HIGHEST)
    ks_ref[...] += jnp.sum(key_map, axis=0, keepdims=True)

    @pl.when(step == pl.num_programs(0) - 1)
    def _():
        live = jnp.full((1, D), count_ref[0].astype(jnp.float32))
        for t, part in enumerate(pack_sums(kv_ref[...], [ks_ref[0:1], live])):
            packed_ref[:, t * D : (t + 1) * D] = part


def agg_kernel(nbr_ref, count_ref, feats_ref, left_ref, right_ref, agg_ref, hits_ref, count_col_ref):
    total = feats_ref.shape[0]
    rim = left_ref.shape[0]
    wide = total + 2 * rim
    sub = 32
    lane = lax.broadcasted_iota(jnp.int32, (128, 128), 1)
    sublane = lax.broadcasted_iota(jnp.int32, (128, 128), 0)
    for b in range(total // 128):
        row = jnp.broadcast_to(count_ref[b : b + 1, :], (128, 128))
        column = jnp.sum(jnp.where(lane == sublane, row, 0), axis=1, keepdims=True)
        count_col_ref[b * 128 : (b + 1) * 128, :] = column
    slots = nbr_ref.shape[1]

    def body(i, carry):
        first = pl.multiple_of(i * sub, sub)
        counts = count_col_ref[pl.ds(first, sub), :]
        slot = lax.broadcasted_iota(jnp.int32, (sub, slots), 1)
        named = jnp.where(slot < counts, nbr_ref[pl.ds(first, sub), :], -1)
        place = lax.broadcasted_iota(jnp.int32, (sub, wide), 1)
        own = lax.broadcasted_iota(jnp.int32, (sub, wide), 0) + first
        hits = (place == own).astype(jnp.float32)
        for s in range(slots):
            hits = hits + (place == named[:, s : s + 1]).astype(jnp.float32)
        hits_ref[pl.ds(first, sub), :] = hits.astype(jnp.bfloat16)
        return carry

    lax.fori_loop(0, total // sub, body, 0)
    summed = dot(hits_ref[:, :total], feats_ref[...])
    summed += dot(hits_ref[:, total : total + rim], left_ref[...])
    summed += dot(hits_ref[:, total + rim :], right_ref[...])
    agg_ref[...] = (summed / (1.0 + count_col_ref[...].astype(jnp.float32))).astype(jnp.bfloat16)


def mix_kernel(
    count_ref, packed_ref, feats_ref, agg_ref, grad_ref, w_ref, wg_ref, gain_ref,
    out_ref, dnum_ref, packed_out_ref, q_term_ref, g_term_ref, kv_ref, dkv_ref, dks_ref,
):
    step = pl.program_id(0)
    rows = feats_ref.shape[0]

    @pl.when(step == 0)
    def _():
        kv_ref[...] = unpack_sums(packed_ref[...])[0]
        dkv_ref[...] = jnp.zeros_like(dkv_ref)
        dks_ref[...] = jnp.zeros_like(dks_ref)
        q_term_ref[...] = jnp.zeros_like(q_term_ref)
        g_term_ref[...] = jnp.zeros_like(g_term_ref)

    ks = packed_ref[0:1, 4 * D : 5 * D]
    live = packed_ref[1:2, 4 * D : 5 * D]
    factor = 1.0 / (DH * live)
    kv = kv_ref[...]
    heads = same_head().astype(jnp.float32)
    gain = gain_ref[...]
    feats = feats_ref[...]
    agg = agg_ref[...]
    alive = alive_of(count_ref[0], rows, step * rows)

    queries = dot(feats, w_ref[0])
    value_rows = dot(feats, w_ref[2])
    query_map = feature_map(queries)
    numer = value_rows + factor * dot(query_map, kv, precision=HIGHEST)
    denom = 1.0 + factor * dot(query_map * ks, heads, precision=HIGHEST)
    inverse = 1.0 / denom
    attn = numer * inverse
    mixed = 0.5 * attn + 0.5 * dot(agg, wg_ref[...])
    mean = jnp.sum(mixed, -1, keepdims=True) / D
    spread = jnp.sum(mixed * mixed, -1, keepdims=True) / D - mean * mean
    rstd = lax.rsqrt(spread + 1e-05)
    normed = (mixed - mean) * rstd
    out_ref[...] = (normed * gain * alive).astype(jnp.bfloat16)
    dnormed = grad_ref[...].astype(jnp.float32) * alive * gain
    dmixed = rstd * (
        dnormed
        - jnp.sum(dnormed, -1, keepdims=True) / D
        - normed * (jnp.sum(dnormed * normed, -1, keepdims=True) / D)
    )
    dattn = 0.5 * dmixed
    g_term_ref[...] += dot(agg, dattn.astype(jnp.bfloat16), ROWS_FIRST)
    dnum = dattn * inverse
    dnum_ref[...] = dnum
    dden = -dot(dattn * attn, heads, precision=HIGHEST) * inverse
    dkv_ref[...] += dot(query_map, dnum, ROWS_FIRST, HIGHEST)
    dks_ref[...] += jnp.sum(query_map * dden, axis=0, keepdims=True)
    dquery = factor * (dot(dnum, kv, COLS_LAST, HIGHEST) + dden * ks) * feature_slope(queries)
    q_term_ref[...] += dot(feats, dquery.astype(jnp.bfloat16), ROWS_FIRST)

    @pl.when(step == pl.num_programs(0) - 1)
    def _():
        for t, part in enumerate(pack_sums(factor * dkv_ref[...], [factor * dks_ref[0:1]])):
            packed_out_ref[:, t * D : (t + 1) * D] = part


def grad_kernel(count_ref, packed_ref, feats_ref, dnum_ref, w_ref, q_term_ref, g_term_ref, terms_ref, dkv_ref):
    step = pl.program_id(0)
    rows = feats_ref.shape[0]

    @pl.when(step == 0)
    def _():
        dkv_ref[...] = unpack_sums(packed_ref[...])[0]
        terms_ref[0] = q_term_ref[...]
        terms_ref[1] = jnp.zeros((D, D), jnp.float32)
        terms_ref[2] = jnp.zeros((D, D), jnp.float32)
        terms_ref[3] = g_term_ref[...]

    dks = packed_ref[0:1, 4 * D : 5 * D]
    dkv = dkv_ref[...]
    feats = feats_ref[...]
    alive = alive_of(count_ref[0], rows, step * rows)
    key_rows = dot(feats, w_ref[1])
    value_rows = dot(feats, w_ref[2])
    key_map = feature_map(key_rows) * alive
    dvalue = dnum_ref[...] + dot(key_map, dkv, precision=HIGHEST)
    dkey = (dot(value_rows, dkv, COLS_LAST, HIGHEST) + dks) * alive * feature_slope(key_rows)
    terms_ref[1] += dot(feats, dkey.astype(jnp.bfloat16), ROWS_FIRST)
    terms_ref[2] += dot(feats, dvalue.astype(jnp.bfloat16), ROWS_FIRST)


def scatter_sum(value, axes, count):
    parts = lax.all_to_all(value, axes, 0, 0, tiled=True)
    return jnp.sum(parts.reshape(count, value.shape[0] // count, *value.shape[1:]), axis=0)


def gather(value, axes, count):
    copies = jnp.broadcast_to(value[None], (count, *value.shape)).reshape(count * value.shape[0], *value.shape[1:])
    return lax.all_to_all(copies, axes, 0, 0, tiled=True)


def sum_packed(packed, sizes):
    near = sizes["x"] * sizes["c"]
    far = sizes["y"] * sizes["z"]
    share = scatter_sum(packed.reshape(TILE, PACK), ("x", "c"), near)
    share = jnp.sum(gather(share, ("y", "z"), far).reshape(far, *share.shape), axis=0)
    return gather(share, ("x", "c"), near)


def sum_terms(terms, sizes, scale):
    far = sizes["y"] * sizes["z"]
    value = scatter_sum(terms, "c", sizes["c"])
    value = scatter_sum(value, "x", sizes["x"])
    value = scatter_sum(value, ("y", "z"), far) * scale
    value = gather(value, ("y", "z"), far)
    value = gather(value, "x", sizes["x"])
    return gather(value, "c", sizes["c"])


def local(sizes, node_feats, w_qkv, w_graph, ln_gain, out_grad, part_counts, send_rows, neighbours, neighbour_counts):
    rows = node_feats.shape[0]
    rim = send_rows.shape[2]
    steps = rows // BLOCK
    f32, bf16 = jnp.float32, jnp.bfloat16
    smem = pl.BlockSpec(memory_space=pltpu.SMEM)

    def whole(*shape):
        return pl.BlockSpec(shape, lambda i: (0,) * len(shape))

    by_row = pl.BlockSpec((BLOCK, D), lambda i: (i, 0))
    shape = jax.ShapeDtypeStruct

    packed, to_before, to_after = pl.pallas_call(
        key_kernel,
        grid=(steps,),
        in_specs=[smem, by_row, whole(rows, D), whole(3, D, D), whole(1, 2, rim)],
        out_specs=[whole(TILE, PACK), whole(rim, D), whole(rim, D)],
        out_shape=[shape((TILE, PACK), f32), shape((rim, D), bf16), shape((rim, D), bf16)],
        scratch_shapes=[pltpu.VMEM((D, D), f32), pltpu.VMEM((1, D), f32)],
        name="keys",
    )(part_counts, node_feats, node_feats, w_qkv, send_rows)

    parts = sizes["x"] * sizes["y"] * sizes["c"] * sizes["z"]
    up = [(i, i + 1) for i in range(parts - 1)]
    down = [(j, i) for i, j in up]
    left = lax.ppermute(to_after, FINE, up)
    right = lax.ppermute(to_before, FINE, down)
    packed = sum_packed(packed, sizes)

    agg = pl.pallas_call(
        agg_kernel,
        out_shape=shape((rows, D), bf16),
        scratch_shapes=[pltpu.VMEM((rows, rows + 2 * rim), bf16), pltpu.VMEM((rows, 1), jnp.int32)],
        name="aggregate",
    )(neighbours, neighbour_counts.reshape(rows // 128, 128), node_feats, left, right)

    node_out, dnum, dpacked, q_term, g_term = pl.pallas_call(
        mix_kernel,
        grid=(steps,),
        in_specs=[smem, whole(TILE, PACK), by_row, by_row, by_row, whole(3, D, D), whole(D, D), whole(1, D)],
        out_specs=[by_row, by_row, whole(TILE, PACK), whole(D, D), whole(D, D)],
        out_shape=[
            shape((rows, D), bf16), shape((rows, D), f32), shape((TILE, PACK), f32),
            shape((D, D), f32), shape((D, D), f32),
        ],
        scratch_shapes=[pltpu.VMEM((D, D), f32), pltpu.VMEM((D, D), f32), pltpu.VMEM((1, D), f32)],
        name="mix",
    )(part_counts, packed, node_feats, agg, out_grad, w_qkv, w_graph, ln_gain.reshape(1, D))

    dpacked = sum_packed(dpacked, sizes)

    terms = pl.pallas_call(
        grad_kernel,
        grid=(steps,),
        in_specs=[smem, whole(TILE, PACK), by_row, by_row, whole(3, D, D), whole(D, D), whole(D, D)],
        out_specs=whole(4, D, D),
        out_shape=shape((4, D, D), f32),
        scratch_shapes=[pltpu.VMEM((D, D), f32)],
        name="grads",
    )(part_counts, dpacked, node_feats, dnum, w_qkv, q_term, g_term)

    scale = lax.rsqrt(packed[1:2, 4 * D : 4 * D + 1])
    total = sum_terms(terms.reshape(4 * D, D), sizes, scale).reshape(4, D, D)
    return node_out, total[:3], total[3]


def solution(mesh):
    sizes = dict(zip(FINE, (*MESH_FACTORS[mesh.shape["dom"]], mesh.shape["head"])))
    fine = Mesh(mesh.devices.reshape(tuple(sizes.values())), FINE)
    return jax.shard_map(
        functools.partial(local, sizes),
        mesh=fine,
        in_specs=(
            P(FINE, None), P(), P(), P(), P(FINE, None), P(FINE), P(FINE, None, None), P(FINE, None), P(FINE),
        ),
        out_specs=(P(FINE, None), P(), P()),
        check_vma=False,
    )
```

time: 557 us -> 204 us (0.37)
  waiting for transfers between devices: 270 us -> 9.94 us
  blocking collectives: 193 us -> 136 us
  local copies, waits for them, and re-layouts: 37.8 us -> 9.11 us
  Pallas kernels: 0 us -> 26.9 us
  between operations: 16.4 us -> 2.09 us
  matrix products: 13.1 us -> 0 us
  other arithmetic: 12.3 us -> 0.74 us
    psum x1 -> x0, waiting for transfers between devices: 270 us -> none  [local(): qkv_total, graph_total = lax.psum((qkv_term, graph_term), ('dom', 'head'))]
    psum x2 -> x0, blocking collectives: 193 us -> none  [the longest x1 98.5 us: local(): kv_sum, ks_sum = lax.psum((kv_part, ks_part), ('dom', 'head'))]
    all_to_all x0 -> x10, blocking collectives: none -> 136 us  [the longest x6 91.3 us: gather(): return lax.all_to_all(copies, axes, 0, 0, tiled=True)]
    gather x3 -> x0, local copies, waits for them, and re-layouts: 31 us -> none  [the longest x2 29.2 us: one_block(): picked = extended[nbr_block].astype(jnp.float32)]
    pallas_call x0 -> x4, Pallas kernels: none -> 26.9 us  [the longest x1 8.85 us: local(): pl.pallas_call(mix_kernel, grid=(steps,), in_specs=[smem, whole(TILE, PAC...]
    dot_general x10 -> x0, matrix products: 13.1 us -> none  [the longest x1 1.77 us: local(): jnp.einsum('rhi,hij->rhj', key_map, dkv_sum, precision=highest)]
    all_to_all x0 -> x2, starting transfers between devices: none -> 11.1 us  [the longest x1 6.49 us: gather(): return lax.all_to_all(copies, axes, 0, 0, tiled=True)]
    all_to_all x0 -> x2, waiting for transfers between devices: none -> 9.79 us  [the longest x1 9.79 us: scatter_sum(): parts = lax.all_to_all(value, axes, 0, 0, tiled=True)]
  transfers between devices with their start and end apart: 3 -> 4, of which waited for: 1 -> 2; matrix products, arithmetic and copies ran while one was open for 1% -> 1% of each run, Pallas kernels for 0% -> 3%
where the time goes in v1:
time: 204 us; the launch traced here: 202 us
  blocking collectives  136 us (67%)
  Pallas kernels  26.9 us (13%)
  starting transfers between devices  17.9 us (9%)
  waiting for transfers between devices  9.94 us (5%)
  local copies, waits for them, and re-layouts  9.11 us (4%)
  between operations  2.09 us (1%)
    all_to_all x6, blocking collectives, gather(): return lax.all_to_all(copies, axes, 0, 0, tiled=True)  91.3 us
    all_to_all x4, blocking collectives, scatter_sum(): parts = lax.all_to_all(value, axes, 0, 0, tiled=True)  44.6 us
    all_to_all x1, waiting for transfers between devices, scatter_sum(): parts = lax.all_to_all(value, axes, 0, 0, tiled=True)  9.79 us
    pallas_call x1, Pallas kernels, local(): pl.pallas_call(mix_kernel, grid=(steps,), in_specs=[smem, whole(TILE, PAC...  8.85 us
    pallas_call x1, Pallas kernels, local(): pl.pallas_call(agg_kernel, out_shape=shape((rows, D), bf16), scratch_shap...  7.01 us
    all_to_all x1, starting transfers between devices, gather(): return lax.all_to_all(copies, axes, 0, 0, tiled=True)  6.49 us
    pallas_call x1, Pallas kernels, local(): pl.pallas_call(grad_kernel, grid=(steps,), in_specs=[smem, whole(TILE, PA...  6.3 us
    pallas_call x1, Pallas kernels, local(): pl.pallas_call(key_kernel, grid=(steps,), in_specs=[smem, by_row, whole(r...  4.72 us
  transfers between devices with their start and end apart: 4, of which 2 were waited for; matrix products, arithmetic and copies ran while one was open for 1% of the time, Pallas kernels for 3%

profile of v1, /device:TPU:1, one launch (start us, length us, event | category | flops | bytes accessed | tf_op | source)
XLA Modules:
  0.0 202.4 jit_solution(10453320333339065459)
XLA Ops:
  1.3 4.7 %keys.1 = (f32[8,1280]{1,0:T(8,128)}, bf16[64,256]{1,0:T(8,128)(2,1)}, bf16[64,256]{1,0:T(8,128)(2,1)}) custom-call(s32[1]{0:T(128)S(6)} %copy.35.count_ref, bf16[512,256]{1,0:T(8,128)(2,1)} %feats_ref.7, bf16[512,256]{1,0:T(8,128)(2,1)} %feats_ref.7, bf16[3,256,256]{2,1,0:T(8,128)(2,1)} %w_ref.5, s32[1,2,64]{2,1,0:T(2,128)} %send_ref.1), custom_call_target="tpu_custom_call" | custom-call | tf_op jit(solution)/shard_map/keys/pallas_call | solution.py:250
  6.0 0.8 copy.20
  6.8 14.0 %all_to_all.94 = f32[8,1,1280]{2,1,0:T(1,128)S(1)} all-to-all(f32[8,1,1280]{2,1,0:T(1,128)S(1)} %copy.20), channel_id=1, replica_groups=mesh['x'=4,'y'=8,'c'=2,'z'=8] {'x','c'}, dimensions={0} | all-to-all | bytes 81920 | tf_op jit(solution)/shard_map/all_to_all | solution.py:210
  20.8 0.2 reshape.109
  21.0 26.2 %all_to_all.95 = f32[64,1,1280]{2,1,0:T(1,128)S(1)} all-to-all(f32[64,1,1280]{2,1,0:T(1,128)S(1)} %reshape.109), channel_id=1, replica_groups=mesh['x'=4,'y'=8,'c'=2,'z'=8] {'y','z'}, dimensions={0} | all-to-all | bytes 655360 | tf_op jit(solution)/shard_map/all_to_all | solution.py:216
  47.2 0.2 reduce_sum.64
  47.5 0.0 copy-start.4
  47.5 0.6 reshape.110
  48.1 0.0 copy-start.3
  48.1 0.0 copy-start
  48.1 6.5 %all-to-all-start.2 = ((f32[8,1,1280]{2,1,0:T(1,128)}), f32[8,1,1280]{2,1,0:T(1,128)S(1)}, u32[]{:S(2)}, u32[]{:S(2)}) async-start(f32[8,1,1280]{2,1,0:T(1,128)} %reshape.110), calls=%async_computation.2 | async-start | bytes 81920 | tf_op jit(solution)/shard_map/all_to_all | solution.py:216
  54.6 0.0 copy-done.4
  54.6 2.7 %collective-permute-start = (bf16[64,256]{1,0:T(8,128)(2,1)S(1)}, bf16[64,256]{1,0:T(8,128)(2,1)S(1)}, u32[]{:S(2)}, u32[]{:S(2)}) collective-permute-start(bf16[64,256]{1,0:T(8,128)(2,1)S(1)} %copy-done.4), channel_id=1, source_target_pairs={{0,1},{1,2},{2,3},{3,4},{4,5},{5,6},{6,7},{7,8},{8,9},{9,10},{10,1... | collective-permute-start | bytes 98312 | tf_op jit(solution)/shard_map/ppermute | solution.py:263
  57.3 0.0 copy-done.3
  57.3 4.1 %collective-permute-start.1 = (bf16[64,256]{1,0:T(8,128)(2,1)S(1)}, bf16[64,256]{1,0:T(8,128)(2,1)S(1)}, u32[]{:S(2)}, u32[]{:S(2)}) collective-permute-start(bf16[64,256]{1,0:T(8,128)(2,1)S(1)} %copy-done.3), channel_id=1, source_target_pairs={{1,0},{2,1},{3,2},{4,3},{5,4},{6,5},{7,6},{8,7},{9,8},{10,9},{11,1... | collective-permute-start | bytes 98312 | tf_op jit(solution)/shard_map/ppermute | solution.py:264
  61.4 0.0 copy-done
  61.4 0.8 copy.22.nbr_ref
  62.2 0.0 collective-permute-done.left_ref
  62.2 0.0 copy-start.1
  62.2 0.1 collective-permute-done.1.right_ref
  62.4 0.0 copy-start.2
  62.4 0.5 copy-done.1
  62.9 0.1 copy-done.2
  63.0 7.0 %aggregate.1.agg_ref = bf16[512,256]{1,0:T(8,128)(2,1)} custom-call(s32[512,16]{1,0:T(8,128)} %copy.22.nbr_ref, s32[4,128]{1,0:T(4,128)} %bitcast.27, bf16[512,256]{1,0:T(8,128)(2,1)} %feats_ref.7, bf16[64,256]{1,0:T(8,128)(2,1)} %copy-done.1, bf16[64,256]{1,0:T(8,128)(2,1)} %copy-done.2), custom_call_target="tpu_custom_call" | custom-call | tf_op jit(solution)/shard_map/aggregate/pallas_call | solution.py:267
  70.0 0.0 all-to-all-done.2
  70.0 0.6 copy.34
  70.6 8.8 %mix.1 = (bf16[512,256]{1,0:T(8,128)(2,1)}, f32[512,256]{1,0:T(8,128)}, f32[8,1280]{1,0:T(8,128)}, f32[256,256]{1,0:T(8,128)}, f32[256,256]{1,0:T(8,128)}) custom-call(s32[1]{0:T(128)S(6)} %copy.35.count_ref, f32[8,1280]{1,0:T(8,128)} %bitcast.22, bf16[512,256]{1,0:T(8,128)(2,1)} %feats_ref.7, bf16[512,256]{1,0:T(8,128)(2,1)} %aggregate.1.agg_ref, ...), custom_call_target="tpu_custom_call" | custom-call | tf_op jit(solution)/shard_map/mix/pallas_call | solution.py:274
  79.5 0.8 copy.23
  80.3 12.9 %all_to_all.96 = f32[8,1,1280]{2,1,0:T(1,128)S(1)} all-to-all(f32[8,1,1280]{2,1,0:T(1,128)S(1)} %copy.23), channel_id=1, replica_groups=mesh['x'=4,'y'=8,'c'=2,'z'=8] {'x','c'}, dimensions={0} | all-to-all | bytes 81920 | tf_op jit(solution)/shard_map/all_to_all | solution.py:210
  93.3 0.2 reshape.113
  93.4 21.2 %all_to_all.97 = f32[64,1,1280]{2,1,0:T(1,128)S(1)} all-to-all(f32[64,1,1280]{2,1,0:T(1,128)S(1)} %reshape.113), channel_id=1, replica_groups=mesh['x'=4,'y'=8,'c'=2,'z'=8] {'y','z'}, dimensions={0} | all-to-all | bytes 655360 | tf_op jit(solution)/shard_map/all_to_all | solution.py:216
  114.7 0.2 reduce_sum.66
  114.9 10.2 %all_to_all.98 = f32[8,1,1280]{2,1,0:T(1,128)S(1)} all-to-all(f32[8,1,1280]{2,1,0:T(1,128)S(1)} %reshape.114), channel_id=1, replica_groups=mesh['x'=4,'y'=8,'c'=2,'z'=8] {'x','c'}, dimensions={0} | all-to-all | bytes 81920 | tf_op jit(solution)/shard_map/all_to_all | solution.py:216
  125.2 0.6 copy.33
  125.8 6.3 %grads.1 = f32[4,256,256]{2,1,0:T(8,128)} custom-call(s32[1]{0:T(128)S(6)} %copy.35.count_ref, f32[8,1280]{1,0:T(8,128)} %bitcast.24, bf16[512,256]{1,0:T(8,128)(2,1)} %feats_ref.7, f32[512,256]{1,0:T(8,128)} %get-tuple-element.16.dnum_ref, bf16[3,256,256]{2,1,0:T(8,128)(2,1)} %w_ref.5, f32[256,256]{1,0:T(8,128)} %get-tuple-element.17.q_term_ref, ...), custom_call_target="tpu_custom_call" | custom-call | tf_op jit(solution)/shard_map/grads/pallas_call | solution.py:289
  132.1 6.1 %all_to_all.99 = f32[2,512,256]{2,1,0:T(8,128)S(1)} all-to-all(f32[2,512,256]{2,1,0:T(8,128)} %bitcast.16), channel_id=1, replica_groups=mesh['x'=4,'y'=8,'c'=2,'z'=8] {'c'}, dimensions={0} | all-to-all | bytes 2097152 | tf_op jit(solution)/shard_map/all_to_all | solution.py:210
  138.1 0.1 reduce_sum.67
  138.2 11.6 %all_to_all.100 = f32[4,128,256]{2,1,0:T(8,128)S(1)} all-to-all(f32[4,128,256]{2,1,0:T(8,128)S(1)} %bitcast.20), channel_id=1, replica_groups=mesh['x'=4,'y'=8,'c'=2,'z'=8] {'x'}, dimensions={0} | all-to-all | bytes 1048576 | tf_op jit(solution)/shard_map/all_to_all | solution.py:210
  149.9 0.7 all_to_all.76
  150.6 4.6 %all-to-all-start.8 = ((f32[64,2,256]{2,1,0:T(2,128)}), f32[64,2,256]{2,1,0:T(2,128)S(1)}, u32[]{:S(2)}, u32[]{:S(2)}) async-start(f32[64,2,256]{2,1,0:T(2,128)} %all_to_all.76), calls=%async_computation.8 | async-start | bytes 262144 | tf_op jit(solution)/shard_map/all_to_all | solution.py:210
  155.2 1.2 slice.17
  157.1 9.8 %all-to-all-done.8 = f32[64,2,256]{2,1,0:T(2,128)S(1)} async-done(((f32[64,2,256]{2,1,0:T(2,128)}), f32[64,2,256]{2,1,0:T(2,128)S(1)}, u32[]{:S(2)}, u32[]{:S(2)}) %all-to-all-start.8) | async-done | bytes 131104 | tf_op jit(solution)/shard_map/all_to_all | solution.py:210
  166.9 0.1 reduce_sum.69
  167.0 15.4 %all_to_all.101 = f32[64,2,256]{2,1,0:T(2,128)S(1)} all-to-all(f32[64,2,256]{2,1,0:T(2,128)S(1)} %broadcast_in_dim.10), channel_id=1, replica_groups=mesh['x'=4,'y'=8,'c'=2,'z'=8] {'y','z'}, dimensions={0} | all-to-all | bytes 262144 | tf_op jit(solution)/shard_map/all_to_all | solution.py:216
  182.5 0.1 broadcast_in_dim.11
  182.6 9.3 %all_to_all.102 = f32[4,128,256]{2,1,0:T(8,128)S(1)} all-to-all(f32[4,128,256]{2,1,0:T(8,128)S(1)} %broadcast_in_dim.12), channel_id=1, replica_groups=mesh['x'=4,'y'=8,'c'=2,'z'=8] {'x'}, dimensions={0} | all-to-all | bytes 1048576 | tf_op jit(solution)/shard_map/all_to_all | solution.py:216
  191.9 0.1 broadcast_in_dim.14
  192.0 8.8 %all_to_all.103 = f32[2,512,256]{2,1,0:T(8,128)S(1)} all-to-all(f32[2,512,256]{2,1,0:T(8,128)S(1)} %broadcast_in_dim.14), channel_id=1, replica_groups=mesh['x'=4,'y'=8,'c'=2,'z'=8] {'c'}, dimensions={0} | all-to-all | bytes 2097152 | tf_op jit(solution)/shard_map/all_to_all | solution.py:216
  200.8 0.7 slice.19
  201.5 0.9 slice.18
  (7 shorter events, 0.2 us)
Async XLA Ops:
  47.5 7.1 %copy-start.4 = (bf16[64,256]{1,0:T(8,128)(2,1)S(1)}, bf16[64,256]{1,0:T(8,128)(2,1)}, u32[]{:S(2)}) copy-start(bf16[64,256]{1,0:T(8,128)(2,1)} %get-tuple-element.12) | copy-start | bytes 98308
  48.1 9.2 %copy-start.3 = (bf16[64,256]{1,0:T(8,128)(2,1)S(1)}, bf16[64,256]{1,0:T(8,128)(2,1)}, u32[]{:S(2)}) copy-start(bf16[64,256]{1,0:T(8,128)(2,1)} %get-tuple-element.13) | copy-start | bytes 98308
  48.1 13.3 %copy-start = (s32[512,16]{0,1:T(8,128)S(1)}, s32[512,16]{0,1:T(8,128)}, u32[]{:S(2)}) copy-start(s32[512,16]{0,1:T(8,128)} %param.16) | copy-start | bytes 98308
  48.1 21.9 %all-to-all-start.2 = ((f32[8,1,1280]{2,1,0:T(1,128)}), f32[8,1,1280]{2,1,0:T(1,128)S(1)}, u32[]{:S(2)}, u32[]{:S(2)}) async-start(f32[8,1,1280]{2,1,0:T(1,128)} %reshape.110), calls=%async_computation.2 | async-start | bytes 81920 | tf_op jit(solution)/shard_map/all_to_all | solution.py:216
  54.6 7.6 %collective-permute-start = (bf16[64,256]{1,0:T(8,128)(2,1)S(1)}, bf16[64,256]{1,0:T(8,128)(2,1)S(1)}, u32[]{:S(2)}, u32[]{:S(2)}) collective-permute-start(bf16[64,256]{1,0:T(8,128)(2,1)S(1)} %copy-done.4), channel_id=1, source_target_pairs={{0,1},{1,2},{2,3},{3,4},{4,5},{5,6},{6,7},{7,8},{8,9},{9,10},{10,1... | collective-permute-start | bytes 98312 | tf_op jit(solution)/shard_map/ppermute | solution.py:263
  57.3 5.1 %collective-permute-start.1 = (bf16[64,256]{1,0:T(8,128)(2,1)S(1)}, bf16[64,256]{1,0:T(8,128)(2,1)S(1)}, u32[]{:S(2)}, u32[]{:S(2)}) collective-permute-start(bf16[64,256]{1,0:T(8,128)(2,1)S(1)} %copy-done.3), channel_id=1, source_target_pairs={{1,0},{2,1},{3,2},{4,3},{5,4},{6,5},{7,6},{8,7},{9,8},{10,9},{11,1... | collective-permute-start | bytes 98312 | tf_op jit(solution)/shard_map/ppermute | solution.py:264
  62.2 0.6 copy-start.1
  62.4 0.6 copy-start.2
  150.6 16.3 %all-to-all-start.8 = ((f32[64,2,256]{2,1,0:T(2,128)}), f32[64,2,256]{2,1,0:T(2,128)S(1)}, u32[]{:S(2)}, u32[]{:S(2)}) async-start(f32[64,2,256]{2,1,0:T(2,128)} %all_to_all.76), calls=%async_computation.8 | async-start | bytes 262144 | tf_op jit(solution)/shard_map/all_to_all | solution.py:210

commit v2 on v1

v2 whole, which is shorter than its diff:
```python
import functools

import jax
import jax.numpy as jnp
from jax import lax
from jax.experimental import pallas as pl
from jax.experimental.pallas import tpu as pltpu
from jax.sharding import Mesh, PartitionSpec as P

D = 256
DH = 32
HEADS = D // DH
TILE = 8
PACK = 5 * D
BLOCK = 128
MESH_FACTORS = {64: (4, 8, 2), 8: (2, 2, 2)}
FINE = ("x", "y", "c", "z")
ROWS_FIRST = (((0,), (0,)), ((), ()))
COLS_LAST = (((1,), (1,)), ((), ()))


def dot(a, b, dims=(((1,), (0,)), ((), ()))):
    return lax.dot_general(a, b, dims, preferred_element_type=jnp.float32)


def feature_map(value):
    return jnp.where(value > 0, value + 1.0, jnp.exp(jnp.minimum(value, 0.0)))


def same_head():
    row = lax.broadcasted_iota(jnp.int32, (D, D), 0) // DH
    col = lax.broadcasted_iota(jnp.int32, (D, D), 1) // DH
    return row == col


def alive_of(count, rows, first):
    return (lax.broadcasted_iota(jnp.int32, (rows, 1), 0) + first < count).astype(jnp.float32)


def store_packed(out_ref, dense, vectors):
    kept = jnp.where(same_head(), dense, 0.0)
    folded = kept[0:DH]
    for h in range(1, HEADS):
        folded = folded + kept[h * DH : (h + 1) * DH]
    row = lax.broadcasted_iota(jnp.int32, (TILE, D), 0)
    last = jnp.zeros((TILE, D), jnp.float32)
    for i, vector in enumerate(vectors):
        last = jnp.where(row == i, vector, last)
    tiles = [folded[t * TILE : (t + 1) * TILE] for t in range(4)] + [last]
    for t, tile in enumerate(tiles):
        for r in range(TILE):
            out_ref[r, :, t * D : (t + 1) * D] = tile[r : r + 1]


def load_packed(packed_ref):
    tiles = [
        jnp.concatenate([packed_ref[r, :, t * D : (t + 1) * D] for r in range(TILE)], axis=0) for t in range(5)
    ]
    folded = jnp.concatenate(tiles[:4], axis=0)
    return jnp.where(same_head(), jnp.concatenate([folded] * HEADS, axis=0), 0.0), tiles[4]


def halves(value):
    high = value.astype(jnp.bfloat16)
    return high, (value - high.astype(jnp.float32)).astype(jnp.bfloat16)


def dot3(a, b, dims=(((1,), (0,)), ((), ()))):
    return dot(a[0], b[0], dims) + (dot(a[0], b[1], dims) + dot(a[1], b[0], dims))


def head_sums(value, heads):
    high, low = halves(value)
    return dot(high, heads) + dot(low, heads)


def key_kernel(
    count_ref, feats_ref, all_ref, w_ref, send_ref,
    packed_ref, before_ref, after_ref, key_ref, value_ref, kv_ref, ks_ref,
):
    step = pl.program_id(0)
    rows = feats_ref.shape[0]

    @pl.when(step == 0)
    def _():
        kv_ref[...] = jnp.zeros_like(kv_ref)
        ks_ref[...] = jnp.zeros_like(ks_ref)
        source = all_ref[...]
        slot = lax.broadcasted_iota(jnp.int32, (source.shape[0], send_ref.shape[2]), 0)
        for side, out in ((0, before_ref), (1, after_ref)):
            chosen = (slot == send_ref[0, side : side + 1, :]).astype(jnp.bfloat16)
            out[...] = dot(chosen, source, ROWS_FIRST).astype(jnp.bfloat16)

    feats = feats_ref[...]
    alive = alive_of(count_ref[0], rows, step * rows)
    key_map = feature_map(dot(feats, w_ref[1]))
    value_rows = dot(feats, w_ref[2])
    key_ref[...] = key_map
    value_ref[...] = value_rows
    key_map = key_map * alive
    kv_ref[...] += dot3(halves(key_map), halves(value_rows), ROWS_FIRST)
    ks_ref[...] += jnp.sum(key_map, axis=0, keepdims=True)

    @pl.when(step == pl.num_programs(0) - 1)
    def _():
        live = jnp.full((1, D), count_ref[0].astype(jnp.float32))
        store_packed(packed_ref, kv_ref[...], [ks_ref[...], live])


def prep_kernel(nbr_ref, count_ref, feats_ref, left_ref, right_ref, w_ref, wg_ref, agg_ref, graph_ref, query_ref, hits_ref):
    total = feats_ref.shape[0]
    rim = left_ref.shape[0]
    wide = total + 2 * rim
    slots = nbr_ref.shape[0]
    sub = 32
    for b in range(total // 128):
        at = slice(b * 128, (b + 1) * 128)
        slot = lax.broadcasted_iota(jnp.int32, (slots, 128), 0)
        named = jnp.where(slot < count_ref[:, at], nbr_ref[:, at], -1)
        rows = [jnp.broadcast_to(named[s : s + 1], (sub, 128)) for s in range(slots)]
        own = lax.broadcasted_iota(jnp.int32, (sub, 128), 1) + b * 128
        place0 = lax.broadcasted_iota(jnp.int32, (sub, 128), 0)

        def body(i, carry):
            first = pl.multiple_of(i * sub, sub)
            place = place0 + first
            hits = (place == own).astype(jnp.float32)
            for s in range(slots):
                hits = hits + (place == rows[s]).astype(jnp.float32)
            hits_ref[pl.ds(first, sub), at] = hits.astype(jnp.bfloat16)
            return carry

        lax.fori_loop(0, wide // sub, body, 0)
    ones = jnp.ones((wide, 128), jnp.bfloat16)
    for b in range(total // 128):
        at = slice(b * 128, (b + 1) * 128)
        summed = dot(hits_ref[:total, at], feats_ref[...], ROWS_FIRST)
        summed += dot(hits_ref[total : total + rim, at], left_ref[...], ROWS_FIRST)
        summed += dot(hits_ref[total + rim :, at], right_ref[...], ROWS_FIRST)
        named = dot(hits_ref[:, at], ones, ROWS_FIRST)
        agg = (summed / jnp.concatenate([named, named], axis=1)).astype(jnp.bfloat16)
        agg_ref[at, :] = agg
        graph_ref[at, :] = dot(agg, wg_ref[...])
        query_ref[at, :] = feature_map(dot(feats_ref[at, :], w_ref[0]))


def mix_kernel(
    count_ref, packed_ref, query_ref, value_ref, graph_ref, grad_ref, gain_ref,
    out_ref, dgraph_ref, dnum_ref, dden_ref, packed_out_ref, kv_ref, vec_ref, dkv_ref, dks_ref,
):
    step = pl.program_id(0)
    rows = query_ref.shape[0]

    @pl.when(step == 0)
    def _():
        kv, vectors = load_packed(packed_ref)
        kv_ref[0], kv_ref[1] = halves(kv)
        vec_ref[...] = vectors
        dkv_ref[...] = jnp.zeros_like(dkv_ref)
        dks_ref[...] = jnp.zeros_like(dks_ref)

    ks = vec_ref[0:1]
    factor = 1.0 / (DH * vec_ref[1:2])
    heads = same_head().astype(jnp.bfloat16)
    gain = gain_ref[...]
    alive = alive_of(count_ref[0], rows, step * rows)

    query_map = query_ref[...]
    query_halves = halves(query_map)
    numer = value_ref[...] + factor * dot3(query_halves, (kv_ref[0], kv_ref[1]))
    denom = 1.0 + factor * head_sums(query_map * ks, heads)
    inverse = 1.0 / denom
    attn = numer * inverse
    mixed = 0.5 * attn + 0.5 * graph_ref[...]
    mean = jnp.sum(mixed, -1, keepdims=True) / D
    spread = jnp.sum(mixed * mixed, -1, keepdims=True) / D - mean * mean
    rstd = lax.rsqrt(spread + 1e-05)
    normed = (mixed - mean) * rstd
    gain_alive = gain * alive
    out_ref[...] = (normed * gain_alive).astype(jnp.bfloat16)
    dnormed = grad_ref[...].astype(jnp.float32) * gain_alive
    dmixed = rstd * (
        dnormed
        - jnp.sum(dnormed, -1, keepdims=True) / D
        - normed * (jnp.sum(dnormed * normed, -1, keepdims=True) / D)
    )
    dattn = 0.5 * dmixed
    dgraph_ref[...] = dattn.astype(jnp.bfloat16)
    dnum = dattn * inverse
    dnum_ref[...] = dnum
    dden = -head_sums(dattn * attn, heads) * inverse
    dden_ref[...] = dden
    dkv_ref[...] += dot3(query_halves, halves(dnum), ROWS_FIRST)
    dks_ref[...] += jnp.sum(query_map * dden, axis=0, keepdims=True)

    @pl.when(step == pl.num_programs(0) - 1)
    def _():
        store_packed(packed_out_ref, factor * dkv_ref[...], [factor * dks_ref[...]])


def query_kernel(packed_ref, feats_ref, agg_ref, query_ref, dgraph_ref, dnum_ref, dden_ref, terms_ref, kv_ref, vec_ref):
    step = pl.program_id(0)

    @pl.when(step == 0)
    def _():
        kv, vectors = load_packed(packed_ref)
        kv_ref[0], kv_ref[1] = halves(kv)
        vec_ref[...] = vectors
        terms_ref[...] = jnp.zeros_like(terms_ref)

    factor = 1.0 / (DH * vec_ref[1:2])
    slope = jnp.minimum(query_ref[...], 1.0)
    dquery = factor * (
        dot3(halves(dnum_ref[...]), (kv_ref[0], kv_ref[1]), COLS_LAST) + dden_ref[...] * vec_ref[0:1]
    ) * slope
    terms_ref[0] += dot(agg_ref[...], dgraph_ref[...], ROWS_FIRST)
    terms_ref[1] += dot(feats_ref[...], dquery.astype(jnp.bfloat16), ROWS_FIRST)


def grad_kernel(count_ref, packed_ref, feats_ref, key_ref, value_ref, dnum_ref, held_ref, terms_ref, kv_ref, vec_ref):
    del held_ref
    step = pl.program_id(0)
    rows = feats_ref.shape[0]

    @pl.when(step == 0)
    def _():
        dkv, vectors = load_packed(packed_ref)
        kv_ref[0], kv_ref[1] = halves(dkv)
        vec_ref[...] = vectors
        terms_ref[...] = jnp.zeros_like(terms_ref)

    dkv = (kv_ref[0], kv_ref[1])
    feats = feats_ref[...]
    alive = alive_of(count_ref[0], rows, step * rows)
    key_map = key_ref[...]
    slope = jnp.minimum(key_map, 1.0) * alive
    dvalue = dnum_ref[...] + dot3(halves(key_map * alive), dkv)
    dkey = (dot3(halves(value_ref[...]), dkv, COLS_LAST) + vec_ref[0:1]) * slope
    terms_ref[0] += dot(feats, dkey.astype(jnp.bfloat16), ROWS_FIRST)
    terms_ref[1] += dot(feats, dvalue.astype(jnp.bfloat16), ROWS_FIRST)


def scatter_sum(value, axes, count):
    parts = lax.all_to_all(value, axes, 0, 0, tiled=True)
    return jnp.sum(parts.reshape(count, value.shape[0] // count, *value.shape[1:]), axis=0)


def gather(value, axes, count):
    copies = jnp.broadcast_to(value[None], (count, *value.shape)).reshape(count * value.shape[0], *value.shape[1:])
    return lax.all_to_all(copies, axes, 0, 0, tiled=True)


def gather_sum(value, axes, count):
    return jnp.sum(gather(value, axes, count).reshape(count, *value.shape), axis=0)


def sum_terms(terms, sizes, scale):
    value = scatter_sum(terms, "c", sizes["c"])
    value = scatter_sum(value, "x", sizes["x"])
    value = scatter_sum(value, "y", sizes["y"])
    value = gather_sum(value, "z", sizes["z"]) * scale
    value = gather(value, "y", sizes["y"])
    value = gather(value, "x", sizes["x"])
    return gather(value, "c", sizes["c"])


def local(sizes, node_feats, w_qkv, w_graph, ln_gain, out_grad, part_counts, send_rows, neighbours, neighbour_counts):
    rows = node_feats.shape[0]
    rim = send_rows.shape[2]
    steps = rows // BLOCK
    near = sizes["x"] * sizes["c"]
    parts = near * sizes["y"] * sizes["z"]
    f32, bf16 = jnp.float32, jnp.bfloat16
    smem = pl.BlockSpec(memory_space=pltpu.SMEM)
    shape = jax.ShapeDtypeStruct

    def whole(*shape):
        return pl.BlockSpec(shape, lambda i: (0,) * len(shape))

    by_row = pl.BlockSpec((BLOCK, D), lambda i: (i, 0))
    rows_f32, rows_bf16 = shape((rows, D), f32), shape((rows, D), bf16)
    packed_whole, packed_shape = whole(TILE, 1, PACK), shape((TILE, 1, PACK), f32)
    kv_halves, vectors = pltpu.VMEM((2, D, D), bf16), pltpu.VMEM((TILE, D), f32)

    packed, to_before, to_after, key_map, value_rows = pl.pallas_call(
        key_kernel,
        grid=(steps,),
        in_specs=[smem, by_row, whole(rows, D), whole(3, D, D), whole(1, 2, rim)],
        out_specs=[packed_whole, whole(rim, D), whole(rim, D), by_row, by_row],
        out_shape=[packed_shape, shape((rim, D), bf16), shape((rim, D), bf16), rows_f32, rows_f32],
        scratch_shapes=[pltpu.VMEM((D, D), f32), pltpu.VMEM((1, D), f32)],
        name="keys",
    )(part_counts, node_feats, node_feats, w_qkv, send_rows)

    up = [(i, i + 1) for i in range(parts - 1)]
    down = [(j, i) for i, j in up]
    share = scatter_sum(packed, ("x", "c"), near)
    left = lax.ppermute(to_after, FINE, up)
    right = lax.ppermute(to_before, FINE, down)
    share = gather_sum(share, "y", sizes["y"])
    share, left, right = lax.optimization_barrier((share, left, right))
    agg, graph, query_map = pl.pallas_call(
        prep_kernel,
        out_shape=[rows_bf16, rows_f32, rows_f32],
        scratch_shapes=[pltpu.VMEM((rows + 2 * rim, rows), bf16)],
        cost_estimate=pl.CostEstimate(flops=10**9, bytes_accessed=10**7, transcendentals=0),
        name="prepare",
    )(neighbours.T, neighbour_counts.reshape(1, rows), node_feats, left, right, w_qkv, w_graph)
    share = gather_sum(share, "z", sizes["z"])
    share, agg, graph, query_map = lax.optimization_barrier((share, agg, graph, query_map))
    packed = gather(share, ("x", "c"), near)

    node_out, dgraph, dnum, dden, dpacked = pl.pallas_call(
        mix_kernel,
        grid=(steps,),
        in_specs=[smem, packed_whole, by_row, by_row, by_row, by_row, whole(1, D)],
        out_specs=[by_row, by_row, by_row, by_row, packed_whole],
        out_shape=[rows_bf16, rows_bf16, rows_f32, rows_f32, packed_shape],
        scratch_shapes=[kv_halves, vectors, pltpu.VMEM((D, D), f32), pltpu.VMEM((1, D), f32)],
        name="mix",
    )(part_counts, packed, query_map, value_rows, graph, out_grad, ln_gain.reshape(1, D))

    share = scatter_sum(dpacked, ("x", "c"), near)
    share = gather_sum(share, "y", sizes["y"])
    terms = pl.pallas_call(
        query_kernel,
        grid=(steps,),
        in_specs=[packed_whole, by_row, by_row, by_row, by_row, by_row, by_row],
        out_specs=whole(2, D, D),
        out_shape=shape((4, D, D), f32),
        scratch_shapes=[kv_halves, vectors],
        cost_estimate=pl.CostEstimate(flops=10**9, bytes_accessed=10**7, transcendentals=0),
        name="queries",
    )(packed, node_feats, agg, query_map, dgraph, dnum, dden)
    share = gather_sum(share, "z", sizes["z"])
    share, terms = lax.optimization_barrier((share, terms))
    dpacked = gather(share, ("x", "c"), near)

    terms = pl.pallas_call(
        grad_kernel,
        grid=(steps,),
        in_specs=[smem, packed_whole, by_row, by_row, by_row, by_row, pl.BlockSpec(memory_space=pl.ANY)],
        out_specs=pl.BlockSpec((2, D, D), lambda i: (1, 0, 0)),
        out_shape=shape((4, D, D), f32),
        scratch_shapes=[kv_halves, vectors],
        input_output_aliases={6: 0},
        name="grads",
    )(part_counts, dpacked, node_feats, key_map, value_rows, dnum, terms)

    scale = lax.rsqrt(packed[1, :, 4 * D : 4 * D + 1])
    total = sum_terms(terms.reshape(4 * D, D), sizes, scale).reshape(4, D, D)
    return node_out, total[1:], total[0]


def solution(mesh):
    sizes = dict(zip(FINE, (*MESH_FACTORS[mesh.shape["dom"]], mesh.shape["head"])))
    fine = Mesh(mesh.devices.reshape(tuple(sizes.values())), FINE)
    return jax.shard_map(
        functools.partial(local, sizes),
        mesh=fine,
        in_specs=(
            P(FINE, None), P(), P(), P(), P(FINE, None), P(FINE), P(FINE, None, None), P(FINE, None), P(FINE),
        ),
        out_specs=(P(FINE, None), P(), P()),
        check_vma=False,
    )
```

time: 204 us -> 192 us (0.941)
  blocking collectives: 136 us -> 117 us
  starting transfers between devices: 17.9 us -> 29.9 us
  local copies, waits for them, and re-layouts: 9.11 us -> 5.62 us
    all_to_all x6, blocking collectives: 91.3 us -> 65.4 us  [gather(): return lax.all_to_all(copies, axes, 0, 0, tiled=True)]
    all_to_all x1 -> x4, starting transfers between devices: 6.49 us -> 17.2 us  [gather(): return lax.all_to_all(copies, axes, 0, 0, tiled=True)]
    all_to_all x1 -> x0, waiting for transfers between devices: 9.79 us -> none  [scatter_sum(): parts = lax.all_to_all(value, axes, 0, 0, tiled=True)]
    all_to_all x1 -> x4, waiting for transfers between devices: 0.01 us -> 8.73 us  [gather(): return lax.all_to_all(copies, axes, 0, 0, tiled=True)]
    all_to_all x4 -> x5, blocking collectives: 44.6 us -> 51.6 us  [scatter_sum(): parts = lax.all_to_all(value, axes, 0, 0, tiled=True)]
    ppermute x1, starting transfers between devices: 4.1 us -> 9.5 us  [local(): right = lax.ppermute(to_before, FINE, down)]
    all_to_all x1 -> x0, starting transfers between devices: 4.62 us -> none  [scatter_sum(): parts = lax.all_to_all(value, axes, 0, 0, tiled=True)]
    unnamed x13 -> x8, local copies, waits for them, and re-layouts: 2.67 us -> 0.02 us
  transfers between devices with their start and end apart: 4 -> 6, of which waited for: 2 -> 4; matrix products, arithmetic and copies ran while one was open for 1% -> 1% of each run, Pallas kernels for 3% -> 6%
where the time goes in v2:
time: 192 us; the launch traced here: 191 us
  blocking collectives  117 us (61%)
  starting transfers between devices  29.9 us (16%)
  Pallas kernels  26.3 us (14%)
  waiting for transfers between devices  9.65 us (5%)
  local copies, waits for them, and re-layouts  5.62 us (3%)
  between operations  2.17 us (1%)
    all_to_all x6, blocking collectives, gather(): return lax.all_to_all(copies, axes, 0, 0, tiled=True)  65.4 us
    all_to_all x5, blocking collectives, scatter_sum(): parts = lax.all_to_all(value, axes, 0, 0, tiled=True)  51.6 us
    all_to_all x4, starting transfers between devices, gather(): return lax.all_to_all(copies, axes, 0, 0, tiled=True)  17.2 us
    ppermute x1, starting transfers between devices, local(): right = lax.ppermute(to_before, FINE, down)  9.5 us
    all_to_all x4, waiting for transfers between devices, gather(): return lax.all_to_all(copies, axes, 0, 0, tiled=True)  8.73 us
    pallas_call x1, Pallas kernels, local(): pl.pallas_call(prep_kernel, out_shape=[rows_bf16, rows_f32, rows_f32], sc...  6.42 us
    pallas_call x1, Pallas kernels, local(): pl.pallas_call(mix_kernel, grid=(steps,), in_specs=[smem, packed_whole, b...  5.42 us
    pallas_call x1, Pallas kernels, local(): pl.pallas_call(grad_kernel, grid=(steps,), in_specs=[smem, packed_whole,...  4.9 us
  transfers between devices with their start and end apart: 6, of which 4 were waited for; matrix products, arithmetic and copies ran while one was open for 1% of the time, Pallas kernels for 6%

profile of v2, /device:TPU:1, one launch (start us, length us, event | category | flops | bytes accessed | tf_op | source)
XLA Modules:
  0.0 191.1 jit_solution(15965285188806554508)
XLA Ops:
  1.3 4.7 %keys.1 = (f32[8,1,1280]{2,1,0:T(1,128)}, bf16[64,256]{1,0:T(8,128)(2,1)}, bf16[64,256]{1,0:T(8,128)(2,1)}, f32[512,256]{1,0:T(8,128)}, f32[512,256]{1,0:T(8,128)}) custom-call(s32[1]{0:T(128)S(6)} %copy.22.count_ref, bf16[512,256]{1,0:T(8,128)(2,1)} %feats_ref.7, bf16[512,256]{1,0:T(8,128)(2,1)} %feats_ref.7, bf16[3,256,256]{2,1,0:T(8,128)(2,1)} %w_ref.3, ...), custom_call_target="tpu_custom_call" | custom-call | tf_op jit(solution)/shard_map/keys/pallas_call | solution.py:285
  6.0 14.8 %all_to_all.94 = f32[8,1,1280]{2,1,0:T(1,128)S(1)} all-to-all(f32[8,1,1280]{2,1,0:T(1,128)} %get-tuple-element.25), channel_id=1, replica_groups=mesh['x'=4,'y'=8,'c'=2,'z'=8] {'x','c'}, dimensions={0} | all-to-all | bytes 81920 | tf_op jit(solution)/shard_map/all_to_all | solution.py:244
  20.8 0.6 reshape.109
  21.5 0.0 copy-start.2
  21.5 0.0 copy-start
  21.5 3.5 %all-to-all-start.1 = ((f32[8,1,1280]{2,1,0:T(1,128)}), f32[8,1,1280]{2,1,0:T(1,128)S(1)}, u32[]{:S(2)}, u32[]{:S(2)}) async-start(f32[8,1,1280]{2,1,0:T(1,128)} %reshape.109), calls=%async_computation.1 | async-start | bytes 81920 | tf_op jit(solution)/shard_map/all_to_all | solution.py:250
  25.0 0.0 copy-done.2
  25.0 3.2 %collective-permute-start = (bf16[64,256]{1,0:T(8,128)(2,1)S(1)}, bf16[64,256]{1,0:T(8,128)(2,1)S(1)}, u32[]{:S(2)}, u32[]{:S(2)}) collective-permute-start(bf16[64,256]{1,0:T(8,128)(2,1)S(1)} %copy-done.2), channel_id=1, source_target_pairs={{0,1},{1,2},{2,3},{3,4},{4,5},{5,6},{6,7},{7,8},{8,9},{9,10},{10,1... | collective-permute-start | bytes 98312 | tf_op jit(solution)/shard_map/ppermute | solution.py:298
  28.2 0.0 copy-done
  28.2 9.5 %collective-permute-start.1 = (bf16[64,256]{1,0:T(8,128)(2,1)S(1)}, bf16[64,256]{1,0:T(8,128)(2,1)S(1)}, u32[]{:S(2)}, u32[]{:S(2)}) collective-permute-start(bf16[64,256]{1,0:T(8,128)(2,1)S(1)} %copy-done), channel_id=1, source_target_pairs={{1,0},{2,1},{3,2},{4,3},{5,4},{6,5},{7,6},{8,7},{9,8},{10,9},{11,1... | collective-permute-start | bytes 98312 | tf_op jit(solution)/shard_map/ppermute | solution.py:299
  37.7 0.0 all-to-all-done.1
  37.7 0.0 collective-permute-done.left_ref
  37.7 0.0 copy-start.1
  37.8 0.9 collective-permute-done.1.right_ref
  38.7 0.0 copy-start.3
  38.7 0.6 reshape.110
  39.3 0.0 copy-done.1
  39.3 0.0 copy-done.3
  39.3 4.8 %all-to-all-start.2 = ((f32[8,1,1280]{2,1,0:T(1,128)}), f32[8,1,1280]{2,1,0:T(1,128)S(1)}, u32[]{:S(2)}, u32[]{:S(2)}) async-start(f32[8,1,1280]{2,1,0:T(1,128)} %reshape.110), calls=%async_computation.2 | async-start | bytes 81920 | tf_op jit(solution)/shard_map/all_to_all | solution.py:250
  44.1 6.4 %prepare.1 = (bf16[512,256]{1,0:T(8,128)(2,1)}, f32[512,256]{1,0:T(8,128)}, f32[512,256]{1,0:T(8,128)}) custom-call(s32[16,512]{1,0:T(8,128)} %bitcast.20, s32[1,512]{1,0:T(1,128)} %bitcast.21, bf16[512,256]{1,0:T(8,128)(2,1)} %feats_ref.7, bf16[64,256]{1,0:T(8,128)(2,1)} %copy-done.1, bf16[64,256]{1,0:T(8,128)(2,1)} %copy-done.3, ...), custom_call_target="tpu_custom_call" | custom-call | flops 1000000000 | bytes 10000000 | tf_op jit(solution)/shard_map/prepare/pallas_call | solution.py:302
  50.6 0.5 all-to-all-done.2
  51.2 10.5 %all_to_all.95.packed_ref = f32[8,1,1280]{2,1,0:T(1,128)} all-to-all(f32[8,1,1280]{2,1,0:T(1,128)S(1)} %reshape.112), channel_id=1, replica_groups=mesh['x'=4,'y'=8,'c'=2,'z'=8] {'x','c'}, dimensions={0} | all-to-all | bytes 81920 | tf_op jit(solution)/shard_map/all_to_all | solution.py:250
  61.7 5.4 %mix.1 = (bf16[512,256]{1,0:T(8,128)(2,1)}, bf16[512,256]{1,0:T(8,128)(2,1)}, f32[512,256]{1,0:T(8,128)}, f32[512,256]{1,0:T(8,128)}, f32[8,1,1280]{2,1,0:T(1,128)}) custom-call(s32[1]{0:T(128)S(6)} %copy.22.count_ref, f32[8,1,1280]{2,1,0:T(1,128)} %all_to_all.95.packed_ref, f32[512,256]{1,0:T(8,128)} %get-tuple-element.35.query_ref, ...), custom_call_target="tpu_custom_call" | custom-call | tf_op jit(solution)/shard_map/mix/pallas_call | solution.py:313
  67.1 8.7 %all_to_all.96 = f32[8,1,1280]{2,1,0:T(1,128)S(1)} all-to-all(f32[8,1,1280]{2,1,0:T(1,128)} %get-tuple-element.39), channel_id=1, replica_groups=mesh['x'=4,'y'=8,'c'=2,'z'=8] {'x','c'}, dimensions={0} | all-to-all | bytes 81920 | tf_op jit(solution)/shard_map/all_to_all | solution.py:244
  75.9 13.7 %all_to_all.97 = f32[8,1,1280]{2,1,0:T(1,128)S(1)} all-to-all(f32[8,1,1280]{2,1,0:T(1,128)S(1)} %reshape.114), channel_id=1, replica_groups=mesh['x'=4,'y'=8,'c'=2,'z'=8] {'y'}, dimensions={0} | all-to-all | bytes 81920 | tf_op jit(solution)/shard_map/all_to_all | solution.py:250
  89.6 0.6 reshape.115
  90.3 5.2 %all-to-all-start.6 = ((f32[8,1,1280]{2,1,0:T(1,128)}), f32[8,1,1280]{2,1,0:T(1,128)S(1)}, u32[]{:S(2)}, u32[]{:S(2)}) async-start(f32[8,1,1280]{2,1,0:T(1,128)} %reshape.115), calls=%async_computation.6 | async-start | bytes 81920 | tf_op jit(solution)/shard_map/all_to_all | solution.py:250
  95.5 4.9 %queries.1.held_ref = f32[4,256,256]{2,1,0:T(8,128)} custom-call(f32[8,1,1280]{2,1,0:T(1,128)} %all_to_all.95.packed_ref, bf16[512,256]{1,0:T(8,128)(2,1)} %feats_ref.7, bf16[512,256]{1,0:T(8,128)(2,1)} %get-tuple-element.40.agg_ref, f32[512,256]{1,0:T(8,128)} %get-tuple-element.35.query_ref, bf16[512,256]{1,0:T(8,128)(2,1)} %get-tuple-element.41.dgraph_ref, ...), custom_call_target="tpu_custom_call" | custom-call | flops 1000000000 | bytes 10000000 | tf_op jit(solution)/shard_map/queries/pallas_call | solution.py:325
  100.4 2.1 %all-to-all-done.6 = f32[8,1,1280]{2,1,0:T(1,128)S(1)} async-done(((f32[8,1,1280]{2,1,0:T(1,128)}), f32[8,1,1280]{2,1,0:T(1,128)S(1)}, u32[]{:S(2)}, u32[]{:S(2)}) %all-to-all-start.6) | async-done | bytes 40992 | tf_op jit(solution)/shard_map/all_to_all | solution.py:250
  102.6 11.4 %all_to_all.98.packed_ref = f32[8,1,1280]{2,1,0:T(1,128)} all-to-all(f32[8,1,1280]{2,1,0:T(1,128)S(1)} %reshape.116), channel_id=1, replica_groups=mesh['x'=4,'y'=8,'c'=2,'z'=8] {'x','c'}, dimensions={0} | all-to-all | bytes 81920 | tf_op jit(solution)/shard_map/all_to_all | solution.py:250
  114.0 4.9 %grads.1 = f32[4,256,256]{2,1,0:T(8,128)} custom-call(s32[1]{0:T(128)S(6)} %copy.22.count_ref, f32[8,1,1280]{2,1,0:T(1,128)} %all_to_all.98.packed_ref, bf16[512,256]{1,0:T(8,128)(2,1)} %feats_ref.7, f32[512,256]{1,0:T(8,128)} %get-tuple-element.45.key_ref, f32[512,256]{1,0:T(8,128)} %get-tuple-element.36.value_ref, ...), custom_call_target="tpu_custom_call", output_to_operand_aliasing={{}: (6, {})} | custom-call | tf_op jit(solution)/shard_map/grads/pallas_call | solution.py:339
  118.9 6.1 %all_to_all.99 = f32[2,512,256]{2,1,0:T(8,128)S(1)} all-to-all(f32[2,512,256]{2,1,0:T(8,128)} %bitcast.13), channel_id=1, replica_groups=mesh['x'=4,'y'=8,'c'=2,'z'=8] {'c'}, dimensions={0} | all-to-all | bytes 2097152 | tf_op jit(solution)/shard_map/all_to_all | solution.py:244
  124.9 0.1 reduce_sum.105
  125.0 11.6 %all_to_all.100 = f32[4,128,256]{2,1,0:T(8,128)S(1)} all-to-all(f32[4,128,256]{2,1,0:T(8,128)S(1)} %bitcast.15), channel_id=1, replica_groups=mesh['x'=4,'y'=8,'c'=2,'z'=8] {'x'}, dimensions={0} | all-to-all | bytes 1048576 | tf_op jit(solution)/shard_map/all_to_all | solution.py:244
  136.7 10.3 %all_to_all.101 = f32[8,16,256]{2,1,0:T(8,128)S(1)} all-to-all(f32[8,16,256]{2,1,0:T(8,128)S(1)} %bitcast.18), channel_id=1, replica_groups=mesh['x'=4,'y'=8,'c'=2,'z'=8] {'y'}, dimensions={0} | all-to-all | bytes 262144 | tf_op jit(solution)/shard_map/all_to_all | solution.py:244
  147.1 0.7 broadcast_in_dim.21
  147.7 3.7 %all-to-all-start.11 = ((f32[8,16,256]{2,1,0:T(8,128)}), f32[8,16,256]{2,1,0:T(8,128)S(1)}, u32[]{:S(2)}, u32[]{:S(2)}) async-start(f32[8,16,256]{2,1,0:T(8,128)} %broadcast_in_dim.21), calls=%async_computation.11 | async-start | bytes 262144 | tf_op jit(solution)/shard_map/all_to_all | solution.py:250
  151.4 1.2 slice.17
  153.2 6.1 %all-to-all-done.11 = f32[8,16,256]{2,1,0:T(8,128)S(1)} async-done(((f32[8,16,256]{2,1,0:T(8,128)}), f32[8,16,256]{2,1,0:T(8,128)S(1)}, u32[]{:S(2)}, u32[]{:S(2)}) %all-to-all-start.11) | async-done | bytes 131104 | tf_op jit(solution)/shard_map/all_to_all | solution.py:250
  159.4 10.3 %all_to_all.102 = f32[8,16,256]{2,1,0:T(8,128)S(1)} all-to-all(f32[8,16,256]{2,1,0:T(8,128)S(1)} %broadcast_in_dim.22), channel_id=1, replica_groups=mesh['x'=4,'y'=8,'c'=2,'z'=8] {'y'}, dimensions={0} | all-to-all | bytes 262144 | tf_op jit(solution)/shard_map/all_to_all | solution.py:250
  169.7 9.3 %all_to_all.103 = f32[4,128,256]{2,1,0:T(8,128)S(1)} all-to-all(f32[4,128,256]{2,1,0:T(8,128)S(1)} %broadcast_in_dim.24), channel_id=1, replica_groups=mesh['x'=4,'y'=8,'c'=2,'z'=8] {'x'}, dimensions={0} | all-to-all | bytes 1048576 | tf_op jit(solution)/shard_map/all_to_all | solution.py:250
  179.1 0.1 broadcast_in_dim.26
  179.1 10.3 %all_to_all.104 = f32[2,512,256]{2,1,0:T(8,128)S(1)} all-to-all(f32[2,512,256]{2,1,0:T(8,128)S(1)} %broadcast_in_dim.26), channel_id=1, replica_groups=mesh['x'=4,'y'=8,'c'=2,'z'=8] {'c'}, dimensions={0} | all-to-all | bytes 2097152 | tf_op jit(solution)/shard_map/all_to_all | solution.py:250
  189.4 0.9 slice.18
  190.3 0.7 slice.19
  (21 shorter events, 0.5 us)
Async XLA Ops:
  21.5 3.5 %copy-start.2 = (bf16[64,256]{1,0:T(8,128)(2,1)S(1)}, bf16[64,256]{1,0:T(8,128)(2,1)}, u32[]{:S(2)}) copy-start(bf16[64,256]{1,0:T(8,128)(2,1)} %get-tuple-element.26) | copy-start | bytes 98308
  21.5 6.7 %copy-start = (bf16[64,256]{1,0:T(8,128)(2,1)S(1)}, bf16[64,256]{1,0:T(8,128)(2,1)}, u32[]{:S(2)}) copy-start(bf16[64,256]{1,0:T(8,128)(2,1)} %get-tuple-element.27) | copy-start | bytes 98308
  21.5 16.2 %all-to-all-start.1 = ((f32[8,1,1280]{2,1,0:T(1,128)}), f32[8,1,1280]{2,1,0:T(1,128)S(1)}, u32[]{:S(2)}, u32[]{:S(2)}) async-start(f32[8,1,1280]{2,1,0:T(1,128)} %reshape.109), calls=%async_computation.1 | async-start | bytes 81920 | tf_op jit(solution)/shard_map/all_to_all | solution.py:250
  25.0 12.8 %collective-permute-start = (bf16[64,256]{1,0:T(8,128)(2,1)S(1)}, bf16[64,256]{1,0:T(8,128)(2,1)S(1)}, u32[]{:S(2)}, u32[]{:S(2)}) collective-permute-start(bf16[64,256]{1,0:T(8,128)(2,1)S(1)} %copy-done.2), channel_id=1, source_target_pairs={{0,1},{1,2},{2,3},{3,4},{4,5},{5,6},{6,7},{7,8},{8,9},{9,10},{10,1... | collective-permute-start | bytes 98312 | tf_op jit(solution)/shard_map/ppermute | solution.py:298
  28.2 10.5 %collective-permute-start.1 = (bf16[64,256]{1,0:T(8,128)(2,1)S(1)}, bf16[64,256]{1,0:T(8,128)(2,1)S(1)}, u32[]{:S(2)}, u32[]{:S(2)}) collective-permute-start(bf16[64,256]{1,0:T(8,128)(2,1)S(1)} %copy-done), channel_id=1, source_target_pairs={{1,0},{2,1},{3,2},{4,3},{5,4},{6,5},{7,6},{8,7},{9,8},{10,9},{11,1... | collective-permute-start | bytes 98312 | tf_op jit(solution)/shard_map/ppermute | solution.py:299
  37.7 1.6 copy-start.1
  38.7 0.7 copy-start.3
  39.3 11.8 %all-to-all-start.2 = ((f32[8,1,1280]{2,1,0:T(1,128)}), f32[8,1,1280]{2,1,0:T(1,128)S(1)}, u32[]{:S(2)}, u32[]{:S(2)}) async-start(f32[8,1,1280]{2,1,0:T(1,128)} %reshape.110), calls=%async_computation.2 | async-start | bytes 81920 | tf_op jit(solution)/shard_map/all_to_all | solution.py:250
  90.3 12.2 %all-to-all-start.6 = ((f32[8,1,1280]{2,1,0:T(1,128)}), f32[8,1,1280]{2,1,0:T(1,128)S(1)}, u32[]{:S(2)}, u32[]{:S(2)}) async-start(f32[8,1,1280]{2,1,0:T(1,128)} %reshape.115), calls=%async_computation.6 | async-start | bytes 81920 | tf_op jit(solution)/shard_map/all_to_all | solution.py:250
  147.7 11.6 %all-to-all-start.11 = ((f32[8,16,256]{2,1,0:T(8,128)}), f32[8,16,256]{2,1,0:T(8,128)S(1)}, u32[]{:S(2)}, u32[]{:S(2)}) async-start(f32[8,16,256]{2,1,0:T(8,128)} %broadcast_in_dim.21), calls=%async_computation.11 | async-start | bytes 262144 | tf_op jit(solution)/shard_map/all_to_all | solution.py:250

commit v3 on v2

v3 whole, which is shorter than its diff:
```python
import functools

import jax
import jax.numpy as jnp
from jax import lax
from jax.experimental import pallas as pl
from jax.experimental.pallas import tpu as pltpu
from jax.sharding import Mesh, PartitionSpec as P

D = 256
DH = 32
HEADS = D // DH
TILE = 8
PACK = 5 * D
VMEM_LIMIT = 16 << 20
MESH_FACTORS = {64: (4, 8, 2), 8: (2, 2, 2)}
FINE = ("x", "y", "c", "z")
ROWS_FIRST = (((0,), (0,)), ((), ()))
COLS_LAST = (((1,), (1,)), ((), ()))


def dot(a, b, dims=(((1,), (0,)), ((), ()))):
    return lax.dot_general(a, b, dims, preferred_element_type=jnp.float32)


def feature_map(value):
    return jnp.where(value > 0, value + 1.0, jnp.exp(jnp.minimum(value, 0.0)))


def same_head():
    row = lax.broadcasted_iota(jnp.int32, (D, D), 0) // DH
    col = lax.broadcasted_iota(jnp.int32, (D, D), 1) // DH
    return row == col


def alive_of(count_ref, rows):
    return (lax.broadcasted_iota(jnp.int32, (rows, 1), 0) < count_ref[...]).astype(jnp.float32)


def store_packed(out_ref, dense, vectors):
    kept = jnp.where(same_head(), dense, 0.0)
    folded = kept[0:DH]
    for h in range(1, HEADS):
        folded = folded + kept[h * DH : (h + 1) * DH]
    row = lax.broadcasted_iota(jnp.int32, (TILE, D), 0)
    last = jnp.zeros((TILE, D), jnp.float32)
    for i, vector in enumerate(vectors):
        last = jnp.where(row == i, vector, last)
    tiles = [folded[t * TILE : (t + 1) * TILE] for t in range(4)] + [last]
    for t, tile in enumerate(tiles):
        for r in range(TILE):
            out_ref[r, :, t * D : (t + 1) * D] = tile[r : r + 1]


def load_packed(packed_ref):
    tiles = [
        jnp.concatenate([packed_ref[r, :, t * D : (t + 1) * D] for r in range(TILE)], axis=0) for t in range(5)
    ]
    folded = jnp.concatenate(tiles[:4], axis=0)
    return jnp.where(same_head(), jnp.concatenate([folded] * HEADS, axis=0), 0.0), tiles[4]


def halves(value):
    high = value.astype(jnp.bfloat16)
    return high, (value - high.astype(jnp.float32)).astype(jnp.bfloat16)


def dot3(a, b, dims=(((1,), (0,)), ((), ()))):
    return dot(a[0], b[0], dims) + (dot(a[0], b[1], dims) + dot(a[1], b[0], dims))


def head_sums(value, heads):
    high, low = halves(value)
    return dot(high, heads) + dot(low, heads)


def key_kernel(count_ref, feats_ref, w_ref, send_ref, packed_ref, before_ref, after_ref, key_ref, value_ref):
    feats = feats_ref[...]
    slot = lax.broadcasted_iota(jnp.int32, (feats.shape[0], send_ref.shape[2]), 0)
    for side, out in ((0, before_ref), (1, after_ref)):
        chosen = (slot == send_ref[0, side : side + 1, :]).astype(jnp.bfloat16)
        out[...] = dot(chosen, feats, ROWS_FIRST).astype(jnp.bfloat16)
    key_map = feature_map(dot(feats, w_ref[1]))
    value_rows = dot(feats, w_ref[2])
    key_ref[...] = key_map
    value_ref[...] = value_rows
    key_map = key_map * alive_of(count_ref, feats.shape[0])
    kv = dot3(halves(key_map), halves(value_rows), ROWS_FIRST)
    live = jnp.broadcast_to(count_ref[...].astype(jnp.float32), (1, D))
    store_packed(packed_ref, kv, [jnp.sum(key_map, axis=0, keepdims=True), live])


def hit_kernel(nbr_ref, count_ref, hits_ref):
    wide, total = hits_ref.shape
    slots = nbr_ref.shape[0]
    sub = 32
    for b in range(total // 128):
        at = slice(b * 128, (b + 1) * 128)
        slot = lax.broadcasted_iota(jnp.int32, (slots, 128), 0)
        named = jnp.where(slot < count_ref[:, at], nbr_ref[:, at], -1)
        rows = [jnp.broadcast_to(named[s : s + 1], (sub, 128)) for s in range(slots)]
        own = lax.broadcasted_iota(jnp.int32, (sub, 128), 1) + b * 128
        place0 = lax.broadcasted_iota(jnp.int32, (sub, 128), 0)

        def body(i, carry):
            first = pl.multiple_of(i * sub, sub)
            place = place0 + first
            hits = (place == own).astype(jnp.float32)
            for s in range(slots):
                hits = hits + (place == rows[s]).astype(jnp.float32)
            hits_ref[pl.ds(first, sub), at] = hits.astype(jnp.bfloat16)
            return carry

        lax.fori_loop(0, wide // sub, body, 0)


def graph_kernel(hits_ref, feats_ref, left_ref, right_ref, wg_ref, agg_ref, graph_ref):
    total = feats_ref.shape[0]
    rim = left_ref.shape[0]
    summed = dot(hits_ref[:total, :], feats_ref[...], ROWS_FIRST)
    summed += dot(hits_ref[total : total + rim, :], left_ref[...], ROWS_FIRST)
    summed += dot(hits_ref[total + rim :, :], right_ref[...], ROWS_FIRST)
    named = dot(hits_ref[...], jnp.ones((total + 2 * rim, 128), jnp.bfloat16), ROWS_FIRST)
    agg = (summed / jnp.concatenate([named, named], axis=1)).astype(jnp.bfloat16)
    agg_ref[...] = agg
    graph_ref[...] = 0.5 * dot(agg, wg_ref[...])


def project_kernel(feats_ref, w_ref, query_ref):
    query_ref[...] = feature_map(dot(feats_ref[...], w_ref[0]))


def mix_kernel(
    count_ref, packed_ref, query_ref, value_ref, graph_ref, grad_ref, gain_ref,
    out_ref, dgraph_ref, dnum_ref, dden_ref, packed_out_ref, scale_ref,
):
    kv, vectors = load_packed(packed_ref)
    kv = halves(kv)
    ks, live = vectors[0:1], vectors[1:2]
    factor = 1.0 / (DH * live)
    scale_ref[...] = lax.rsqrt(live)
    heads = same_head().astype(jnp.bfloat16)
    gain_alive = gain_ref[...] * alive_of(count_ref, query_ref.shape[0])

    query_map = query_ref[...]
    query_halves = halves(query_map)
    numer = value_ref[...] + factor * dot3(query_halves, kv)
    denom = 1.0 + factor * head_sums(query_map * ks, heads)
    inverse = 1.0 / denom
    attn = numer * inverse
    mixed = 0.5 * attn + graph_ref[...]
    mean = jnp.sum(mixed, -1, keepdims=True) / D
    spread = jnp.sum(mixed * mixed, -1, keepdims=True) / D - mean * mean
    rstd = lax.rsqrt(spread + 1e-05)
    normed = (mixed - mean) * rstd
    out_ref[...] = (normed * gain_alive).astype(jnp.bfloat16)
    dnormed = grad_ref[...].astype(jnp.float32) * gain_alive
    dmixed = rstd * (
        dnormed
        - jnp.sum(dnormed, -1, keepdims=True) / D
        - normed * (jnp.sum(dnormed * normed, -1, keepdims=True) / D)
    )
    dattn = 0.5 * dmixed
    dgraph_ref[...] = dattn.astype(jnp.bfloat16)
    dnum = dattn * inverse
    dnum_ref[...] = dnum
    dden = -head_sums(dattn * attn, heads) * inverse
    dden_ref[...] = dden
    dkv = dot3(query_halves, halves(dnum), ROWS_FIRST)
    dks = jnp.sum(query_map * dden, axis=0, keepdims=True)
    store_packed(packed_out_ref, factor * dkv, [factor * dks])


def query_kernel(packed_ref, feats_ref, agg_ref, query_ref, dgraph_ref, dnum_ref, dden_ref, terms_ref):
    kv, vectors = load_packed(packed_ref)
    factor = 1.0 / (DH * vectors[1:2])
    slope = jnp.minimum(query_ref[...], 1.0)
    dquery = factor * (dot3(halves(dnum_ref[...]), halves(kv), COLS_LAST) + dden_ref[...] * vectors[0:1]) * slope
    terms_ref[0] = dot(agg_ref[...], dgraph_ref[...], ROWS_FIRST)
    terms_ref[1] = dot(feats_ref[...], dquery.astype(jnp.bfloat16), ROWS_FIRST)


def grad_kernel(count_ref, packed_ref, feats_ref, key_ref, value_ref, dnum_ref, held_ref, terms_ref):
    terms_ref[0] = held_ref[0]
    terms_ref[1] = held_ref[1]
    dkv, vectors = load_packed(packed_ref)
    dkv = halves(dkv)
    feats = feats_ref[...]
    alive = alive_of(count_ref, feats.shape[0])
    key_map = key_ref[...]
    slope = jnp.minimum(key_map, 1.0) * alive
    dvalue = dnum_ref[...] + dot3(halves(key_map * alive), dkv)
    dkey = (dot3(halves(value_ref[...]), dkv, COLS_LAST) + vectors[0:1]) * slope
    terms_ref[2] = dot(feats, dkey.astype(jnp.bfloat16), ROWS_FIRST)
    terms_ref[3] = dot(feats, dvalue.astype(jnp.bfloat16), ROWS_FIRST)


def call(kernel, name, shapes, *args):
    def here(one):
        return pl.BlockSpec(memory_space=pltpu.VMEM)

    return pl.pallas_call(
        kernel,
        in_specs=[here(arg) for arg in args],
        out_specs=jax.tree.map(here, shapes),
        out_shape=shapes,
        cost_estimate=pl.CostEstimate(flops=10**9, bytes_accessed=10**7, transcendentals=0),
        compiler_params=pltpu.CompilerParams(vmem_limit_bytes=VMEM_LIMIT),
        name=name,
    )(*args)


def scatter_sum(value, axes, count):
    parts = lax.all_to_all(value, axes, 0, 0, tiled=True)
    return jnp.sum(parts.reshape(count, value.shape[0] // count, *value.shape[1:]), axis=0)


def gather(value, axes, count):
    copies = jnp.broadcast_to(value[None], (count, *value.shape)).reshape(count * value.shape[0], *value.shape[1:])
    return lax.all_to_all(copies, axes, 0, 0, tiled=True)


def gather_sum(value, axes, count):
    return jnp.sum(gather(value, axes, count).reshape(count, *value.shape), axis=0)


def sum_terms(terms, sizes, scale):
    value = scatter_sum(terms, "c", sizes["c"])
    value = scatter_sum(value, "x", sizes["x"])
    value = scatter_sum(value, "y", sizes["y"])
    value = gather_sum(value, "z", sizes["z"]) * scale
    value = gather(value, "y", sizes["y"])
    value = gather(value, "x", sizes["x"])
    return gather(value, "c", sizes["c"])


def local(sizes, node_feats, w_qkv, w_graph, ln_gain, out_grad, part_counts, send_rows, neighbours, neighbour_counts):
    rows = node_feats.shape[0]
    rim = send_rows.shape[2]
    near = sizes["x"] * sizes["c"]
    parts = near * sizes["y"] * sizes["z"]
    f32, bf16 = jnp.float32, jnp.bfloat16
    shape = jax.ShapeDtypeStruct
    count = part_counts.reshape(1, 1)
    rows_f32, rows_bf16 = shape((rows, D), f32), shape((rows, D), bf16)
    packed_shape, rim_shape = shape((TILE, 1, PACK), f32), shape((rim, D), bf16)
    together = lax.optimization_barrier

    packed, to_before, to_after, key_map, value_rows = call(
        key_kernel, "keys", [packed_shape, rim_shape, rim_shape, rows_f32, rows_f32],
        count, node_feats, w_qkv, send_rows,
    )

    up = [(i, i + 1) for i in range(parts - 1)]
    down = [(j, i) for i, j in up]
    hits = call(
        hit_kernel, "hits", shape((rows + 2 * rim, rows), bf16), neighbours.T, neighbour_counts.reshape(1, rows)
    )
    share = scatter_sum(packed, ("x", "c"), near)
    share, hits, to_before, to_after = together((share, hits, to_before, to_after))
    left = lax.ppermute(to_after, FINE, up)
    right = lax.ppermute(to_before, FINE, down)
    share = gather_sum(share, "y", sizes["y"])
    share, left, right = together((share, left, right))
    agg, graph = call(graph_kernel, "graph", [rows_bf16, rows_f32], hits, node_feats, left, right, w_graph)
    share = gather_sum(share, "z", sizes["z"])
    share, agg, graph, feats_here = together((share, agg, graph, node_feats))
    query_map = call(project_kernel, "project", rows_f32, feats_here, w_qkv)
    packed = gather(share, ("x", "c"), near)

    node_out, dgraph, dnum, dden, dpacked, scale = call(
        mix_kernel, "mix", [rows_bf16, rows_bf16, rows_f32, rows_f32, packed_shape, shape((1, D), f32)],
        count, packed, query_map, value_rows, graph, out_grad, ln_gain.reshape(1, D),
    )

    share = scatter_sum(dpacked, ("x", "c"), near)
    share = gather_sum(share, "y", sizes["y"])
    terms = call(
        query_kernel, "queries", shape((2, D, D), f32), packed, node_feats, agg, query_map, dgraph, dnum, dden
    )
    share = gather_sum(share, "z", sizes["z"])
    share, terms = together((share, terms))
    dpacked = gather(share, ("x", "c"), near)

    terms = call(
        grad_kernel, "grads", shape((4, D, D), f32), count, dpacked, node_feats, key_map, value_rows, dnum, terms
    )

    total = sum_terms(terms.reshape(4 * D, D), sizes, scale).reshape(4, D, D)
    return node_out, total[1:], total[0]


def solution(mesh):
    sizes = dict(zip(FINE, (*MESH_FACTORS[mesh.shape["dom"]], mesh.shape["head"])))
    fine = Mesh(mesh.devices.reshape(tuple(sizes.values())), FINE)
    return jax.shard_map(
        functools.partial(local, sizes),
        mesh=fine,
        in_specs=(
            P(FINE, None), P(), P(), P(), P(FINE, None), P(FINE), P(FINE, None, None), P(FINE, None), P(FINE),
        ),
        out_specs=(P(FINE, None), P(), P()),
        check_vma=False,
    )
```

time: 192 us -> 181 us (0.943)
  blocking collectives: 117 us -> 98.8 us
  Pallas kernels: 26.3 us -> 9.09 us
  starting transfers between devices: 29.9 us -> 41 us
  local copies, waits for them, and re-layouts: 5.62 us -> 14.1 us
  waiting for transfers between devices: 9.65 us -> 14.7 us
    pallas_call x5 -> x7, Pallas kernels: 26.3 us -> 9.09 us  [call(): pl.pallas_call(kernel, in_specs=[here(arg) for arg in args], out_specs=ja...]
    all_to_all x5 -> x4, blocking collectives: 51.6 us -> 34.7 us  [scatter_sum(): parts = lax.all_to_all(value, axes, 0, 0, tiled=True)]
    all_to_all x0 -> x1, starting transfers between devices: none -> 10.2 us  [scatter_sum(): parts = lax.all_to_all(value, axes, 0, 0, tiled=True)]
    unnamed x8 -> x36, local copies, waits for them, and re-layouts: 0.02 us -> 9.73 us
    all_to_all x4, waiting for transfers between devices: 8.73 us -> 13.6 us  [gather(): return lax.all_to_all(copies, axes, 0, 0, tiled=True)]
  transfers between devices with their start and end apart: 6 -> 7, of which waited for: 4 -> 5; matrix products, arithmetic and copies ran while one was open for 1% -> 0% of each run, Pallas kernels for 6% -> 3%
where the time goes in v3:
time: 181 us; the launch traced here: 180 us
  blocking collectives  98.8 us (55%)
  starting transfers between devices  41 us (23%)
  waiting for transfers between devices  14.7 us (8%)
  local copies, waits for them, and re-layouts  14.1 us (8%)
  Pallas kernels  9.09 us (5%)
    all_to_all x6, blocking collectives, gather(): return lax.all_to_all(copies, axes, 0, 0, tiled=True)  64.1 us
    all_to_all x4, blocking collectives, scatter_sum(): parts = lax.all_to_all(value, axes, 0, 0, tiled=True)  34.7 us
    all_to_all x4, starting transfers between devices, gather(): return lax.all_to_all(copies, axes, 0, 0, tiled=True)  18.1 us
    all_to_all x4, waiting for transfers between devices, gather(): return lax.all_to_all(copies, axes, 0, 0, tiled=True)  13.6 us
    all_to_all x1, starting transfers between devices, scatter_sum(): parts = lax.all_to_all(value, axes, 0, 0, tiled=True)  10.2 us
    unnamed x36, local copies, waits for them, and re-layouts  9.73 us
    ppermute x1, starting transfers between devices, local(): right = lax.ppermute(to_before, FINE, down)  9.5 us
    pallas_call x7, Pallas kernels, call(): pl.pallas_call(kernel, in_specs=[here(arg) for arg in args], out_specs=ja...  9.09 us
  transfers between devices with their start and end apart: 7, of which 5 were waited for; matrix products, arithmetic and copies ran while one was open for 0% of the time, Pallas kernels for 3%

profile of v3, /device:TPU:1, one launch (start us, length us, event | category | flops | bytes accessed | tf_op | source)
XLA Modules:
  0.0 179.8 jit_solution(2186502459368155953)
XLA Ops:
  1.3 0.0 copy-start.8
  1.3 0.7 copy-done.8
  2.0 0.0 copy-start
  2.0 1.0 copy-done
  3.0 0.0 copy-start.3
  3.0 0.9 copy-done.3
  3.9 1.6 keys.1
  5.5 10.2 %all-to-all-start = ((f32[8,1,1280]{2,1,0:T(1,128)}), f32[8,1,1280]{2,1,0:T(1,128)S(1)}, u32[]{:S(2)}, u32[]{:S(2)}) async-start(f32[8,1,1280]{2,1,0:T(1,128)} %get-tuple-element.29), calls=%async_computation | async-start | bytes 81920 | tf_op jit(solution)/shard_map/all_to_all | solution.py:214
  15.7 0.0 copy-done.6
  15.7 0.7 copy-done.7
  16.4 3.0 %hits.1.hits_ref = bf16[640,512]{1,0:T(8,128)(2,1)S(1)} custom-call(s32[16,512]{1,0:T(8,128)S(1)} %bitcast.17, s32[1,512]{1,0:T(1,128)S(1)} %bitcast.18), custom_call_target="tpu_custom_call" | custom-call | flops 1000000000 | bytes 10000000 | tf_op jit(solution)/shard_map/hits/pallas_call | solution.py:202
  19.5 0.0 copy-start.16
  19.5 0.8 copy-done.16
  20.3 0.2 all-to-all-done
  20.6 0.6 reshape.127
  21.2 3.5 %all-to-all-start.1 = ((f32[8,1,1280]{2,1,0:T(1,128)}), f32[8,1,1280]{2,1,0:T(1,128)S(1)}, u32[]{:S(2)}, u32[]{:S(2)}) async-start(f32[8,1,1280]{2,1,0:T(1,128)} %reshape.127), calls=%async_computation.1 | async-start | bytes 81920 | tf_op jit(solution)/shard_map/all_to_all | solution.py:220
  24.7 3.1 %collective-permute-start = (bf16[64,256]{1,0:T(8,128)(2,1)S(1)}, bf16[64,256]{1,0:T(8,128)(2,1)S(1)}, u32[]{:S(2)}, u32[]{:S(2)}) collective-permute-start(bf16[64,256]{1,0:T(8,128)(2,1)S(1)} %get-tuple-element.33), channel_id=1, source_target_pairs={{0,1},{1,2},{2,3},{3,4},{4,5},{5,6},{6,7},{7,8},{8,9},{9,10},{10,1... | collective-permute-start | bytes 98312 | tf_op jit(solution)/shard_map/ppermute | solution.py:261
  27.9 9.5 %collective-permute-start.1 = (bf16[64,256]{1,0:T(8,128)(2,1)S(1)}, bf16[64,256]{1,0:T(8,128)(2,1)S(1)}, u32[]{:S(2)}, u32[]{:S(2)}) collective-permute-start(bf16[64,256]{1,0:T(8,128)(2,1)S(1)} %get-tuple-element.34), channel_id=1, source_target_pairs={{1,0},{2,1},{3,2},{4,3},{5,4},{6,5},{7,6},{8,7},{9,8},{10,9},{11,1... | collective-permute-start | bytes 98312 | tf_op jit(solution)/shard_map/ppermute | solution.py:262
  37.4 0.0 all-to-all-done.1
  37.4 0.0 collective-permute-done.left_ref
  37.5 0.9 collective-permute-done.1.right_ref
  38.4 0.6 reshape.128
  39.0 4.8 %all-to-all-start.2 = ((f32[8,1,1280]{2,1,0:T(1,128)}), f32[8,1,1280]{2,1,0:T(1,128)S(1)}, u32[]{:S(2)}, u32[]{:S(2)}) async-start(f32[8,1,1280]{2,1,0:T(1,128)} %reshape.128), calls=%async_computation.2 | async-start | bytes 81920 | tf_op jit(solution)/shard_map/all_to_all | solution.py:220
  43.8 0.0 copy-done.4
  43.8 0.0 copy-done.5
  43.8 0.0 copy-start.17
  43.9 1.1 copy-done.17
  44.9 0.8 graph.1
  45.8 0.0 copy-start.14
  45.8 5.0 %all-to-all-done.2 = f32[8,1,1280]{2,1,0:T(1,128)S(1)} async-done(((f32[8,1,1280]{2,1,0:T(1,128)}), f32[8,1,1280]{2,1,0:T(1,128)S(1)}, u32[]{:S(2)}, u32[]{:S(2)}) %all-to-all-start.2) | async-done | bytes 40992 | tf_op jit(solution)/shard_map/all_to_all | solution.py:220
  50.9 0.6 reshape.129
  51.5 6.5 %all-to-all-start.3 = ((f32[8,1,1280]{2,1,0:T(1,128)}), f32[8,1,1280]{2,1,0:T(1,128)S(1)}, u32[]{:S(2)}, u32[]{:S(2)}) async-start(f32[8,1,1280]{2,1,0:T(1,128)} %reshape.129), calls=%async_computation.3 | async-start | bytes 81920 | tf_op jit(solution)/shard_map/all_to_all | solution.py:220
  58.0 0.0 copy-done.1
  58.0 0.3 project.1.query_ref
  58.3 0.0 copy-done.14
  58.3 4.5 %all-to-all-done.3.packed_ref = f32[8,1,1280]{2,1,0:T(1,128)S(1)} async-done(((f32[8,1,1280]{2,1,0:T(1,128)}), f32[8,1,1280]{2,1,0:T(1,128)S(1)}, u32[]{:S(2)}, u32[]{:S(2)}) %all-to-all-start.3) | async-done | bytes 40992 | tf_op jit(solution)/shard_map/all_to_all | solution.py:220
  62.8 0.0 copy-done.2
  62.8 0.7 copy-done.9
  63.5 1.0 copy-done.15
  64.5 1.7 mix.1
  66.2 0.8 copy-done.10
  67.0 7.9 %all_to_all.94 = f32[8,1,1280]{2,1,0:T(1,128)S(1)} all-to-all(f32[8,1,1280]{2,1,0:T(1,128)S(1)} %get-tuple-element.46), channel_id=1, replica_groups=mesh['x'=4,'y'=8,'c'=2,'z'=8] {'x','c'}, dimensions={0} | all-to-all | bytes 81920 | tf_op jit(solution)/shard_map/all_to_all | solution.py:214
  74.9 13.7 %all_to_all.95 = f32[8,1,1280]{2,1,0:T(1,128)S(1)} all-to-all(f32[8,1,1280]{2,1,0:T(1,128)S(1)} %reshape.131), channel_id=1, replica_groups=mesh['x'=4,'y'=8,'c'=2,'z'=8] {'y'}, dimensions={0} | all-to-all | bytes 81920 | tf_op jit(solution)/shard_map/all_to_all | solution.py:220
  88.7 0.6 reshape.132
  89.3 3.3 %all-to-all-start.6 = ((f32[8,1,1280]{2,1,0:T(1,128)}), f32[8,1,1280]{2,1,0:T(1,128)S(1)}, u32[]{:S(2)}, u32[]{:S(2)}) async-start(f32[8,1,1280]{2,1,0:T(1,128)} %reshape.132), calls=%async_computation.6 | async-start | bytes 81920 | tf_op jit(solution)/shard_map/all_to_all | solution.py:220
  92.6 0.0 copy-done.12
  92.7 0.0 copy-start.11
  92.7 1.0 copy-done.11
  93.7 0.9 copy-done.13
  94.7 0.7 queries.1.held_ref
  95.4 4.1 %all-to-all-done.6 = f32[8,1,1280]{2,1,0:T(1,128)S(1)} async-done(((f32[8,1,1280]{2,1,0:T(1,128)}), f32[8,1,1280]{2,1,0:T(1,128)S(1)}, u32[]{:S(2)}, u32[]{:S(2)}) %all-to-all-start.6) | async-done | bytes 40992 | tf_op jit(solution)/shard_map/all_to_all | solution.py:220
  99.6 10.4 %all_to_all.96.packed_ref = f32[8,1,1280]{2,1,0:T(1,128)S(1)} all-to-all(f32[8,1,1280]{2,1,0:T(1,128)S(1)} %reshape.133), channel_id=1, replica_groups=mesh['x'=4,'y'=8,'c'=2,'z'=8] {'x','c'}, dimensions={0} | all-to-all | bytes 81920 | tf_op jit(solution)/shard_map/all_to_all | solution.py:220
  110.1 0.9 grads.1
  111.0 4.9 %all_to_all.97 = f32[2,512,256]{2,1,0:T(8,128)S(1)} all-to-all(f32[2,512,256]{2,1,0:T(8,128)S(1)} %bitcast.15), channel_id=1, replica_groups=mesh['x'=4,'y'=8,'c'=2,'z'=8] {'c'}, dimensions={0} | all-to-all | bytes 2097152 | tf_op jit(solution)/shard_map/all_to_all | solution.py:214
  115.9 0.1 reduce_sum.108
  116.0 11.6 %all_to_all.98 = f32[4,128,256]{2,1,0:T(8,128)S(1)} all-to-all(f32[4,128,256]{2,1,0:T(8,128)S(1)} %bitcast.23), channel_id=1, replica_groups=mesh['x'=4,'y'=8,'c'=2,'z'=8] {'x'}, dimensions={0} | all-to-all | bytes 1048576 | tf_op jit(solution)/shard_map/all_to_all | solution.py:214
  127.7 10.3 %all_to_all.99 = f32[8,16,256]{2,1,0:T(8,128)S(1)} all-to-all(f32[8,16,256]{2,1,0:T(8,128)S(1)} %bitcast.26), channel_id=1, replica_groups=mesh['x'=4,'y'=8,'c'=2,'z'=8] {'y'}, dimensions={0} | all-to-all | bytes 262144 | tf_op jit(solution)/shard_map/all_to_all | solution.py:214
  138.1 10.4 %all_to_all.100 = f32[8,16,256]{2,1,0:T(8,128)S(1)} all-to-all(f32[8,16,256]{2,1,0:T(8,128)S(1)} %broadcast_in_dim.24), channel_id=1, replica_groups=mesh['x'=4,'y'=8,'c'=2,'z'=8] {'z'}, dimensions={0} | all-to-all | bytes 262144 | tf_op jit(solution)/shard_map/all_to_all | solution.py:220
  148.5 10.4 %all_to_all.101 = f32[8,16,256]{2,1,0:T(8,128)S(1)} all-to-all(f32[8,16,256]{2,1,0:T(8,128)S(1)} %broadcast_in_dim.25), channel_id=1, replica_groups=mesh['x'=4,'y'=8,'c'=2,'z'=8] {'y'}, dimensions={0} | all-to-all | bytes 262144 | tf_op jit(solution)/shard_map/all_to_all | solution.py:220
  159.0 9.3 %all_to_all.102 = f32[4,128,256]{2,1,0:T(8,128)S(1)} all-to-all(f32[4,128,256]{2,1,0:T(8,128)S(1)} %broadcast_in_dim.27), channel_id=1, replica_groups=mesh['x'=4,'y'=8,'c'=2,'z'=8] {'x'}, dimensions={0} | all-to-all | bytes 1048576 | tf_op jit(solution)/shard_map/all_to_all | solution.py:220
  168.3 0.1 broadcast_in_dim.29
  168.4 9.8 %all_to_all.103 = f32[2,512,256]{2,1,0:T(8,128)S(1)} all-to-all(f32[2,512,256]{2,1,0:T(8,128)S(1)} %broadcast_in_dim.29), channel_id=1, replica_groups=mesh['x'=4,'y'=8,'c'=2,'z'=8] {'c'}, dimensions={0} | all-to-all | bytes 2097152 | tf_op jit(solution)/shard_map/all_to_all | solution.py:220
  178.2 0.7 slice.14
  178.9 0.9 slice.13
  (34 shorter events, 0.5 us)
Async XLA Ops:
  1.3 0.7 copy-start.8
  2.0 1.0 copy-start
  3.0 0.9 copy-start.3
  5.5 10.2 %copy-start.6 = (s32[512,16]{0,1:T(8,128)S(1)}, s32[512,16]{0,1:T(8,128)}, u32[]{:S(2)}) copy-start(s32[512,16]{0,1:T(8,128)} %param.16) | copy-start | bytes 98308
  5.5 15.0 %all-to-all-start = ((f32[8,1,1280]{2,1,0:T(1,128)}), f32[8,1,1280]{2,1,0:T(1,128)S(1)}, u32[]{:S(2)}, u32[]{:S(2)}) async-start(f32[8,1,1280]{2,1,0:T(1,128)} %get-tuple-element.29), calls=%async_computation | async-start | bytes 81920 | tf_op jit(solution)/shard_map/all_to_all | solution.py:214
  15.7 0.7 copy-start.7
  19.5 0.8 copy-start.16
  20.3 23.5 %copy-start.4 = (bf16[512,256]{1,0:T(8,128)(2,1)S(1)}, bf16[512,256]{1,0:T(8,128)(2,1)}, u32[]{:S(2)}) copy-start(bf16[512,256]{1,0:T(8,128)(2,1)} %feats_ref.8) | copy-start | bytes 786436
  21.2 22.6 %copy-start.5 = (bf16[256,256]{1,0:T(8,128)(2,1)S(1)}, bf16[256,256]{1,0:T(8,128)(2,1)}, u32[]{:S(2)}) copy-start(bf16[256,256]{1,0:T(8,128)(2,1)} %wg_ref.1) | copy-start | bytes 393220
  21.2 16.1 %all-to-all-start.1 = ((f32[8,1,1280]{2,1,0:T(1,128)}), f32[8,1,1280]{2,1,0:T(1,128)S(1)}, u32[]{:S(2)}, u32[]{:S(2)}) async-start(f32[8,1,1280]{2,1,0:T(1,128)} %reshape.127), calls=%async_computation.1 | async-start | bytes 81920 | tf_op jit(solution)/shard_map/all_to_all | solution.py:220
  24.7 12.7 %collective-permute-start = (bf16[64,256]{1,0:T(8,128)(2,1)S(1)}, bf16[64,256]{1,0:T(8,128)(2,1)S(1)}, u32[]{:S(2)}, u32[]{:S(2)}) collective-permute-start(bf16[64,256]{1,0:T(8,128)(2,1)S(1)} %get-tuple-element.33), channel_id=1, source_target_pairs={{0,1},{1,2},{2,3},{3,4},{4,5},{5,6},{6,7},{7,8},{8,9},{9,10},{10,1... | collective-permute-start | bytes 98312 | tf_op jit(solution)/shard_map/ppermute | solution.py:261
  27.9 10.5 %collective-permute-start.1 = (bf16[64,256]{1,0:T(8,128)(2,1)S(1)}, bf16[64,256]{1,0:T(8,128)(2,1)S(1)}, u32[]{:S(2)}, u32[]{:S(2)}) collective-permute-start(bf16[64,256]{1,0:T(8,128)(2,1)S(1)} %get-tuple-element.34), channel_id=1, source_target_pairs={{1,0},{2,1},{3,2},{4,3},{5,4},{6,5},{7,6},{8,7},{9,8},{10,9},{11,1... | collective-permute-start | bytes 98312 | tf_op jit(solution)/shard_map/ppermute | solution.py:262
  39.0 11.8 %all-to-all-start.2 = ((f32[8,1,1280]{2,1,0:T(1,128)}), f32[8,1,1280]{2,1,0:T(1,128)S(1)}, u32[]{:S(2)}, u32[]{:S(2)}) async-start(f32[8,1,1280]{2,1,0:T(1,128)} %reshape.128), calls=%async_computation.2 | async-start | bytes 81920 | tf_op jit(solution)/shard_map/all_to_all | solution.py:220
  43.8 1.1 copy-start.17
  44.9 13.1 %copy-start.1 = (bf16[3,256,256]{2,1,0:T(8,128)(2,1)S(1)}, bf16[3,256,256]{2,1,0:T(8,128)(2,1)}, u32[]{:S(2)}) copy-start(bf16[3,256,256]{2,1,0:T(8,128)(2,1)} %w_ref.3) | copy-start | bytes 1179652
  45.8 12.5 %copy-start.14 = (f32[512,256]{1,0:T(8,128)}, f32[512,256]{1,0:T(8,128)S(1)}, u32[]{:S(2)}) copy-start(f32[512,256]{1,0:T(8,128)S(1)} %get-tuple-element.44.graph_ref) | copy-start | bytes 1572868
  51.5 11.3 %all-to-all-start.3 = ((f32[8,1,1280]{2,1,0:T(1,128)}), f32[8,1,1280]{2,1,0:T(1,128)S(1)}, u32[]{:S(2)}, u32[]{:S(2)}) async-start(f32[8,1,1280]{2,1,0:T(1,128)} %reshape.129), calls=%async_computation.3 | async-start | bytes 81920 | tf_op jit(solution)/shard_map/all_to_all | solution.py:220
  58.0 4.8 %copy-start.2 = (bf16[512,256]{1,0:T(8,128)(2,1)S(1)}, bf16[512,256]{1,0:T(8,128)(2,1)}, u32[]{:S(2)}) copy-start(bf16[512,256]{1,0:T(8,128)(2,1)} %grad_ref.1) | copy-start | bytes 786436
  62.8 0.7 copy-start.9
  63.5 1.0 copy-start.15
  66.2 0.8 copy-start.10
  67.0 25.6 %copy-start.12 = (bf16[512,256]{1,0:T(8,128)(2,1)}, bf16[512,256]{1,0:T(8,128)(2,1)S(1)}, u32[]{:S(2)}) copy-start(bf16[512,256]{1,0:T(8,128)(2,1)S(1)} %get-tuple-element.48.dgraph_ref) | copy-start | bytes 786436
  89.3 10.2 %all-to-all-start.6 = ((f32[8,1,1280]{2,1,0:T(1,128)}), f32[8,1,1280]{2,1,0:T(1,128)S(1)}, u32[]{:S(2)}, u32[]{:S(2)}) async-start(f32[8,1,1280]{2,1,0:T(1,128)} %reshape.132), calls=%async_computation.6 | async-start | bytes 81920 | tf_op jit(solution)/shard_map/all_to_all | solution.py:220
  92.7 1.0 copy-start.11
  93.7 0.9 copy-start.13

commit v4 on v3

--- a/solution.py
+++ b/solution.py
@@ -74,16 +74,23 @@
     return dot(high, heads) + dot(low, heads)
 
 
-def key_kernel(count_ref, feats_ref, w_ref, send_ref, packed_ref, before_ref, after_ref, key_ref, value_ref):
+def key_kernel(
+    count_ref, feats_hbm, w_hbm, send_hbm, packed_ref, before_ref, after_ref,
+    feats_ref, w_ref, send_ref, sems,
+):
+    sources = [(feats_hbm, feats_ref), (w_hbm.at[pl.ds(1, 2)], w_ref), (send_hbm, send_ref)]
+    copies = [pltpu.make_async_copy(*pair, sems.at[i]) for i, pair in enumerate(sources)]
+    for copy in copies:
+        copy.start()
+    for copy in copies:
+        copy.wait()
     feats = feats_ref[...]
     slot = lax.broadcasted_iota(jnp.int32, (feats.shape[0], send_ref.shape[2]), 0)
     for side, out in ((0, before_ref), (1, after_ref)):
         chosen = (slot == send_ref[0, side : side + 1, :]).astype(jnp.bfloat16)
         out[...] = dot(chosen, feats, ROWS_FIRST).astype(jnp.bfloat16)
-    key_map = feature_map(dot(feats, w_ref[1]))
-    value_rows = dot(feats, w_ref[2])
-    key_ref[...] = key_map
-    value_ref[...] = value_rows
+    key_map = feature_map(dot(feats, w_ref[0]))
+    value_rows = dot(feats, w_ref[1])
     key_map = key_map * alive_of(count_ref, feats.shape[0])
     kv = dot3(halves(key_map), halves(value_rows), ROWS_FIRST)
     live = jnp.broadcast_to(count_ref[...].astype(jnp.float32), (1, D))
@@ -94,27 +101,28 @@
     wide, total = hits_ref.shape
     slots = nbr_ref.shape[0]
     sub = 32
+    one, none = jnp.ones((sub, 128), jnp.bfloat16), jnp.zeros((sub, 128), jnp.bfloat16)
     for b in range(total // 128):
         at = slice(b * 128, (b + 1) * 128)
         slot = lax.broadcasted_iota(jnp.int32, (slots, 128), 0)
         named = jnp.where(slot < count_ref[:, at], nbr_ref[:, at], -1)
-        rows = [jnp.broadcast_to(named[s : s + 1], (sub, 128)) for s in range(slots)]
-        own = lax.broadcasted_iota(jnp.int32, (sub, 128), 1) + b * 128
+        rows = [jnp.broadcast_to(named[s : s + 1], (sub, 128)).astype(jnp.int16) for s in range(slots)]
+        own = (lax.broadcasted_iota(jnp.int32, (sub, 128), 1) + b * 128).astype(jnp.int16)
         place0 = lax.broadcasted_iota(jnp.int32, (sub, 128), 0)
 
         def body(i, carry):
             first = pl.multiple_of(i * sub, sub)
-            place = place0 + first
-            hits = (place == own).astype(jnp.float32)
+            place = (place0 + first).astype(jnp.int16)
+            hits = jnp.where(place == own, one, none)
             for s in range(slots):
-                hits = hits + (place == rows[s]).astype(jnp.float32)
-            hits_ref[pl.ds(first, sub), at] = hits.astype(jnp.bfloat16)
+                hits = hits + jnp.where(place == rows[s], one, none)
+            hits_ref[pl.ds(first, sub), at] = hits
             return carry
 
         lax.fori_loop(0, wide // sub, body, 0)
 
 
-def graph_kernel(hits_ref, feats_ref, left_ref, right_ref, wg_ref, agg_ref, graph_ref):
+def graph_kernel(hits_ref, feats_ref, left_ref, right_ref, wg_ref, w_ref, agg_ref, graph_ref, query_ref, key_ref, value_ref):
     total = feats_ref.shape[0]
     rim = left_ref.shape[0]
     summed = dot(hits_ref[:total, :], feats_ref[...], ROWS_FIRST)
@@ -124,15 +132,15 @@
     agg = (summed / jnp.concatenate([named, named], axis=1)).astype(jnp.bfloat16)
     agg_ref[...] = agg
     graph_ref[...] = 0.5 * dot(agg, wg_ref[...])
-
-
-def project_kernel(feats_ref, w_ref, query_ref):
-    query_ref[...] = feature_map(dot(feats_ref[...], w_ref[0]))
+    feats = feats_ref[...]
+    query_ref[...] = feature_map(dot(feats, w_ref[0]))
+    key_ref[...] = feature_map(dot(feats, w_ref[1]))
+    value_ref[...] = dot(feats, w_ref[2])
 
 
 def mix_kernel(
-    count_ref, packed_ref, query_ref, value_ref, graph_ref, grad_ref, gain_ref,
-    out_ref, dgraph_ref, dnum_ref, dden_ref, packed_out_ref, scale_ref,
+    count_ref, packed_ref, feats_ref, agg_ref, query_ref, value_ref, graph_ref, grad_ref, gain_ref,
+    out_ref, dnum_ref, packed_out_ref, terms_ref, scale_ref,
 ):
     kv, vectors = load_packed(packed_ref)
     kv = halves(kv)
@@ -161,22 +169,14 @@
         - normed * (jnp.sum(dnormed * normed, -1, keepdims=True) / D)
     )
     dattn = 0.5 * dmixed
-    dgraph_ref[...] = dattn.astype(jnp.bfloat16)
     dnum = dattn * inverse
     dnum_ref[...] = dnum
     dden = -head_sums(dattn * attn, heads) * inverse
-    dden_ref[...] = dden
     dkv = dot3(query_halves, halves(dnum), ROWS_FIRST)
     dks = jnp.sum(query_map * dden, axis=0, keepdims=True)
     store_packed(packed_out_ref, factor * dkv, [factor * dks])
-
-
-def query_kernel(packed_ref, feats_ref, agg_ref, query_ref, dgraph_ref, dnum_ref, dden_ref, terms_ref):
-    kv, vectors = load_packed(packed_ref)
-    factor = 1.0 / (DH * vectors[1:2])
-    slope = jnp.minimum(query_ref[...], 1.0)
-    dquery = factor * (dot3(halves(dnum_ref[...]), halves(kv), COLS_LAST) + dden_ref[...] * vectors[0:1]) * slope
-    terms_ref[0] = dot(agg_ref[...], dgraph_ref[...], ROWS_FIRST)
+    terms_ref[0] = dot(agg_ref[...], dattn.astype(jnp.bfloat16), ROWS_FIRST)
+    dquery = factor * (dot3(halves(dnum), kv, COLS_LAST) + dden * ks) * jnp.minimum(query_map, 1.0)
     terms_ref[1] = dot(feats_ref[...], dquery.astype(jnp.bfloat16), ROWS_FIRST)
 
 
@@ -195,17 +195,28 @@
     terms_ref[3] = dot(feats, dvalue.astype(jnp.bfloat16), ROWS_FIRST)
 
 
-def call(kernel, name, shapes, *args):
-    def here(one):
-        return pl.BlockSpec(memory_space=pltpu.VMEM)
-
+def split_kernel(total_ref, qkv_ref, graph_ref, sems):
+    copies = [
+        pltpu.make_async_copy(total_ref.at[pl.ds(1, 3)], qkv_ref, sems.at[0]),
+        pltpu.make_async_copy(total_ref.at[0], graph_ref, sems.at[1]),
+    ]
+    for copy in copies:
+        copy.start()
+    for copy in copies:
+        copy.wait()
+
+
+def call(kernel, name, shapes, *args, away=(), outs_away=False, scratch=(), limit=VMEM_LIMIT):
+    near = pl.BlockSpec(memory_space=pltpu.VMEM)
+    far = pl.BlockSpec(memory_space=pltpu.MemorySpace.HBM)
     return pl.pallas_call(
         kernel,
-        in_specs=[here(arg) for arg in args],
-        out_specs=jax.tree.map(here, shapes),
+        in_specs=[far if i in away else near for i in range(len(args))],
+        out_specs=jax.tree.map(lambda one: far if outs_away else near, shapes),
         out_shape=shapes,
+        scratch_shapes=scratch,
         cost_estimate=pl.CostEstimate(flops=10**9, bytes_accessed=10**7, transcendentals=0),
-        compiler_params=pltpu.CompilerParams(vmem_limit_bytes=VMEM_LIMIT),
+        compiler_params=pltpu.CompilerParams(vmem_limit_bytes=limit),
         name=name,
     )(*args)
 
@@ -246,48 +257,52 @@
     packed_shape, rim_shape = shape((TILE, 1, PACK), f32), shape((rim, D), bf16)
     together = lax.optimization_barrier
 
-    packed, to_before, to_after, key_map, value_rows = call(
-        key_kernel, "keys", [packed_shape, rim_shape, rim_shape, rows_f32, rows_f32],
-        count, node_feats, w_qkv, send_rows,
+    packed, to_before, to_after = call(
+        key_kernel, "keys", [packed_shape, rim_shape, rim_shape],
+        count, node_feats, w_qkv, send_rows, away=(1, 2, 3), limit=None,
+        scratch=[
+            pltpu.VMEM((rows, D), bf16), pltpu.VMEM((2, D, D), bf16), pltpu.VMEM(send_rows.shape, jnp.int32),
+            pltpu.SemaphoreType.DMA((3,)),
+        ],
     )
 
     up = [(i, i + 1) for i in range(parts - 1)]
     down = [(j, i) for i, j in up]
+    left = lax.ppermute(to_after, FINE, up)
+    right = lax.ppermute(to_before, FINE, down)
+    share = scatter_sum(packed, ("x", "c"), near)
+    share, left, right = together((share, left, right))
     hits = call(
         hit_kernel, "hits", shape((rows + 2 * rim, rows), bf16), neighbours.T, neighbour_counts.reshape(1, rows)
     )
-    share = scatter_sum(packed, ("x", "c"), near)
-    share, hits, to_before, to_after = together((share, hits, to_before, to_after))
-    left = lax.ppermute(to_after, FINE, up)
-    right = lax.ppermute(to_before, FINE, down)
+    agg, graph, query_map, key_map, value_rows = call(
+        graph_kernel, "graph", [rows_bf16, rows_f32, rows_f32, rows_f32, rows_f32],
+        hits, node_feats, left, right, w_graph, w_qkv,
+    )
     share = gather_sum(share, "y", sizes["y"])
-    share, left, right = together((share, left, right))
-    agg, graph = call(graph_kernel, "graph", [rows_bf16, rows_f32], hits, node_feats, left, right, w_graph)
+    share, agg, graph, query_map, key_map, value_rows = together((share, agg, graph, query_map, key_map, value_rows))
     share = gather_sum(share, "z", sizes["z"])
-    share, agg, graph, feats_here = together((share, agg, graph, node_feats))
-    query_map = call(project_kernel, "project", rows_f32, feats_here, w_qkv)
     packed = gather(share, ("x", "c"), near)
 
-    node_out, dgraph, dnum, dden, dpacked, scale = call(
-        mix_kernel, "mix", [rows_bf16, rows_bf16, rows_f32, rows_f32, packed_shape, shape((1, D), f32)],
-        count, packed, query_map, value_rows, graph, out_grad, ln_gain.reshape(1, D),
+    node_out, dnum, dpacked, terms, scale = call(
+        mix_kernel, "mix", [rows_bf16, rows_f32, packed_shape, shape((2, D, D), f32), shape((1, D), f32)],
+        count, packed, node_feats, agg, query_map, value_rows, graph, out_grad, ln_gain.reshape(1, D),
     )
 
     share = scatter_sum(dpacked, ("x", "c"), near)
     share = gather_sum(share, "y", sizes["y"])
-    terms = call(
-        query_kernel, "queries", shape((2, D, D), f32), packed, node_feats, agg, query_map, dgraph, dnum, dden
-    )
     share = gather_sum(share, "z", sizes["z"])
-    share, terms = together((share, terms))
     dpacked = gather(share, ("x", "c"), near)
 
     terms = call(
         grad_kernel, "grads", shape((4, D, D), f32), count, dpacked, node_feats, key_map, value_rows, dnum, terms
     )
-
     total = sum_terms(terms.reshape(4 * D, D), sizes, scale).reshape(4, D, D)
-    return node_out, total[1:], total[0]
+    qkv_grad, graph_grad = call(
+        split_kernel, "split", [shape((3, D, D), f32), shape((D, D), f32)], total,
+        outs_away=True, scratch=[pltpu.SemaphoreType.DMA((2,))],
+    )
+    return node_out, qkv_grad, graph_grad
 
 
 def solution(mesh):

time: 181 us -> 175 us (0.967)
  blocking collectives: 98.8 us -> 127 us
  starting transfers between devices: 41 us -> 25.1 us
  waiting for transfers between devices: 14.7 us -> 4.87 us
  local copies, waits for them, and re-layouts: 14.1 us -> 4.39 us
    all_to_all x6 -> x9, blocking collectives: 64.1 us -> 92.6 us  [gather(): return lax.all_to_all(copies, axes, 0, 0, tiled=True)]
    all_to_all x4 -> x1, starting transfers between devices: 18.1 us -> 6.82 us  [gather(): return lax.all_to_all(copies, axes, 0, 0, tiled=True)]
    all_to_all x4 -> x1, waiting for transfers between devices: 13.6 us -> 4.86 us  [gather(): return lax.all_to_all(copies, axes, 0, 0, tiled=True)]
    unnamed x36 -> x24, local copies, waits for them, and re-layouts: 9.73 us -> 3.5 us
    ppermute x1, starting transfers between devices: 9.5 us -> 6.26 us  [local(): right = lax.ppermute(to_before, FINE, down)]
    reshape x6, local copies, waits for them, and re-layouts: 2.6 us -> 0.76 us  [gather(): jnp.broadcast_to(value[None], (count, *value.shape))]
    pallas_call x7 -> x6, Pallas kernels: 9.09 us -> 10.5 us  [call(): pl.pallas_call(kernel, in_specs=[far if i in away else near for i in rang...]
  transfers between devices with their start and end apart: 7 -> 4, of which waited for: 5 -> 1; matrix products, arithmetic and copies ran while one was open for 0% -> 0% of each run, Pallas kernels for 3% -> 2%
where the time goes in v4:
time: 175 us; the launch traced here: 174 us
  blocking collectives  127 us (73%)
  starting transfers between devices  25.1 us (14%)
  Pallas kernels  10.5 us (6%)
  waiting for transfers between devices  4.87 us (3%)
  local copies, waits for them, and re-layouts  4.39 us (3%)
    all_to_all x9, blocking collectives, gather(): return lax.all_to_all(copies, axes, 0, 0, tiled=True)  92.6 us
    all_to_all x4, blocking collectives, scatter_sum(): parts = lax.all_to_all(value, axes, 0, 0, tiled=True)  34.7 us
    pallas_call x6, Pallas kernels, call(): pl.pallas_call(kernel, in_specs=[far if i in away else near for i in rang...  10.5 us
    all_to_all x1, starting transfers between devices, scatter_sum(): parts = lax.all_to_all(value, axes, 0, 0, tiled=True)  10.1 us
    all_to_all x1, starting transfers between devices, gather(): return lax.all_to_all(copies, axes, 0, 0, tiled=True)  6.82 us
    ppermute x1, starting transfers between devices, local(): right = lax.ppermute(to_before, FINE, down)  6.26 us
    all_to_all x1, waiting for transfers between devices, gather(): return lax.all_to_all(copies, axes, 0, 0, tiled=True)  4.86 us
    unnamed x24, local copies, waits for them, and re-layouts  3.5 us
  transfers between devices with their start and end apart: 4, of which 1 were waited for; matrix products, arithmetic and copies ran while one was open for 0% of the time, Pallas kernels for 2%

profile of v4, /device:TPU:1, one launch (start us, length us, event | category | flops | bytes accessed | tf_op | source)
XLA Modules:
  0.0 174.2 jit_solution(11793649233236528267)
XLA Ops:
  1.3 2.7 %keys.1 = (f32[8,1,1280]{2,1,0:T(1,128)}, bf16[64,256]{1,0:T(8,128)(2,1)}, bf16[64,256]{1,0:T(8,128)(2,1)}) custom-call(s32[1,1]{1,0:T(1,128)} %bitcast.11.count_ref, bf16[512,256]{1,0:T(8,128)(2,1)} %feats_ref.5, bf16[3,256,256]{2,1,0:T(8,128)(2,1)} %w_ref.1, s32[1,2,64]{2,1,0:T(2,128)} %send_hbm.1), custom_call_target="tpu_custom_call" | custom-call | flops 1000000000 | bytes 10000000 | tf_op jit(solution)/shard_map/keys/pallas_call | solution.py:212
  4.0 0.0 copy-start.11
  4.0 0.0 copy-start.4
  4.0 10.1 %all-to-all-start = ((f32[8,1,1280]{2,1,0:T(1,128)}), f32[8,1,1280]{2,1,0:T(1,128)S(1)}, u32[]{:S(2)}, u32[]{:S(2)}) async-start(f32[8,1,1280]{2,1,0:T(1,128)} %get-tuple-element.27), calls=%async_computation | async-start | bytes 81920 | tf_op jit(solution)/shard_map/all_to_all | solution.py:225
  14.1 1.9 %collective-permute-start = (bf16[64,256]{1,0:T(8,128)(2,1)}, bf16[64,256]{1,0:T(8,128)(2,1)S(1)}, u32[]{:S(2)}, u32[]{:S(2)}) collective-permute-start(bf16[64,256]{1,0:T(8,128)(2,1)} %get-tuple-element.28), channel_id=1, source_target_pairs={{0,1},{1,2},{2,3},{3,4},{4,5},{5,6},{6,7},{7,8},{8,9},{9,10},{10,1... | collective-permute-start | bytes 98312 | tf_op jit(solution)/shard_map/ppermute | solution.py:271
  16.0 0.0 copy-done.11
  16.0 0.0 copy-start.5
  16.0 6.3 %collective-permute-start.1 = (bf16[64,256]{1,0:T(8,128)(2,1)S(1)}, bf16[64,256]{1,0:T(8,128)(2,1)S(1)}, u32[]{:S(2)}, u32[]{:S(2)}) collective-permute-start(bf16[64,256]{1,0:T(8,128)(2,1)S(1)} %copy-done.11), channel_id=1, source_target_pairs={{1,0},{2,1},{3,2},{4,3},{5,4},{6,5},{7,6},{8,7},{9,8},{10,9},{11,1... | collective-permute-start | bytes 98312 | tf_op jit(solution)/shard_map/ppermute | solution.py:272
  22.3 0.0 copy-done.4
  22.3 0.0 copy-done.5
  22.3 0.0 copy-start
  22.3 0.0 copy-start.2
  22.3 2.0 %hits.1.hits_ref = bf16[640,512]{1,0:T(8,128)(2,1)S(1)} custom-call(s32[16,512]{1,0:T(8,128)S(1)} %bitcast.17, s32[1,512]{1,0:T(1,128)S(1)} %bitcast.18), custom_call_target="tpu_custom_call" | custom-call | flops 1000000000 | bytes 10000000 | tf_op jit(solution)/shard_map/hits/pallas_call | solution.py:212
  24.3 0.0 copy-start.3
  24.3 0.0 all-to-all-done
  24.4 0.0 collective-permute-done.left_ref
  24.4 0.0 collective-permute-done.1.right_ref
  24.5 0.6 reshape.128
  25.1 6.8 %all-to-all-start.1 = ((f32[8,1,1280]{2,1,0:T(1,128)}), f32[8,1,1280]{2,1,0:T(1,128)S(1)}, u32[]{:S(2)}, u32[]{:S(2)}) async-start(f32[8,1,1280]{2,1,0:T(1,128)} %reshape.128), calls=%async_computation.1 | async-start | bytes 81920 | tf_op jit(solution)/shard_map/all_to_all | solution.py:231
  31.9 0.0 copy-done
  31.9 0.0 copy-done.2
  31.9 0.0 copy-done.3
  31.9 1.3 graph.1
  33.2 0.0 copy-start.7
  33.2 0.8 copy-done.7
  34.0 0.0 copy-start.9
  34.0 0.0 copy-start.1
  34.0 4.9 %all-to-all-done.1 = f32[8,1,1280]{2,1,0:T(1,128)S(1)} async-done(((f32[8,1,1280]{2,1,0:T(1,128)}), f32[8,1,1280]{2,1,0:T(1,128)S(1)}, u32[]{:S(2)}, u32[]{:S(2)}) %all-to-all-start.1) | async-done | bytes 40992 | tf_op jit(solution)/shard_map/all_to_all | solution.py:231
  39.0 11.8 %all_to_all.91 = f32[8,1,1280]{2,1,0:T(1,128)S(1)} all-to-all(f32[8,1,1280]{2,1,0:T(1,128)S(1)} %reshape.130), channel_id=1, replica_groups=mesh['x'=4,'y'=8,'c'=2,'z'=8] {'z'}, dimensions={0} | all-to-all | bytes 81920 | tf_op jit(solution)/shard_map/all_to_all | solution.py:231
  50.9 12.0 %all_to_all.92.packed_ref = f32[8,1,1280]{2,1,0:T(1,128)S(1)} all-to-all(f32[8,1,1280]{2,1,0:T(1,128)S(1)} %reshape.131), channel_id=1, replica_groups=mesh['x'=4,'y'=8,'c'=2,'z'=8] {'x','c'}, dimensions={0} | all-to-all | bytes 81920 | tf_op jit(solution)/shard_map/all_to_all | solution.py:231
  62.9 0.0 copy-done.9
  62.9 0.0 copy-start.6
  62.9 0.0 copy-done.1
  62.9 0.7 copy-done.6
  63.6 0.0 copy-start.8
  63.6 1.0 copy-done.8
  64.6 0.0 copy-start.10
  64.6 0.9 copy-done.10
  65.6 2.7 %mix.1 = (bf16[512,256]{1,0:T(8,128)(2,1)}, f32[512,256]{1,0:T(8,128)S(1)}, f32[8,1,1280]{2,1,0:T(1,128)S(1)}, f32[2,256,256]{2,1,0:T(8,128)S(1)}, f32[1,256]{1,0:T(1,128)S(1)}) custom-call(s32[1,1]{1,0:T(1,128)} %bitcast.12.count_ref, f32[8,1,1280]{2,1,0:T(1,128)S(1)} %all_to_all.92.packed_ref, bf16[512,256]{1,0:T(8,128)(2,1)S(1)} %copy-done.2, ...), custom_call_target="tpu_custom_call" | custom-call | flops 1000000000 | bytes 10000000 | tf_op jit(solution)/shard_map/mix/pallas_call | solution.py:212
  68.3 7.8 %all_to_all.93 = f32[8,1,1280]{2,1,0:T(1,128)S(1)} all-to-all(f32[8,1,1280]{2,1,0:T(1,128)S(1)} %get-tuple-element.44), channel_id=1, replica_groups=mesh['x'=4,'y'=8,'c'=2,'z'=8] {'x','c'}, dimensions={0} | all-to-all | bytes 81920 | tf_op jit(solution)/shard_map/all_to_all | solution.py:225
  76.2 9.4 %all_to_all.94 = f32[8,1,1280]{2,1,0:T(1,128)S(1)} all-to-all(f32[8,1,1280]{2,1,0:T(1,128)S(1)} %reshape.133), channel_id=1, replica_groups=mesh['x'=4,'y'=8,'c'=2,'z'=8] {'y'}, dimensions={0} | all-to-all | bytes 81920 | tf_op jit(solution)/shard_map/all_to_all | solution.py:231
  85.7 9.3 %all_to_all.95 = f32[8,1,1280]{2,1,0:T(1,128)S(1)} all-to-all(f32[8,1,1280]{2,1,0:T(1,128)S(1)} %reshape.134), channel_id=1, replica_groups=mesh['x'=4,'y'=8,'c'=2,'z'=8] {'z'}, dimensions={0} | all-to-all | bytes 81920 | tf_op jit(solution)/shard_map/all_to_all | solution.py:231
  95.1 10.1 %all_to_all.96.packed_ref = f32[8,1,1280]{2,1,0:T(1,128)S(1)} all-to-all(f32[8,1,1280]{2,1,0:T(1,128)S(1)} %reshape.135), channel_id=1, replica_groups=mesh['x'=4,'y'=8,'c'=2,'z'=8] {'x','c'}, dimensions={0} | all-to-all | bytes 81920 | tf_op jit(solution)/shard_map/all_to_all | solution.py:231
  105.2 0.9 grads.1
  106.1 4.9 %all_to_all.97 = f32[2,512,256]{2,1,0:T(8,128)S(1)} all-to-all(f32[2,512,256]{2,1,0:T(8,128)S(1)} %bitcast.14), channel_id=1, replica_groups=mesh['x'=4,'y'=8,'c'=2,'z'=8] {'c'}, dimensions={0} | all-to-all | bytes 2097152 | tf_op jit(solution)/shard_map/all_to_all | solution.py:225
  111.0 0.1 reduce_sum.102
  111.1 11.6 %all_to_all.98 = f32[4,128,256]{2,1,0:T(8,128)S(1)} all-to-all(f32[4,128,256]{2,1,0:T(8,128)S(1)} %bitcast.21), channel_id=1, replica_groups=mesh['x'=4,'y'=8,'c'=2,'z'=8] {'x'}, dimensions={0} | all-to-all | bytes 1048576 | tf_op jit(solution)/shard_map/all_to_all | solution.py:225
  122.8 10.3 %all_to_all.99 = f32[8,16,256]{2,1,0:T(8,128)S(1)} all-to-all(f32[8,16,256]{2,1,0:T(8,128)S(1)} %bitcast.23), channel_id=1, replica_groups=mesh['x'=4,'y'=8,'c'=2,'z'=8] {'y'}, dimensions={0} | all-to-all | bytes 262144 | tf_op jit(solution)/shard_map/all_to_all | solution.py:225
  133.2 10.4 %all_to_all.100 = f32[8,16,256]{2,1,0:T(8,128)S(1)} all-to-all(f32[8,16,256]{2,1,0:T(8,128)S(1)} %broadcast_in_dim.18), channel_id=1, replica_groups=mesh['x'=4,'y'=8,'c'=2,'z'=8] {'z'}, dimensions={0} | all-to-all | bytes 262144 | tf_op jit(solution)/shard_map/all_to_all | solution.py:231
  143.6 10.4 %all_to_all.101 = f32[8,16,256]{2,1,0:T(8,128)S(1)} all-to-all(f32[8,16,256]{2,1,0:T(8,128)S(1)} %broadcast_in_dim.19), channel_id=1, replica_groups=mesh['x'=4,'y'=8,'c'=2,'z'=8] {'y'}, dimensions={0} | all-to-all | bytes 262144 | tf_op jit(solution)/shard_map/all_to_all | solution.py:231
  154.1 9.3 %all_to_all.102 = f32[4,128,256]{2,1,0:T(8,128)S(1)} all-to-all(f32[4,128,256]{2,1,0:T(8,128)S(1)} %broadcast_in_dim.21), channel_id=1, replica_groups=mesh['x'=4,'y'=8,'c'=2,'z'=8] {'x'}, dimensions={0} | all-to-all | bytes 1048576 | tf_op jit(solution)/shard_map/all_to_all | solution.py:231
  163.4 0.1 broadcast_in_dim.23
  163.5 9.8 %all_to_all.103 = f32[2,512,256]{2,1,0:T(8,128)S(1)} all-to-all(f32[2,512,256]{2,1,0:T(8,128)S(1)} %broadcast_in_dim.23), channel_id=1, replica_groups=mesh['x'=4,'y'=8,'c'=2,'z'=8] {'c'}, dimensions={0} | all-to-all | bytes 2097152 | tf_op jit(solution)/shard_map/all_to_all | solution.py:231
  173.3 1.0 split.1
  (22 shorter events, 0.5 us)
Async XLA Ops:
  4.0 12.0 %copy-start.11 = (bf16[64,256]{1,0:T(8,128)(2,1)S(1)}, bf16[64,256]{1,0:T(8,128)(2,1)}, u32[]{:S(2)}) copy-start(bf16[64,256]{1,0:T(8,128)(2,1)} %get-tuple-element.29) | copy-start | bytes 98308
  4.0 18.3 %copy-start.4 = (s32[512,16]{0,1:T(8,128)S(1)}, s32[512,16]{0,1:T(8,128)}, u32[]{:S(2)}) copy-start(s32[512,16]{0,1:T(8,128)} %param.16) | copy-start | bytes 98308
  4.0 20.4 %all-to-all-start = ((f32[8,1,1280]{2,1,0:T(1,128)}), f32[8,1,1280]{2,1,0:T(1,128)S(1)}, u32[]{:S(2)}, u32[]{:S(2)}) async-start(f32[8,1,1280]{2,1,0:T(1,128)} %get-tuple-element.27), calls=%async_computation | async-start | bytes 81920 | tf_op jit(solution)/shard_map/all_to_all | solution.py:225
  14.1 10.3 %collective-permute-start = (bf16[64,256]{1,0:T(8,128)(2,1)}, bf16[64,256]{1,0:T(8,128)(2,1)S(1)}, u32[]{:S(2)}, u32[]{:S(2)}) collective-permute-start(bf16[64,256]{1,0:T(8,128)(2,1)} %get-tuple-element.28), channel_id=1, source_target_pairs={{0,1},{1,2},{2,3},{3,4},{4,5},{5,6},{6,7},{7,8},{8,9},{9,10},{10,1... | collective-permute-start | bytes 98312 | tf_op jit(solution)/shard_map/ppermute | solution.py:271
  16.0 6.3 %copy-start.5 = (s32[512]{0:T(512)S(1)}, s32[512]{0:T(512)}, u32[]{:S(2)}) copy-start(s32[512]{0:T(512)} %param.17) | copy-start | bytes 6148
  16.0 8.4 %collective-permute-start.1 = (bf16[64,256]{1,0:T(8,128)(2,1)S(1)}, bf16[64,256]{1,0:T(8,128)(2,1)S(1)}, u32[]{:S(2)}, u32[]{:S(2)}) collective-permute-start(bf16[64,256]{1,0:T(8,128)(2,1)S(1)} %copy-done.11), channel_id=1, source_target_pairs={{1,0},{2,1},{3,2},{4,3},{5,4},{6,5},{7,6},{8,7},{9,8},{10,9},{11,1... | collective-permute-start | bytes 98312 | tf_op jit(solution)/shard_map/ppermute | solution.py:272
  22.3 9.6 %copy-start = (bf16[3,256,256]{2,1,0:T(8,128)(2,1)S(1)}, bf16[3,256,256]{2,1,0:T(8,128)(2,1)}, u32[]{:S(2)}) copy-start(bf16[3,256,256]{2,1,0:T(8,128)(2,1)} %w_ref.1) | copy-start | bytes 1179652
  22.3 9.6 %copy-start.2 = (bf16[512,256]{1,0:T(8,128)(2,1)S(1)}, bf16[512,256]{1,0:T(8,128)(2,1)}, u32[]{:S(2)}) copy-start(bf16[512,256]{1,0:T(8,128)(2,1)} %feats_ref.5) | copy-start | bytes 786436
  24.3 7.6 %copy-start.3 = (bf16[256,256]{1,0:T(8,128)(2,1)S(1)}, bf16[256,256]{1,0:T(8,128)(2,1)}, u32[]{:S(2)}) copy-start(bf16[256,256]{1,0:T(8,128)(2,1)} %wg_ref.1) | copy-start | bytes 393220
  25.1 13.8 %all-to-all-start.1 = ((f32[8,1,1280]{2,1,0:T(1,128)}), f32[8,1,1280]{2,1,0:T(1,128)S(1)}, u32[]{:S(2)}, u32[]{:S(2)}) async-start(f32[8,1,1280]{2,1,0:T(1,128)} %reshape.128), calls=%async_computation.1 | async-start | bytes 81920 | tf_op jit(solution)/shard_map/all_to_all | solution.py:231
  33.2 0.8 copy-start.7
  34.0 28.9 %copy-start.9 = (bf16[512,256]{1,0:T(8,128)(2,1)}, bf16[512,256]{1,0:T(8,128)(2,1)S(1)}, u32[]{:S(2)}) copy-start(bf16[512,256]{1,0:T(8,128)(2,1)S(1)} %get-tuple-element.39.agg_ref) | copy-start | bytes 786436
  34.0 28.9 %copy-start.1 = (bf16[512,256]{1,0:T(8,128)(2,1)S(1)}, bf16[512,256]{1,0:T(8,128)(2,1)}, u32[]{:S(2)}) copy-start(bf16[512,256]{1,0:T(8,128)(2,1)} %grad_ref.1) | copy-start | bytes 786436
  62.9 0.7 copy-start.6
  63.6 1.0 copy-start.8
  64.6 0.9 copy-start.10

commit v5 on v4

--- a/solution.py
+++ b/solution.py
@@ -75,7 +75,7 @@
 
 
 def key_kernel(
-    count_ref, feats_hbm, w_hbm, send_hbm, packed_ref, before_ref, after_ref,
+    count_ref, feats_hbm, w_hbm, send_hbm, packed_ref, first_ref, second_ref,
     feats_ref, w_ref, send_ref, sems,
 ):
     sources = [(feats_hbm, feats_ref), (w_hbm.at[pl.ds(1, 2)], w_ref), (send_hbm, send_ref)]
@@ -86,8 +86,11 @@
         copy.wait()
     feats = feats_ref[...]
     slot = lax.broadcasted_iota(jnp.int32, (feats.shape[0], send_ref.shape[2]), 0)
-    for side, out in ((0, before_ref), (1, after_ref)):
-        chosen = (slot == send_ref[0, side : side + 1, :]).astype(jnp.bfloat16)
+    odd = lax.axis_index("z") % 2
+    for turn, out in ((0, first_ref), (1, second_ref)):
+        to_after = send_ref[0, 1:2, :] * (1 - odd) + send_ref[0, 0:1, :] * odd
+        to_before = send_ref[0, 0:1, :] * (1 - odd) + send_ref[0, 1:2, :] * odd
+        chosen = (slot == (to_before if turn else to_after)).astype(jnp.bfloat16)
         out[...] = dot(chosen, feats, ROWS_FIRST).astype(jnp.bfloat16)
     key_map = feature_map(dot(feats, w_ref[0]))
     value_rows = dot(feats, w_ref[1])
@@ -122,24 +125,24 @@
         lax.fori_loop(0, wide // sub, body, 0)
 
 
-def graph_kernel(hits_ref, feats_ref, left_ref, right_ref, wg_ref, w_ref, agg_ref, graph_ref, query_ref, key_ref, value_ref):
+def graph_kernel(hits_ref, feats_ref, first_ref, second_ref, grad_ref, gain_ref, held_ref, gain_out_ref):
     total = feats_ref.shape[0]
-    rim = left_ref.shape[0]
+    rim = first_ref.shape[0]
+    odd = lax.axis_index("z") % 2 == 1
+    left = jnp.where(odd, first_ref[...], second_ref[...])
+    right = jnp.where(odd, second_ref[...], first_ref[...])
     summed = dot(hits_ref[:total, :], feats_ref[...], ROWS_FIRST)
-    summed += dot(hits_ref[total : total + rim, :], left_ref[...], ROWS_FIRST)
-    summed += dot(hits_ref[total + rim :, :], right_ref[...], ROWS_FIRST)
+    summed += dot(hits_ref[total : total + rim, :], left, ROWS_FIRST)
+    summed += dot(hits_ref[total + rim :, :], right, ROWS_FIRST)
     named = dot(hits_ref[...], jnp.ones((total + 2 * rim, 128), jnp.bfloat16), ROWS_FIRST)
     agg = (summed / jnp.concatenate([named, named], axis=1)).astype(jnp.bfloat16)
-    agg_ref[...] = agg
-    graph_ref[...] = 0.5 * dot(agg, wg_ref[...])
-    feats = feats_ref[...]
-    query_ref[...] = feature_map(dot(feats, w_ref[0]))
-    key_ref[...] = feature_map(dot(feats, w_ref[1]))
-    value_ref[...] = dot(feats, w_ref[2])
+    held_ref[0] = agg
+    held_ref[1] = grad_ref[...]
+    gain_out_ref[...] = gain_ref[...]
 
 
 def mix_kernel(
-    count_ref, packed_ref, feats_ref, agg_ref, query_ref, value_ref, graph_ref, grad_ref, gain_ref,
+    count_ref, packed_ref, feats_ref, w_ref, wg_ref, held_ref, gain_ref,
     out_ref, dnum_ref, packed_out_ref, terms_ref, scale_ref,
 ):
     kv, vectors = load_packed(packed_ref)
@@ -148,21 +151,22 @@
     factor = 1.0 / (DH * live)
     scale_ref[...] = lax.rsqrt(live)
     heads = same_head().astype(jnp.bfloat16)
-    gain_alive = gain_ref[...] * alive_of(count_ref, query_ref.shape[0])
-
-    query_map = query_ref[...]
+    gain_alive = gain_ref[...] * alive_of(count_ref, feats_ref.shape[0])
+
+    feats, agg = feats_ref[...], held_ref[0]
+    query_map = feature_map(dot(feats, w_ref[0]))
     query_halves = halves(query_map)
-    numer = value_ref[...] + factor * dot3(query_halves, kv)
+    numer = dot(feats, w_ref[2]) + factor * dot3(query_halves, kv)
     denom = 1.0 + factor * head_sums(query_map * ks, heads)
     inverse = 1.0 / denom
     attn = numer * inverse
-    mixed = 0.5 * attn + graph_ref[...]
+    mixed = 0.5 * attn + 0.5 * dot(agg, wg_ref[...])
     mean = jnp.sum(mixed, -1, keepdims=True) / D
     spread = jnp.sum(mixed * mixed, -1, keepdims=True) / D - mean * mean
     rstd = lax.rsqrt(spread + 1e-05)
     normed = (mixed - mean) * rstd
     out_ref[...] = (normed * gain_alive).astype(jnp.bfloat16)
-    dnormed = grad_ref[...].astype(jnp.float32) * gain_alive
+    dnormed = held_ref[1].astype(jnp.float32) * gain_alive
     dmixed = rstd * (
         dnormed
         - jnp.sum(dnormed, -1, keepdims=True) / D
@@ -175,22 +179,22 @@
     dkv = dot3(query_halves, halves(dnum), ROWS_FIRST)
     dks = jnp.sum(query_map * dden, axis=0, keepdims=True)
     store_packed(packed_out_ref, factor * dkv, [factor * dks])
-    terms_ref[0] = dot(agg_ref[...], dattn.astype(jnp.bfloat16), ROWS_FIRST)
+    terms_ref[0] = dot(agg, dattn.astype(jnp.bfloat16), ROWS_FIRST)
     dquery = factor * (dot3(halves(dnum), kv, COLS_LAST) + dden * ks) * jnp.minimum(query_map, 1.0)
-    terms_ref[1] = dot(feats_ref[...], dquery.astype(jnp.bfloat16), ROWS_FIRST)
-
-
-def grad_kernel(count_ref, packed_ref, feats_ref, key_ref, value_ref, dnum_ref, held_ref, terms_ref):
-    terms_ref[0] = held_ref[0]
-    terms_ref[1] = held_ref[1]
+    terms_ref[1] = dot(feats, dquery.astype(jnp.bfloat16), ROWS_FIRST)
+
+
+def grad_kernel(count_ref, packed_ref, feats_ref, w_ref, dnum_ref, early_ref, terms_ref):
+    terms_ref[0] = early_ref[0]
+    terms_ref[1] = early_ref[1]
     dkv, vectors = load_packed(packed_ref)
     dkv = halves(dkv)
     feats = feats_ref[...]
     alive = alive_of(count_ref, feats.shape[0])
-    key_map = key_ref[...]
+    key_map = feature_map(dot(feats, w_ref[1]))
     slope = jnp.minimum(key_map, 1.0) * alive
     dvalue = dnum_ref[...] + dot3(halves(key_map * alive), dkv)
-    dkey = (dot3(halves(value_ref[...]), dkv, COLS_LAST) + vectors[0:1]) * slope
+    dkey = (dot3(halves(dot(feats, w_ref[2])), dkv, COLS_LAST) + vectors[0:1]) * slope
     terms_ref[2] = dot(feats, dkey.astype(jnp.bfloat16), ROWS_FIRST)
     terms_ref[3] = dot(feats, dvalue.astype(jnp.bfloat16), ROWS_FIRST)
 
@@ -257,7 +261,7 @@
     packed_shape, rim_shape = shape((TILE, 1, PACK), f32), shape((rim, D), bf16)
     together = lax.optimization_barrier
 
-    packed, to_before, to_after = call(
+    packed, first, second = call(
         key_kernel, "keys", [packed_shape, rim_shape, rim_shape],
         count, node_feats, w_qkv, send_rows, away=(1, 2, 3), limit=None,
         scratch=[
@@ -266,27 +270,27 @@
         ],
     )
 
-    up = [(i, i + 1) for i in range(parts - 1)]
-    down = [(j, i) for i, j in up]
-    left = lax.ppermute(to_after, FINE, up)
-    right = lax.ppermute(to_before, FINE, down)
+    swap = [(i, i ^ 1) for i in range(parts)]
+    cross = [pair for i in range(1, parts - 1, 2) for pair in ((i, i + 1), (i + 1, i))]
+    first = lax.ppermute(first, FINE, swap)
+    second = lax.ppermute(second, FINE, cross)
     share = scatter_sum(packed, ("x", "c"), near)
-    share, left, right = together((share, left, right))
+    share, first, second, named = together((share, first, second, neighbours))
     hits = call(
-        hit_kernel, "hits", shape((rows + 2 * rim, rows), bf16), neighbours.T, neighbour_counts.reshape(1, rows)
-    )
-    agg, graph, query_map, key_map, value_rows = call(
-        graph_kernel, "graph", [rows_bf16, rows_f32, rows_f32, rows_f32, rows_f32],
-        hits, node_feats, left, right, w_graph, w_qkv,
+        hit_kernel, "hits", shape((rows + 2 * rim, rows), bf16), named.T, neighbour_counts.reshape(1, rows)
+    )
+    held, gain = call(
+        graph_kernel, "graph", [shape((2, rows, D), bf16), shape((1, D), f32)],
+        hits, node_feats, first, second, out_grad, ln_gain.reshape(1, D),
     )
     share = gather_sum(share, "y", sizes["y"])
-    share, agg, graph, query_map, key_map, value_rows = together((share, agg, graph, query_map, key_map, value_rows))
+    share, held, gain = together((share, held, gain))
     share = gather_sum(share, "z", sizes["z"])
     packed = gather(share, ("x", "c"), near)
 
     node_out, dnum, dpacked, terms, scale = call(
         mix_kernel, "mix", [rows_bf16, rows_f32, packed_shape, shape((2, D, D), f32), shape((1, D), f32)],
-        count, packed, node_feats, agg, query_map, value_rows, graph, out_grad, ln_gain.reshape(1, D),
+        count, packed, node_feats, w_qkv, w_graph, held, gain,
     )
 
     share = scatter_sum(dpacked, ("x", "c"), near)
@@ -294,9 +298,7 @@
     share = gather_sum(share, "z", sizes["z"])
     dpacked = gather(share, ("x", "c"), near)
 
-    terms = call(
-        grad_kernel, "grads", shape((4, D, D), f32), count, dpacked, node_feats, key_map, value_rows, dnum, terms
-    )
+    terms = call(grad_kernel, "grads", shape((4, D, D), f32), count, dpacked, node_feats, w_qkv, dnum, terms)
     total = sum_terms(terms.reshape(4 * D, D), sizes, scale).reshape(4, D, D)
     qkv_grad, graph_grad = call(
         split_kernel, "split", [shape((3, D, D), f32), shape((D, D), f32)], total,

time: 175 us -> 174 us (level)
  local copies, waits for them, and re-layouts: 4.39 us -> 2.25 us
  blocking collectives: 127 us -> 129 us
    unnamed x24 -> x18, local copies, waits for them, and re-layouts: 3.5 us -> 1.36 us
    all_to_all x1, waiting for transfers between devices: 4.86 us -> 2.93 us  [gather(): return lax.all_to_all(copies, axes, 0, 0, tiled=True)]
  transfers between devices with their start and end apart: 4 -> 4, of which waited for: 1 -> 2; matrix products, arithmetic and copies ran while one was open for 0% -> 0% of each run, Pallas kernels for 2% -> 2%
where the time goes in v5:
time: 174 us; the launch traced here: 173 us
  blocking collectives  129 us (74%)
  starting transfers between devices  25.8 us (15%)
  Pallas kernels  10.2 us (6%)
  waiting for transfers between devices  4.44 us (3%)
  local copies, waits for them, and re-layouts  2.25 us (1%)
    all_to_all x9, blocking collectives, gather(): return lax.all_to_all(copies, axes, 0, 0, tiled=True)  94.1 us
    all_to_all x4, blocking collectives, scatter_sum(): parts = lax.all_to_all(value, axes, 0, 0, tiled=True)  34.7 us
    pallas_call x6, Pallas kernels, call(): pl.pallas_call(kernel, in_specs=[far if i in away else near for i in rang...  10.2 us
    all_to_all x1, starting transfers between devices, scatter_sum(): parts = lax.all_to_all(value, axes, 0, 0, tiled=True)  10.1 us
    all_to_all x1, starting transfers between devices, gather(): return lax.all_to_all(copies, axes, 0, 0, tiled=True)  6.96 us
    ppermute x1, starting transfers between devices, local(): second = lax.ppermute(second, FINE, cross)  6.82 us
  transfers between devices with their start and end apart: 4, of which 2 were waited for; matrix products, arithmetic and copies ran while one was open for 0% of the time, Pallas kernels for 2%

profile of v5, /device:TPU:1, one launch (start us, length us, event | category | flops | bytes accessed | tf_op | source)
XLA Modules:
  0.0 173.5 jit_solution(10177378228776823)
XLA Ops:
  1.3 2.7 %keys.1 = (f32[8,1,1280]{2,1,0:T(1,128)}, bf16[64,256]{1,0:T(8,128)(2,1)}, bf16[64,256]{1,0:T(8,128)(2,1)}) custom-call(s32[1,1]{1,0:T(1,128)} %bitcast.11.count_ref, bf16[512,256]{1,0:T(8,128)(2,1)} %feats_ref.5, bf16[3,256,256]{2,1,0:T(8,128)(2,1)} %w_ref.3, s32[1,2,64]{2,1,0:T(2,128)} %send_hbm.1), custom_call_target="tpu_custom_call" | custom-call | flops 1000000000 | bytes 10000000 | tf_op jit(solution)/shard_map/keys/pallas_call | solution.py:216
  4.0 0.0 copy-start.8
  4.0 0.0 copy-start.7
  4.0 10.1 %all-to-all-start = ((f32[8,1,1280]{2,1,0:T(1,128)}), f32[8,1,1280]{2,1,0:T(1,128)S(1)}, u32[]{:S(2)}, u32[]{:S(2)}) async-start(f32[8,1,1280]{2,1,0:T(1,128)} %get-tuple-element.22), calls=%async_computation | async-start | bytes 81920 | tf_op jit(solution)/shard_map/all_to_all | solution.py:229
  14.1 0.0 copy-done.8
  14.1 1.9 %collective-permute-start = (bf16[64,256]{1,0:T(8,128)(2,1)S(1)}, bf16[64,256]{1,0:T(8,128)(2,1)S(1)}, u32[]{:S(2)}, u32[]{:S(2)}) collective-permute-start(bf16[64,256]{1,0:T(8,128)(2,1)S(1)} %copy-done.8), channel_id=1, source_target_pairs={{0,1},{1,0},{2,3},{3,2},{4,5},{5,4},{6,7},{7,6},{8,9},{9,8},{10,11... | collective-permute-start | bytes 98312 | tf_op jit(solution)/shard_map/ppermute | solution.py:275
  16.0 0.0 copy-done.7
  16.0 6.8 %collective-permute-start.1 = (bf16[64,256]{1,0:T(8,128)(2,1)S(1)}, bf16[64,256]{1,0:T(8,128)(2,1)S(1)}, u32[]{:S(2)}, u32[]{:S(2)}) collective-permute-start(bf16[64,256]{1,0:T(8,128)(2,1)S(1)} %copy-done.7), channel_id=1, source_target_pairs={{1,2},{2,1},{3,4},{4,3},{5,6},{6,5},{7,8},{8,7},{9,10},{10,9},{11,... | collective-permute-start | bytes 98312 | tf_op jit(solution)/shard_map/ppermute | solution.py:276
  22.9 0.0 all-to-all-done
  22.9 0.0 collective-permute-done.first_ref
  22.9 1.5 collective-permute-done.1.second_ref
  24.5 0.6 reshape.128
  25.1 0.0 copy-start.4
  25.1 7.0 %all-to-all-start.1 = ((f32[8,1,1280]{2,1,0:T(1,128)}), f32[8,1,1280]{2,1,0:T(1,128)S(1)}, u32[]{:S(2)}, u32[]{:S(2)}) async-start(f32[8,1,1280]{2,1,0:T(1,128)} %reshape.128), calls=%async_computation.1 | async-start | bytes 81920 | tf_op jit(solution)/shard_map/all_to_all | solution.py:235
  32.1 0.0 copy-start.5
  32.1 0.0 copy-done.4
  32.1 0.7 copy-done.5
  32.7 0.0 copy-start.1
  32.7 0.0 copy-start.2
  32.7 2.0 %hits.1.hits_ref = bf16[640,512]{1,0:T(8,128)(2,1)S(1)} custom-call(s32[16,512]{1,0:T(8,128)S(1)} %bitcast.17, s32[1,512]{1,0:T(1,128)S(1)} %bitcast.18), custom_call_target="tpu_custom_call" | custom-call | flops 1000000000 | bytes 10000000 | tf_op jit(solution)/shard_map/hits/pallas_call | solution.py:216
  34.7 0.0 copy-start.6
  34.7 0.0 copy-done.1
  34.8 0.0 copy-done.2
  34.8 0.7 copy-done.6
  35.4 0.0 copy-start.3
  35.4 0.7 graph.1
  36.1 0.0 copy-start
  36.1 2.9 %all-to-all-done.1 = f32[8,1,1280]{2,1,0:T(1,128)S(1)} async-done(((f32[8,1,1280]{2,1,0:T(1,128)}), f32[8,1,1280]{2,1,0:T(1,128)S(1)}, u32[]{:S(2)}, u32[]{:S(2)}) %all-to-all-start.1) | async-done | bytes 40992 | tf_op jit(solution)/shard_map/all_to_all | solution.py:235
  39.1 12.0 %all_to_all.91 = f32[8,1,1280]{2,1,0:T(1,128)S(1)} all-to-all(f32[8,1,1280]{2,1,0:T(1,128)S(1)} %reshape.131), channel_id=1, replica_groups=mesh['x'=4,'y'=8,'c'=2,'z'=8] {'z'}, dimensions={0} | all-to-all | bytes 81920 | tf_op jit(solution)/shard_map/all_to_all | solution.py:235
  51.2 12.7 %all_to_all.92.packed_ref = f32[8,1,1280]{2,1,0:T(1,128)S(1)} all-to-all(f32[8,1,1280]{2,1,0:T(1,128)S(1)} %reshape.132), channel_id=1, replica_groups=mesh['x'=4,'y'=8,'c'=2,'z'=8] {'x','c'}, dimensions={0} | all-to-all | bytes 81920 | tf_op jit(solution)/shard_map/all_to_all | solution.py:235
  64.0 0.0 copy-done.3
  64.0 0.0 copy-done
  64.0 2.7 %mix.1 = (bf16[512,256]{1,0:T(8,128)(2,1)}, f32[512,256]{1,0:T(8,128)S(1)}, f32[8,1,1280]{2,1,0:T(1,128)S(1)}, f32[2,256,256]{2,1,0:T(8,128)S(1)}, f32[1,256]{1,0:T(1,128)S(1)}) custom-call(s32[1,1]{1,0:T(1,128)} %bitcast.12.count_ref, f32[8,1,1280]{2,1,0:T(1,128)S(1)} %all_to_all.92.packed_ref, bf16[512,256]{1,0:T(8,128)(2,1)S(1)} %copy-done.2, ...), custom_call_target="tpu_custom_call" | custom-call | flops 1000000000 | bytes 10000000 | tf_op jit(solution)/shard_map/mix/pallas_call | solution.py:216
  66.7 7.8 %all_to_all.93 = f32[8,1,1280]{2,1,0:T(1,128)S(1)} all-to-all(f32[8,1,1280]{2,1,0:T(1,128)S(1)} %get-tuple-element.35), channel_id=1, replica_groups=mesh['x'=4,'y'=8,'c'=2,'z'=8] {'x','c'}, dimensions={0} | all-to-all | bytes 81920 | tf_op jit(solution)/shard_map/all_to_all | solution.py:229
  74.6 9.6 %all_to_all.94 = f32[8,1,1280]{2,1,0:T(1,128)S(1)} all-to-all(f32[8,1,1280]{2,1,0:T(1,128)S(1)} %reshape.133), channel_id=1, replica_groups=mesh['x'=4,'y'=8,'c'=2,'z'=8] {'y'}, dimensions={0} | all-to-all | bytes 81920 | tf_op jit(solution)/shard_map/all_to_all | solution.py:235
  84.3 9.3 %all_to_all.95 = f32[8,1,1280]{2,1,0:T(1,128)S(1)} all-to-all(f32[8,1,1280]{2,1,0:T(1,128)S(1)} %reshape.134), channel_id=1, replica_groups=mesh['x'=4,'y'=8,'c'=2,'z'=8] {'z'}, dimensions={0} | all-to-all | bytes 81920 | tf_op jit(solution)/shard_map/all_to_all | solution.py:235
  93.7 10.4 %all_to_all.96.packed_ref = f32[8,1,1280]{2,1,0:T(1,128)S(1)} all-to-all(f32[8,1,1280]{2,1,0:T(1,128)S(1)} %reshape.135), channel_id=1, replica_groups=mesh['x'=4,'y'=8,'c'=2,'z'=8] {'x','c'}, dimensions={0} | all-to-all | bytes 81920 | tf_op jit(solution)/shard_map/all_to_all | solution.py:235
  104.1 1.2 grads.1
  105.3 4.9 %all_to_all.97 = f32[2,512,256]{2,1,0:T(8,128)S(1)} all-to-all(f32[2,512,256]{2,1,0:T(8,128)S(1)} %bitcast.14), channel_id=1, replica_groups=mesh['x'=4,'y'=8,'c'=2,'z'=8] {'c'}, dimensions={0} | all-to-all | bytes 2097152 | tf_op jit(solution)/shard_map/all_to_all | solution.py:229
  110.3 0.1 reduce_sum.102
  110.4 11.6 %all_to_all.98 = f32[4,128,256]{2,1,0:T(8,128)S(1)} all-to-all(f32[4,128,256]{2,1,0:T(8,128)S(1)} %bitcast.21), channel_id=1, replica_groups=mesh['x'=4,'y'=8,'c'=2,'z'=8] {'x'}, dimensions={0} | all-to-all | bytes 1048576 | tf_op jit(solution)/shard_map/all_to_all | solution.py:229
  122.0 10.3 %all_to_all.99 = f32[8,16,256]{2,1,0:T(8,128)S(1)} all-to-all(f32[8,16,256]{2,1,0:T(8,128)S(1)} %bitcast.23), channel_id=1, replica_groups=mesh['x'=4,'y'=8,'c'=2,'z'=8] {'y'}, dimensions={0} | all-to-all | bytes 262144 | tf_op jit(solution)/shard_map/all_to_all | solution.py:229
  132.4 10.4 %all_to_all.100 = f32[8,16,256]{2,1,0:T(8,128)S(1)} all-to-all(f32[8,16,256]{2,1,0:T(8,128)S(1)} %broadcast_in_dim.18), channel_id=1, replica_groups=mesh['x'=4,'y'=8,'c'=2,'z'=8] {'z'}, dimensions={0} | all-to-all | bytes 262144 | tf_op jit(solution)/shard_map/all_to_all | solution.py:235
  142.9 10.4 %all_to_all.101 = f32[8,16,256]{2,1,0:T(8,128)S(1)} all-to-all(f32[8,16,256]{2,1,0:T(8,128)S(1)} %broadcast_in_dim.19), channel_id=1, replica_groups=mesh['x'=4,'y'=8,'c'=2,'z'=8] {'y'}, dimensions={0} | all-to-all | bytes 262144 | tf_op jit(solution)/shard_map/all_to_all | solution.py:235
  153.3 9.3 %all_to_all.102 = f32[4,128,256]{2,1,0:T(8,128)S(1)} all-to-all(f32[4,128,256]{2,1,0:T(8,128)S(1)} %broadcast_in_dim.21), channel_id=1, replica_groups=mesh['x'=4,'y'=8,'c'=2,'z'=8] {'x'}, dimensions={0} | all-to-all | bytes 1048576 | tf_op jit(solution)/shard_map/all_to_all | solution.py:235
  162.7 0.1 broadcast_in_dim.23
  162.7 9.8 %all_to_all.103 = f32[2,512,256]{2,1,0:T(8,128)S(1)} all-to-all(f32[2,512,256]{2,1,0:T(8,128)S(1)} %broadcast_in_dim.23), channel_id=1, replica_groups=mesh['x'=4,'y'=8,'c'=2,'z'=8] {'c'}, dimensions={0} | all-to-all | bytes 2097152 | tf_op jit(solution)/shard_map/all_to_all | solution.py:235
  172.5 1.0 split.1
  (22 shorter events, 0.5 us)
Async XLA Ops:
  4.0 10.1 %copy-start.8 = (bf16[64,256]{1,0:T(8,128)(2,1)S(1)}, bf16[64,256]{1,0:T(8,128)(2,1)}, u32[]{:S(2)}) copy-start(bf16[64,256]{1,0:T(8,128)(2,1)} %get-tuple-element.23) | copy-start | bytes 98308
  4.0 12.0 %copy-start.7 = (bf16[64,256]{1,0:T(8,128)(2,1)S(1)}, bf16[64,256]{1,0:T(8,128)(2,1)}, u32[]{:S(2)}) copy-start(bf16[64,256]{1,0:T(8,128)(2,1)} %get-tuple-element.24) | copy-start | bytes 98308
  4.0 18.9 %all-to-all-start = ((f32[8,1,1280]{2,1,0:T(1,128)}), f32[8,1,1280]{2,1,0:T(1,128)S(1)}, u32[]{:S(2)}, u32[]{:S(2)}) async-start(f32[8,1,1280]{2,1,0:T(1,128)} %get-tuple-element.22), calls=%async_computation | async-start | bytes 81920 | tf_op jit(solution)/shard_map/all_to_all | solution.py:229
  14.1 8.8 %collective-permute-start = (bf16[64,256]{1,0:T(8,128)(2,1)S(1)}, bf16[64,256]{1,0:T(8,128)(2,1)S(1)}, u32[]{:S(2)}, u32[]{:S(2)}) collective-permute-start(bf16[64,256]{1,0:T(8,128)(2,1)S(1)} %copy-done.8), channel_id=1, source_target_pairs={{0,1},{1,0},{2,3},{3,2},{4,5},{5,4},{6,7},{7,6},{8,9},{9,8},{10,11... | collective-permute-start | bytes 98312 | tf_op jit(solution)/shard_map/ppermute | solution.py:275
  16.0 8.4 %collective-permute-start.1 = (bf16[64,256]{1,0:T(8,128)(2,1)S(1)}, bf16[64,256]{1,0:T(8,128)(2,1)S(1)}, u32[]{:S(2)}, u32[]{:S(2)}) collective-permute-start(bf16[64,256]{1,0:T(8,128)(2,1)S(1)} %copy-done.7), channel_id=1, source_target_pairs={{1,2},{2,1},{3,4},{4,3},{5,6},{6,5},{7,8},{8,7},{9,10},{10,9},{11,... | collective-permute-start | bytes 98312 | tf_op jit(solution)/shard_map/ppermute | solution.py:276
  25.1 7.0 %copy-start.4 = (s32[512,16]{0,1:T(8,128)S(1)}, s32[512,16]{0,1:T(8,128)}, u32[]{:S(2)}) copy-start(s32[512,16]{0,1:T(8,128)} %param.16) | copy-start | bytes 98308
  25.1 13.9 %all-to-all-start.1 = ((f32[8,1,1280]{2,1,0:T(1,128)}), f32[8,1,1280]{2,1,0:T(1,128)S(1)}, u32[]{:S(2)}, u32[]{:S(2)}) async-start(f32[8,1,1280]{2,1,0:T(1,128)} %reshape.128), calls=%async_computation.1 | async-start | bytes 81920 | tf_op jit(solution)/shard_map/all_to_all | solution.py:235
  32.1 0.7 copy-start.5
  32.7 2.0 %copy-start.1 = (bf16[512,256]{1,0:T(8,128)(2,1)S(1)}, bf16[512,256]{1,0:T(8,128)(2,1)}, u32[]{:S(2)}) copy-start(bf16[512,256]{1,0:T(8,128)(2,1)} %grad_ref.1) | copy-start | bytes 786436
  32.7 2.0 %copy-start.2 = (bf16[512,256]{1,0:T(8,128)(2,1)S(1)}, bf16[512,256]{1,0:T(8,128)(2,1)}, u32[]{:S(2)}) copy-start(bf16[512,256]{1,0:T(8,128)(2,1)} %feats_ref.5) | copy-start | bytes 786436
  34.7 0.7 copy-start.6
  35.4 28.5 %copy-start.3 = (bf16[256,256]{1,0:T(8,128)(2,1)S(1)}, bf16[256,256]{1,0:T(8,128)(2,1)}, u32[]{:S(2)}) copy-start(bf16[256,256]{1,0:T(8,128)(2,1)} %wg_ref.1) | copy-start | bytes 393220
  36.1 27.9 %copy-start = (bf16[3,256,256]{2,1,0:T(8,128)(2,1)S(1)}, bf16[3,256,256]{2,1,0:T(8,128)(2,1)}, u32[]{:S(2)}) copy-start(bf16[3,256,256]{2,1,0:T(8,128)(2,1)} %w_ref.3) | copy-start | bytes 1179652

commit v6 on v5

--- a/solution.py
+++ b/solution.py
@@ -6,6 +6,7 @@
 from jax.experimental import pallas as pl
 from jax.experimental.pallas import tpu as pltpu
 from jax.sharding import Mesh, PartitionSpec as P
+
 
 D = 256
 DH = 32
@@ -210,7 +211,7 @@
         copy.wait()
 
 
-def call(kernel, name, shapes, *args, away=(), outs_away=False, scratch=(), limit=VMEM_LIMIT):
+def call(kernel, shapes, *args, away=(), outs_away=False, scratch=(), limit=VMEM_LIMIT):
     near = pl.BlockSpec(memory_space=pltpu.VMEM)
     far = pl.BlockSpec(memory_space=pltpu.MemorySpace.HBM)
     return pl.pallas_call(
@@ -221,7 +222,6 @@
         scratch_shapes=scratch,
         cost_estimate=pl.CostEstimate(flops=10**9, bytes_accessed=10**7, transcendentals=0),
         compiler_params=pltpu.CompilerParams(vmem_limit_bytes=limit),
-        name=name,
     )(*args)
 
 
@@ -262,7 +262,7 @@
     together = lax.optimization_barrier
 
     packed, first, second = call(
-        key_kernel, "keys", [packed_shape, rim_shape, rim_shape],
+        key_kernel, [packed_shape, rim_shape, rim_shape],
         count, node_feats, w_qkv, send_rows, away=(1, 2, 3), limit=None,
         scratch=[
             pltpu.VMEM((rows, D), bf16), pltpu.VMEM((2, D, D), bf16), pltpu.VMEM(send_rows.shape, jnp.int32),
@@ -275,12 +275,10 @@
     first = lax.ppermute(first, FINE, swap)
     second = lax.ppermute(second, FINE, cross)
     share = scatter_sum(packed, ("x", "c"), near)
-    share, first, second, named = together((share, first, second, neighbours))
-    hits = call(
-        hit_kernel, "hits", shape((rows + 2 * rim, rows), bf16), named.T, neighbour_counts.reshape(1, rows)
-    )
+    share, named = together((share, neighbours))
+    hits = call(hit_kernel, shape((rows + 2 * rim, rows), bf16), named.T, neighbour_counts.reshape(1, rows))
     held, gain = call(
-        graph_kernel, "graph", [shape((2, rows, D), bf16), shape((1, D), f32)],
+        graph_kernel, [shape((2, rows, D), bf16), shape((1, D), f32)],
         hits, node_feats, first, second, out_grad, ln_gain.reshape(1, D),
     )
     share = gather_sum(share, "y", sizes["y"])
@@ -289,7 +287,7 @@
     packed = gather(share, ("x", "c"), near)
 
     node_out, dnum, dpacked, terms, scale = call(
-        mix_kernel, "mix", [rows_bf16, rows_f32, packed_shape, shape((2, D, D), f32), shape((1, D), f32)],
+        mix_kernel, [rows_bf16, rows_f32, packed_shape, shape((2, D, D), f32), shape((1, D), f32)],
         count, packed, node_feats, w_qkv, w_graph, held, gain,
     )
 
@@ -298,10 +296,10 @@
     share = gather_sum(share, "z", sizes["z"])
     dpacked = gather(share, ("x", "c"), near)
 
-    terms = call(grad_kernel, "grads", shape((4, D, D), f32), count, dpacked, node_feats, w_qkv, dnum, terms)
+    terms = call(grad_kernel, shape((4, D, D), f32), count, dpacked, node_feats, w_qkv, dnum, terms)
     total = sum_terms(terms.reshape(4 * D, D), sizes, scale).reshape(4, D, D)
     qkv_grad, graph_grad = call(
-        split_kernel, "split", [shape((3, D, D), f32), shape((D, D), f32)], total,
+        split_kernel, [shape((3, D, D), f32), shape((D, D), f32)], total,
         outs_away=True, scratch=[pltpu.SemaphoreType.DMA((2,))],
     )
     return node_out, qkv_grad, graph_grad

time: 174 us -> 171 us (0.983)
  blocking collectives: 129 us -> 127 us
    all_to_all x9, blocking collectives: 94.1 us -> 92.1 us  [gather(): return lax.all_to_all(copies, axes, 0, 0, tiled=True)]
  transfers between devices with their start and end apart: 4 -> 4, of which waited for: 2 -> 1; matrix products, arithmetic and copies ran while one was open for 0% -> 0% of each run, Pallas kernels for 2% -> 2%
where the time goes in v6:
time: 171 us; the launch traced here: 170 us
  blocking collectives  127 us (74%)
  starting transfers between devices  25.8 us (15%)
  Pallas kernels  10.2 us (6%)
  waiting for transfers between devices  2.94 us (2%)
  local copies, waits for them, and re-layouts  2.23 us (1%)
    all_to_all x9, blocking collectives, gather(): return lax.all_to_all(copies, axes, 0, 0, tiled=True)  92.1 us
    all_to_all x4, blocking collectives, scatter_sum(): parts = lax.all_to_all(value, axes, 0, 0, tiled=True)  34.7 us
    pallas_call x6, Pallas kernels, call(): pl.pallas_call(kernel, in_specs=[far if i in away else near for i in rang...  10.2 us
    all_to_all x1, starting transfers between devices, scatter_sum(): parts = lax.all_to_all(value, axes, 0, 0, tiled=True)  10.1 us
    all_to_all x1, starting transfers between devices, gather(): return lax.all_to_all(copies, axes, 0, 0, tiled=True)  6.96 us
    ppermute x1, starting transfers between devices, local(): second = lax.ppermute(second, FINE, cross)  6.82 us
  transfers between devices with their start and end apart: 4, of which 1 were waited for; matrix products, arithmetic and copies ran while one was open for 0% of the time, Pallas kernels for 2%

profile of v6, /device:TPU:1, one launch (start us, length us, event | category | flops | bytes accessed | tf_op | source)
XLA Modules:
  0.0 169.9 jit_solution(16085636910898779020)
XLA Ops:
  1.3 2.7 %shard_map.112 = (f32[8,1,1280]{2,1,0:T(1,128)}, bf16[64,256]{1,0:T(8,128)(2,1)}, bf16[64,256]{1,0:T(8,128)(2,1)}) custom-call(s32[1,1]{1,0:T(1,128)} %bitcast.11.count_ref, bf16[512,256]{1,0:T(8,128)(2,1)} %feats_ref.5, bf16[3,256,256]{2,1,0:T(8,128)(2,1)} %w_ref.3, s32[1,2,64]{2,1,0:T(2,128)} %send_hbm.1), custom_call_target="tpu_custom_call" | custom-call | flops 1000000000 | bytes 10000000 | tf_op jit(solution)/shard_map/pallas_call | solution.py:217
  4.0 0.0 copy-start.8
  4.0 0.0 copy-start.7
  4.0 10.1 %all-to-all-start = ((f32[8,1,1280]{2,1,0:T(1,128)}), f32[8,1,1280]{2,1,0:T(1,128)S(1)}, u32[]{:S(2)}, u32[]{:S(2)}) async-start(f32[8,1,1280]{2,1,0:T(1,128)} %get-tuple-element.20), calls=%async_computation | async-start | bytes 81920 | tf_op jit(solution)/shard_map/all_to_all | solution.py:229
  14.1 0.0 copy-done.8
  14.1 1.9 %collective-permute-start = (bf16[64,256]{1,0:T(8,128)(2,1)S(1)}, bf16[64,256]{1,0:T(8,128)(2,1)S(1)}, u32[]{:S(2)}, u32[]{:S(2)}) collective-permute-start(bf16[64,256]{1,0:T(8,128)(2,1)S(1)} %copy-done.8), channel_id=1, source_target_pairs={{0,1},{1,0},{2,3},{3,2},{4,5},{5,4},{6,7},{7,6},{8,9},{9,8},{10,11... | collective-permute-start | bytes 98312 | tf_op jit(solution)/shard_map/ppermute | solution.py:275
  16.0 0.0 copy-done.7
  16.0 6.8 %collective-permute-start.1 = (bf16[64,256]{1,0:T(8,128)(2,1)S(1)}, bf16[64,256]{1,0:T(8,128)(2,1)S(1)}, u32[]{:S(2)}, u32[]{:S(2)}) collective-permute-start(bf16[64,256]{1,0:T(8,128)(2,1)S(1)} %copy-done.7), channel_id=1, source_target_pairs={{1,2},{2,1},{3,4},{4,3},{5,6},{6,5},{7,8},{8,7},{9,10},{10,9},{11,... | collective-permute-start | bytes 98312 | tf_op jit(solution)/shard_map/ppermute | solution.py:276
  22.9 0.0 all-to-all-done
  22.9 0.6 reshape.128
  23.6 0.0 copy-start.4
  23.6 7.0 %all-to-all-start.1 = ((f32[8,1,1280]{2,1,0:T(1,128)}), f32[8,1,1280]{2,1,0:T(1,128)S(1)}, u32[]{:S(2)}, u32[]{:S(2)}) async-start(f32[8,1,1280]{2,1,0:T(1,128)} %reshape.128), calls=%async_computation.1 | async-start | bytes 81920 | tf_op jit(solution)/shard_map/all_to_all | solution.py:235
  30.5 0.0 copy-start.5
  30.6 0.0 copy-done.4
  30.6 0.7 copy-done.5
  31.2 0.0 copy-start.1
  31.2 0.0 copy-start.2
  31.2 2.0 %shard_map.113.hits_ref = bf16[640,512]{1,0:T(8,128)(2,1)S(1)} custom-call(s32[16,512]{1,0:T(8,128)S(1)} %bitcast.17, s32[1,512]{1,0:T(1,128)S(1)} %bitcast.18), custom_call_target="tpu_custom_call" | custom-call | flops 1000000000 | bytes 10000000 | tf_op jit(solution)/shard_map/pallas_call | solution.py:217
  33.2 0.0 copy-start.6
  33.2 0.0 collective-permute-done.first_ref
  33.2 0.0 collective-permute-done.1.second_ref
  33.3 0.0 copy-done.1
  33.3 0.0 copy-done.2
  33.3 0.6 copy-done.6
  33.9 0.0 copy-start.3
  33.9 0.7 shard_map.114
  34.6 0.0 copy-start
  34.6 2.9 %all-to-all-done.1 = f32[8,1,1280]{2,1,0:T(1,128)S(1)} async-done(((f32[8,1,1280]{2,1,0:T(1,128)}), f32[8,1,1280]{2,1,0:T(1,128)S(1)}, u32[]{:S(2)}, u32[]{:S(2)}) %all-to-all-start.1) | async-done | bytes 40992 | tf_op jit(solution)/shard_map/all_to_all | solution.py:235
  37.6 9.9 %all_to_all.91 = f32[8,1,1280]{2,1,0:T(1,128)S(1)} all-to-all(f32[8,1,1280]{2,1,0:T(1,128)S(1)} %reshape.131), channel_id=1, replica_groups=mesh['x'=4,'y'=8,'c'=2,'z'=8] {'z'}, dimensions={0} | all-to-all | bytes 81920 | tf_op jit(solution)/shard_map/all_to_all | solution.py:235
  47.6 12.8 %all_to_all.92.packed_ref = f32[8,1,1280]{2,1,0:T(1,128)S(1)} all-to-all(f32[8,1,1280]{2,1,0:T(1,128)S(1)} %reshape.132), channel_id=1, replica_groups=mesh['x'=4,'y'=8,'c'=2,'z'=8] {'x','c'}, dimensions={0} | all-to-all | bytes 81920 | tf_op jit(solution)/shard_map/all_to_all | solution.py:235
  60.4 0.0 copy-done.3
  60.4 0.0 copy-done
  60.4 2.7 %shard_map.115 = (bf16[512,256]{1,0:T(8,128)(2,1)}, f32[512,256]{1,0:T(8,128)S(1)}, f32[8,1,1280]{2,1,0:T(1,128)S(1)}, f32[2,256,256]{2,1,0:T(8,128)S(1)}, f32[1,256]{1,0:T(1,128)S(1)}) custom-call(s32[1,1]{1,0:T(1,128)} %bitcast.12.count_ref, f32[8,1,1280]{2,1,0:T(1,128)S(1)} %all_to_all.92.packed_ref, bf16[512,256]{1,0:T(8,128)(2,1)S(1)} %copy-done.2, ...), custom_call_target="tpu_custom_call" | custom-call | flops 1000000000 | bytes 10000000 | tf_op jit(solution)/shard_map/pallas_call | solution.py:217
  63.1 7.8 %all_to_all.93 = f32[8,1,1280]{2,1,0:T(1,128)S(1)} all-to-all(f32[8,1,1280]{2,1,0:T(1,128)S(1)} %get-tuple-element.31), channel_id=1, replica_groups=mesh['x'=4,'y'=8,'c'=2,'z'=8] {'x','c'}, dimensions={0} | all-to-all | bytes 81920 | tf_op jit(solution)/shard_map/all_to_all | solution.py:229
  71.0 9.6 %all_to_all.94 = f32[8,1,1280]{2,1,0:T(1,128)S(1)} all-to-all(f32[8,1,1280]{2,1,0:T(1,128)S(1)} %reshape.133), channel_id=1, replica_groups=mesh['x'=4,'y'=8,'c'=2,'z'=8] {'y'}, dimensions={0} | all-to-all | bytes 81920 | tf_op jit(solution)/shard_map/all_to_all | solution.py:235
  80.7 9.3 %all_to_all.95 = f32[8,1,1280]{2,1,0:T(1,128)S(1)} all-to-all(f32[8,1,1280]{2,1,0:T(1,128)S(1)} %reshape.134), channel_id=1, replica_groups=mesh['x'=4,'y'=8,'c'=2,'z'=8] {'z'}, dimensions={0} | all-to-all | bytes 81920 | tf_op jit(solution)/shard_map/all_to_all | solution.py:235
  90.1 10.4 %all_to_all.96.packed_ref = f32[8,1,1280]{2,1,0:T(1,128)S(1)} all-to-all(f32[8,1,1280]{2,1,0:T(1,128)S(1)} %reshape.135), channel_id=1, replica_groups=mesh['x'=4,'y'=8,'c'=2,'z'=8] {'x','c'}, dimensions={0} | all-to-all | bytes 81920 | tf_op jit(solution)/shard_map/all_to_all | solution.py:235
  100.6 1.2 shard_map.116
  101.8 4.9 %all_to_all.97 = f32[2,512,256]{2,1,0:T(8,128)S(1)} all-to-all(f32[2,512,256]{2,1,0:T(8,128)S(1)} %bitcast.14), channel_id=1, replica_groups=mesh['x'=4,'y'=8,'c'=2,'z'=8] {'c'}, dimensions={0} | all-to-all | bytes 2097152 | tf_op jit(solution)/shard_map/all_to_all | solution.py:229
  106.7 0.1 reduce_sum.102
  106.8 11.6 %all_to_all.98 = f32[4,128,256]{2,1,0:T(8,128)S(1)} all-to-all(f32[4,128,256]{2,1,0:T(8,128)S(1)} %bitcast.21), channel_id=1, replica_groups=mesh['x'=4,'y'=8,'c'=2,'z'=8] {'x'}, dimensions={0} | all-to-all | bytes 1048576 | tf_op jit(solution)/shard_map/all_to_all | solution.py:229
  118.5 10.3 %all_to_all.99 = f32[8,16,256]{2,1,0:T(8,128)S(1)} all-to-all(f32[8,16,256]{2,1,0:T(8,128)S(1)} %bitcast.23), channel_id=1, replica_groups=mesh['x'=4,'y'=8,'c'=2,'z'=8] {'y'}, dimensions={0} | all-to-all | bytes 262144 | tf_op jit(solution)/shard_map/all_to_all | solution.py:229
  128.9 10.4 %all_to_all.100 = f32[8,16,256]{2,1,0:T(8,128)S(1)} all-to-all(f32[8,16,256]{2,1,0:T(8,128)S(1)} %broadcast_in_dim.18), channel_id=1, replica_groups=mesh['x'=4,'y'=8,'c'=2,'z'=8] {'z'}, dimensions={0} | all-to-all | bytes 262144 | tf_op jit(solution)/shard_map/all_to_all | solution.py:235
  139.3 10.4 %all_to_all.101 = f32[8,16,256]{2,1,0:T(8,128)S(1)} all-to-all(f32[8,16,256]{2,1,0:T(8,128)S(1)} %broadcast_in_dim.19), channel_id=1, replica_groups=mesh['x'=4,'y'=8,'c'=2,'z'=8] {'y'}, dimensions={0} | all-to-all | bytes 262144 | tf_op jit(solution)/shard_map/all_to_all | solution.py:235
  149.8 9.3 %all_to_all.102 = f32[4,128,256]{2,1,0:T(8,128)S(1)} all-to-all(f32[4,128,256]{2,1,0:T(8,128)S(1)} %broadcast_in_dim.21), channel_id=1, replica_groups=mesh['x'=4,'y'=8,'c'=2,'z'=8] {'x'}, dimensions={0} | all-to-all | bytes 1048576 | tf_op jit(solution)/shard_map/all_to_all | solution.py:235
  159.1 0.1 broadcast_in_dim.23
  159.2 9.8 %all_to_all.103 = f32[2,512,256]{2,1,0:T(8,128)S(1)} all-to-all(f32[2,512,256]{2,1,0:T(8,128)S(1)} %broadcast_in_dim.23), channel_id=1, replica_groups=mesh['x'=4,'y'=8,'c'=2,'z'=8] {'c'}, dimensions={0} | all-to-all | bytes 2097152 | tf_op jit(solution)/shard_map/all_to_all | solution.py:235
  169.0 1.0 shard_map.117
  (22 shorter events, 0.5 us)
Async XLA Ops:
  4.0 10.1 %copy-start.8 = (bf16[64,256]{1,0:T(8,128)(2,1)S(1)}, bf16[64,256]{1,0:T(8,128)(2,1)}, u32[]{:S(2)}) copy-start(bf16[64,256]{1,0:T(8,128)(2,1)} %get-tuple-element.23) | copy-start | bytes 98308
  4.0 12.0 %copy-start.7 = (bf16[64,256]{1,0:T(8,128)(2,1)S(1)}, bf16[64,256]{1,0:T(8,128)(2,1)}, u32[]{:S(2)}) copy-start(bf16[64,256]{1,0:T(8,128)(2,1)} %get-tuple-element.24) | copy-start | bytes 98308
  4.0 18.9 %all-to-all-start = ((f32[8,1,1280]{2,1,0:T(1,128)}), f32[8,1,1280]{2,1,0:T(1,128)S(1)}, u32[]{:S(2)}, u32[]{:S(2)}) async-start(f32[8,1,1280]{2,1,0:T(1,128)} %get-tuple-element.20), calls=%async_computation | async-start | bytes 81920 | tf_op jit(solution)/shard_map/all_to_all | solution.py:229
  14.1 19.1 %collective-permute-start = (bf16[64,256]{1,0:T(8,128)(2,1)S(1)}, bf16[64,256]{1,0:T(8,128)(2,1)S(1)}, u32[]{:S(2)}, u32[]{:S(2)}) collective-permute-start(bf16[64,256]{1,0:T(8,128)(2,1)S(1)} %copy-done.8), channel_id=1, source_target_pairs={{0,1},{1,0},{2,3},{3,2},{4,5},{5,4},{6,7},{7,6},{8,9},{9,8},{10,11... | collective-permute-start | bytes 98312 | tf_op jit(solution)/shard_map/ppermute | solution.py:275
  16.0 17.2 %collective-permute-start.1 = (bf16[64,256]{1,0:T(8,128)(2,1)S(1)}, bf16[64,256]{1,0:T(8,128)(2,1)S(1)}, u32[]{:S(2)}, u32[]{:S(2)}) collective-permute-start(bf16[64,256]{1,0:T(8,128)(2,1)S(1)} %copy-done.7), channel_id=1, source_target_pairs={{1,2},{2,1},{3,4},{4,3},{5,6},{6,5},{7,8},{8,7},{9,10},{10,9},{11,... | collective-permute-start | bytes 98312 | tf_op jit(solution)/shard_map/ppermute | solution.py:276
  23.6 7.0 %copy-start.4 = (s32[512,16]{0,1:T(8,128)S(1)}, s32[512,16]{0,1:T(8,128)}, u32[]{:S(2)}) copy-start(s32[512,16]{0,1:T(8,128)} %param.16) | copy-start | bytes 98308
  23.6 13.9 %all-to-all-start.1 = ((f32[8,1,1280]{2,1,0:T(1,128)}), f32[8,1,1280]{2,1,0:T(1,128)S(1)}, u32[]{:S(2)}, u32[]{:S(2)}) async-start(f32[8,1,1280]{2,1,0:T(1,128)} %reshape.128), calls=%async_computation.1 | async-start | bytes 81920 | tf_op jit(solution)/shard_map/all_to_all | solution.py:235
  30.5 0.7 copy-start.5
  31.2 2.0 %copy-start.1 = (bf16[512,256]{1,0:T(8,128)(2,1)S(1)}, bf16[512,256]{1,0:T(8,128)(2,1)}, u32[]{:S(2)}) copy-start(bf16[512,256]{1,0:T(8,128)(2,1)} %grad_ref.1) | copy-start | bytes 786436
  31.2 2.0 %copy-start.2 = (bf16[512,256]{1,0:T(8,128)(2,1)S(1)}, bf16[512,256]{1,0:T(8,128)(2,1)}, u32[]{:S(2)}) copy-start(bf16[512,256]{1,0:T(8,128)(2,1)} %feats_ref.5) | copy-start | bytes 786436
  33.2 0.7 copy-start.6
  33.9 26.5 %copy-start.3 = (bf16[256,256]{1,0:T(8,128)(2,1)S(1)}, bf16[256,256]{1,0:T(8,128)(2,1)}, u32[]{:S(2)}) copy-start(bf16[256,256]{1,0:T(8,128)(2,1)} %wg_ref.1) | copy-start | bytes 393220
  34.6 25.8 %copy-start = (bf16[3,256,256]{2,1,0:T(8,128)(2,1)S(1)}, bf16[3,256,256]{2,1,0:T(8,128)(2,1)}, u32[]{:S(2)}) copy-start(bf16[3,256,256]{2,1,0:T(8,128)(2,1)} %w_ref.3) | copy-start | bytes 1179652

commit v7 on v6

--- a/solution.py
+++ b/solution.py
@@ -240,12 +240,12 @@
 
 
 def sum_terms(terms, sizes, scale):
+    plane = ("x", "z")
+    spread = sizes["x"] * sizes["z"]
     value = scatter_sum(terms, "c", sizes["c"])
-    value = scatter_sum(value, "x", sizes["x"])
-    value = scatter_sum(value, "y", sizes["y"])
-    value = gather_sum(value, "z", sizes["z"]) * scale
-    value = gather(value, "y", sizes["y"])
-    value = gather(value, "x", sizes["x"])
+    value = scatter_sum(value, plane, spread)
+    value = gather_sum(value, "y", sizes["y"]) * scale
+    value = gather(value, plane, spread)
     return gather(value, "c", sizes["c"])
 
 

time: 171 us -> 167 us (0.977)
  blocking collectives: 127 us -> 123 us
    all_to_all x4 -> x3, blocking collectives: 34.7 us -> 30.7 us  [scatter_sum(): parts = lax.all_to_all(value, axes, 0, 0, tiled=True)]
    all_to_all x9 -> x8, blocking collectives: 92.1 us -> 91.9 us  [gather(): return lax.all_to_all(copies, axes, 0, 0, tiled=True)]
where the time goes in v7:
time: 167 us; the launch traced here: 166 us
  blocking collectives  123 us (74%)
  starting transfers between devices  25.8 us (15%)
  Pallas kernels  10.2 us (6%)
  waiting for transfers between devices  2.94 us (2%)
  local copies, waits for them, and re-layouts  2.23 us (1%)
    all_to_all x8, blocking collectives, gather(): return lax.all_to_all(copies, axes, 0, 0, tiled=True)  91.9 us
    all_to_all x3, blocking collectives, scatter_sum(): parts = lax.all_to_all(value, axes, 0, 0, tiled=True)  30.7 us
    pallas_call x6, Pallas kernels, call(): pl.pallas_call(kernel, in_specs=[far if i in away else near for i in rang...  10.2 us
    all_to_all x1, starting transfers between devices, scatter_sum(): parts = lax.all_to_all(value, axes, 0, 0, tiled=True)  10.1 us
    all_to_all x1, starting transfers between devices, gather(): return lax.all_to_all(copies, axes, 0, 0, tiled=True)  6.96 us
    ppermute x1, starting transfers between devices, local(): second = lax.ppermute(second, FINE, cross)  6.82 us
  transfers between devices with their start and end apart: 4, of which 1 were waited for; matrix products, arithmetic and copies ran while one was open for 0% of the time, Pallas kernels for 2%

profile of v7, /device:TPU:1, one launch (start us, length us, event | category | flops | bytes accessed | tf_op | source)
XLA Modules:
  0.0 165.7 jit_solution(16531266778368175443)
XLA Ops:
  1.3 2.7 %shard_map.112 = (f32[8,1,1280]{2,1,0:T(1,128)}, bf16[64,256]{1,0:T(8,128)(2,1)}, bf16[64,256]{1,0:T(8,128)(2,1)}) custom-call(s32[1,1]{1,0:T(1,128)} %bitcast.9.count_ref, bf16[512,256]{1,0:T(8,128)(2,1)} %feats_ref.5, bf16[3,256,256]{2,1,0:T(8,128)(2,1)} %w_ref.3, s32[1,2,64]{2,1,0:T(2,128)} %send_hbm.1), custom_call_target="tpu_custom_call" | custom-call | flops 1000000000 | bytes 10000000 | tf_op jit(solution)/shard_map/pallas_call | solution.py:217
  4.0 0.0 copy-start.8
  4.0 0.0 copy-start.7
  4.0 10.1 %all-to-all-start = ((f32[8,1,1280]{2,1,0:T(1,128)}), f32[8,1,1280]{2,1,0:T(1,128)S(1)}, u32[]{:S(2)}, u32[]{:S(2)}) async-start(f32[8,1,1280]{2,1,0:T(1,128)} %get-tuple-element.20), calls=%async_computation | async-start | bytes 81920 | tf_op jit(solution)/shard_map/all_to_all | solution.py:229
  14.1 0.0 copy-done.8
  14.1 1.9 %collective-permute-start = (bf16[64,256]{1,0:T(8,128)(2,1)S(1)}, bf16[64,256]{1,0:T(8,128)(2,1)S(1)}, u32[]{:S(2)}, u32[]{:S(2)}) collective-permute-start(bf16[64,256]{1,0:T(8,128)(2,1)S(1)} %copy-done.8), channel_id=1, source_target_pairs={{0,1},{1,0},{2,3},{3,2},{4,5},{5,4},{6,7},{7,6},{8,9},{9,8},{10,11... | collective-permute-start | bytes 98312 | tf_op jit(solution)/shard_map/ppermute | solution.py:275
  16.0 0.0 copy-done.7
  16.0 6.8 %collective-permute-start.1 = (bf16[64,256]{1,0:T(8,128)(2,1)S(1)}, bf16[64,256]{1,0:T(8,128)(2,1)S(1)}, u32[]{:S(2)}, u32[]{:S(2)}) collective-permute-start(bf16[64,256]{1,0:T(8,128)(2,1)S(1)} %copy-done.7), channel_id=1, source_target_pairs={{1,2},{2,1},{3,4},{4,3},{5,6},{6,5},{7,8},{8,7},{9,10},{10,9},{11,... | collective-permute-start | bytes 98312 | tf_op jit(solution)/shard_map/ppermute | solution.py:276
  22.9 0.0 all-to-all-done
  22.9 0.6 reshape.118
  23.6 0.0 copy-start.4
  23.6 7.0 %all-to-all-start.1 = ((f32[8,1,1280]{2,1,0:T(1,128)}), f32[8,1,1280]{2,1,0:T(1,128)S(1)}, u32[]{:S(2)}, u32[]{:S(2)}) async-start(f32[8,1,1280]{2,1,0:T(1,128)} %reshape.118), calls=%async_computation.1 | async-start | bytes 81920 | tf_op jit(solution)/shard_map/all_to_all | solution.py:235
  30.5 0.0 copy-start.5
  30.6 0.0 copy-done.4
  30.6 0.7 copy-done.5
  31.2 0.0 copy-start.1
  31.2 0.0 copy-start.2
  31.2 2.0 %shard_map.113.hits_ref = bf16[640,512]{1,0:T(8,128)(2,1)S(1)} custom-call(s32[16,512]{1,0:T(8,128)S(1)} %bitcast.15, s32[1,512]{1,0:T(1,128)S(1)} %bitcast.16), custom_call_target="tpu_custom_call" | custom-call | flops 1000000000 | bytes 10000000 | tf_op jit(solution)/shard_map/pallas_call | solution.py:217
  33.2 0.0 copy-start.6
  33.2 0.0 collective-permute-done.first_ref
  33.2 0.0 collective-permute-done.1.second_ref
  33.3 0.0 copy-done.1
  33.3 0.0 copy-done.2
  33.3 0.6 copy-done.6
  33.9 0.0 copy-start.3
  33.9 0.7 shard_map.114
  34.6 0.0 copy-start
  34.6 2.9 %all-to-all-done.1 = f32[8,1,1280]{2,1,0:T(1,128)S(1)} async-done(((f32[8,1,1280]{2,1,0:T(1,128)}), f32[8,1,1280]{2,1,0:T(1,128)S(1)}, u32[]{:S(2)}, u32[]{:S(2)}) %all-to-all-start.1) | async-done | bytes 40992 | tf_op jit(solution)/shard_map/all_to_all | solution.py:235
  37.6 9.9 %all_to_all.76 = f32[8,1,1280]{2,1,0:T(1,128)S(1)} all-to-all(f32[8,1,1280]{2,1,0:T(1,128)S(1)} %reshape.121), channel_id=1, replica_groups=mesh['x'=4,'y'=8,'c'=2,'z'=8] {'z'}, dimensions={0} | all-to-all | bytes 81920 | tf_op jit(solution)/shard_map/all_to_all | solution.py:235
  47.6 12.8 %all_to_all.77.packed_ref = f32[8,1,1280]{2,1,0:T(1,128)S(1)} all-to-all(f32[8,1,1280]{2,1,0:T(1,128)S(1)} %reshape.122), channel_id=1, replica_groups=mesh['x'=4,'y'=8,'c'=2,'z'=8] {'x','c'}, dimensions={0} | all-to-all | bytes 81920 | tf_op jit(solution)/shard_map/all_to_all | solution.py:235
  60.4 0.0 copy-done.3
  60.4 0.0 copy-done
  60.4 2.7 %shard_map.115 = (bf16[512,256]{1,0:T(8,128)(2,1)}, f32[512,256]{1,0:T(8,128)S(1)}, f32[8,1,1280]{2,1,0:T(1,128)S(1)}, f32[2,256,256]{2,1,0:T(8,128)S(1)}, f32[1,256]{1,0:T(1,128)S(1)}) custom-call(s32[1,1]{1,0:T(1,128)} %bitcast.10.count_ref, f32[8,1,1280]{2,1,0:T(1,128)S(1)} %all_to_all.77.packed_ref, bf16[512,256]{1,0:T(8,128)(2,1)S(1)} %copy-done.2, ...), custom_call_target="tpu_custom_call" | custom-call | flops 1000000000 | bytes 10000000 | tf_op jit(solution)/shard_map/pallas_call | solution.py:217
  63.1 7.8 %all_to_all.78 = f32[8,1,1280]{2,1,0:T(1,128)S(1)} all-to-all(f32[8,1,1280]{2,1,0:T(1,128)S(1)} %get-tuple-element.31), channel_id=1, replica_groups=mesh['x'=4,'y'=8,'c'=2,'z'=8] {'x','c'}, dimensions={0} | all-to-all | bytes 81920 | tf_op jit(solution)/shard_map/all_to_all | solution.py:229
  71.0 9.6 %all_to_all.79 = f32[8,1,1280]{2,1,0:T(1,128)S(1)} all-to-all(f32[8,1,1280]{2,1,0:T(1,128)S(1)} %reshape.123), channel_id=1, replica_groups=mesh['x'=4,'y'=8,'c'=2,'z'=8] {'y'}, dimensions={0} | all-to-all | bytes 81920 | tf_op jit(solution)/shard_map/all_to_all | solution.py:235
  80.7 9.3 %all_to_all.80 = f32[8,1,1280]{2,1,0:T(1,128)S(1)} all-to-all(f32[8,1,1280]{2,1,0:T(1,128)S(1)} %reshape.124), channel_id=1, replica_groups=mesh['x'=4,'y'=8,'c'=2,'z'=8] {'z'}, dimensions={0} | all-to-all | bytes 81920 | tf_op jit(solution)/shard_map/all_to_all | solution.py:235
  90.1 10.4 %all_to_all.81.packed_ref = f32[8,1,1280]{2,1,0:T(1,128)S(1)} all-to-all(f32[8,1,1280]{2,1,0:T(1,128)S(1)} %reshape.125), channel_id=1, replica_groups=mesh['x'=4,'y'=8,'c'=2,'z'=8] {'x','c'}, dimensions={0} | all-to-all | bytes 81920 | tf_op jit(solution)/shard_map/all_to_all | solution.py:235
  100.6 1.2 shard_map.116
  101.8 4.9 %all_to_all.82 = f32[2,512,256]{2,1,0:T(8,128)S(1)} all-to-all(f32[2,512,256]{2,1,0:T(8,128)S(1)} %bitcast.12), channel_id=1, replica_groups=mesh['x'=4,'y'=8,'c'=2,'z'=8] {'c'}, dimensions={0} | all-to-all | bytes 2097152 | tf_op jit(solution)/shard_map/all_to_all | solution.py:229
  106.7 0.1 reduce_sum.93
  106.8 17.9 %all_to_all.83 = f32[32,16,256]{2,1,0:T(8,128)S(1)} all-to-all(f32[32,16,256]{2,1,0:T(8,128)S(1)} %bitcast.19), channel_id=1, replica_groups=mesh['x'=4,'y'=8,'c'=2,'z'=8] {'x','z'}, dimensions={0} | all-to-all | bytes 1048576 | tf_op jit(solution)/shard_map/all_to_all | solution.py:229
  124.8 10.3 %all_to_all.84 = f32[8,16,256]{2,1,0:T(8,128)S(1)} all-to-all(f32[8,16,256]{2,1,0:T(8,128)S(1)} %broadcast_in_dim.14), channel_id=1, replica_groups=mesh['x'=4,'y'=8,'c'=2,'z'=8] {'y'}, dimensions={0} | all-to-all | bytes 262144 | tf_op jit(solution)/shard_map/all_to_all | solution.py:235
  135.1 0.1 broadcast_in_dim.15
  135.2 20.3 %all_to_all.85 = f32[32,16,256]{2,1,0:T(8,128)S(1)} all-to-all(f32[32,16,256]{2,1,0:T(8,128)S(1)} %broadcast_in_dim.15), channel_id=1, replica_groups=mesh['x'=4,'y'=8,'c'=2,'z'=8] {'x','z'}, dimensions={0} | all-to-all | bytes 1048576 | tf_op jit(solution)/shard_map/all_to_all | solution.py:235
  155.4 0.1 broadcast_in_dim.17
  155.5 9.2 %all_to_all.86 = f32[2,512,256]{2,1,0:T(8,128)S(1)} all-to-all(f32[2,512,256]{2,1,0:T(8,128)S(1)} %broadcast_in_dim.17), channel_id=1, replica_groups=mesh['x'=4,'y'=8,'c'=2,'z'=8] {'c'}, dimensions={0} | all-to-all | bytes 2097152 | tf_op jit(solution)/shard_map/all_to_all | solution.py:235
  164.7 1.0 shard_map.117
  (19 shorter events, 0.5 us)
Async XLA Ops:
  4.0 10.1 %copy-start.8 = (bf16[64,256]{1,0:T(8,128)(2,1)S(1)}, bf16[64,256]{1,0:T(8,128)(2,1)}, u32[]{:S(2)}) copy-start(bf16[64,256]{1,0:T(8,128)(2,1)} %get-tuple-element.23) | copy-start | bytes 98308
  4.0 12.0 %copy-start.7 = (bf16[64,256]{1,0:T(8,128)(2,1)S(1)}, bf16[64,256]{1,0:T(8,128)(2,1)}, u32[]{:S(2)}) copy-start(bf16[64,256]{1,0:T(8,128)(2,1)} %get-tuple-element.24) | copy-start | bytes 98308
  4.0 18.9 %all-to-all-start = ((f32[8,1,1280]{2,1,0:T(1,128)}), f32[8,1,1280]{2,1,0:T(1,128)S(1)}, u32[]{:S(2)}, u32[]{:S(2)}) async-start(f32[8,1,1280]{2,1,0:T(1,128)} %get-tuple-element.20), calls=%async_computation | async-start | bytes 81920 | tf_op jit(solution)/shard_map/all_to_all | solution.py:229
  14.1 19.1 %collective-permute-start = (bf16[64,256]{1,0:T(8,128)(2,1)S(1)}, bf16[64,256]{1,0:T(8,128)(2,1)S(1)}, u32[]{:S(2)}, u32[]{:S(2)}) collective-permute-start(bf16[64,256]{1,0:T(8,128)(2,1)S(1)} %copy-done.8), channel_id=1, source_target_pairs={{0,1},{1,0},{2,3},{3,2},{4,5},{5,4},{6,7},{7,6},{8,9},{9,8},{10,11... | collective-permute-start | bytes 98312 | tf_op jit(solution)/shard_map/ppermute | solution.py:275
  16.0 17.2 %collective-permute-start.1 = (bf16[64,256]{1,0:T(8,128)(2,1)S(1)}, bf16[64,256]{1,0:T(8,128)(2,1)S(1)}, u32[]{:S(2)}, u32[]{:S(2)}) collective-permute-start(bf16[64,256]{1,0:T(8,128)(2,1)S(1)} %copy-done.7), channel_id=1, source_target_pairs={{1,2},{2,1},{3,4},{4,3},{5,6},{6,5},{7,8},{8,7},{9,10},{10,9},{11,... | collective-permute-start | bytes 98312 | tf_op jit(solution)/shard_map/ppermute | solution.py:276
  23.6 7.0 %copy-start.4 = (s32[512,16]{0,1:T(8,128)S(1)}, s32[512,16]{0,1:T(8,128)}, u32[]{:S(2)}) copy-start(s32[512,16]{0,1:T(8,128)} %param.16) | copy-start | bytes 98308
  23.6 13.9 %all-to-all-start.1 = ((f32[8,1,1280]{2,1,0:T(1,128)}), f32[8,1,1280]{2,1,0:T(1,128)S(1)}, u32[]{:S(2)}, u32[]{:S(2)}) async-start(f32[8,1,1280]{2,1,0:T(1,128)} %reshape.118), calls=%async_computation.1 | async-start | bytes 81920 | tf_op jit(solution)/shard_map/all_to_all | solution.py:235
  30.5 0.7 copy-start.5
  31.2 2.0 %copy-start.1 = (bf16[512,256]{1,0:T(8,128)(2,1)S(1)}, bf16[512,256]{1,0:T(8,128)(2,1)}, u32[]{:S(2)}) copy-start(bf16[512,256]{1,0:T(8,128)(2,1)} %grad_ref.1) | copy-start | bytes 786436
  31.2 2.0 %copy-start.2 = (bf16[512,256]{1,0:T(8,128)(2,1)S(1)}, bf16[512,256]{1,0:T(8,128)(2,1)}, u32[]{:S(2)}) copy-start(bf16[512,256]{1,0:T(8,128)(2,1)} %feats_ref.5) | copy-start | bytes 786436
  33.2 0.7 copy-start.6
  33.9 26.5 %copy-start.3 = (bf16[256,256]{1,0:T(8,128)(2,1)S(1)}, bf16[256,256]{1,0:T(8,128)(2,1)}, u32[]{:S(2)}) copy-start(bf16[256,256]{1,0:T(8,128)(2,1)} %wg_ref.1) | copy-start | bytes 393220
  34.6 25.8 %copy-start = (bf16[3,256,256]{2,1,0:T(8,128)(2,1)S(1)}, bf16[3,256,256]{2,1,0:T(8,128)(2,1)}, u32[]{:S(2)}) copy-start(bf16[3,256,256]{2,1,0:T(8,128)(2,1)} %w_ref.3) | copy-start | bytes 1179652

commit v8 on v7

--- a/solution.py
+++ b/solution.py
@@ -101,7 +101,7 @@
     store_packed(packed_ref, kv, [jnp.sum(key_map, axis=0, keepdims=True), live])
 
 
-def hit_kernel(nbr_ref, count_ref, hits_ref):
+def count_hits(nbr_ref, count_ref, hits_ref):
     wide, total = hits_ref.shape
     slots = nbr_ref.shape[0]
     sub = 32
@@ -126,7 +126,10 @@
         lax.fori_loop(0, wide // sub, body, 0)
 
 
-def graph_kernel(hits_ref, feats_ref, first_ref, second_ref, grad_ref, gain_ref, held_ref, gain_out_ref):
+def graph_kernel(
+    nbr_ref, count_ref, feats_ref, first_ref, second_ref, grad_ref, gain_ref, held_ref, gain_out_ref, hits_ref
+):
+    count_hits(nbr_ref, count_ref, hits_ref)
     total = feats_ref.shape[0]
     rim = first_ref.shape[0]
     odd = lax.axis_index("z") % 2 == 1
@@ -276,10 +279,10 @@
     second = lax.ppermute(second, FINE, cross)
     share = scatter_sum(packed, ("x", "c"), near)
     share, named = together((share, neighbours))
-    hits = call(hit_kernel, shape((rows + 2 * rim, rows), bf16), named.T, neighbour_counts.reshape(1, rows))
     held, gain = call(
         graph_kernel, [shape((2, rows, D), bf16), shape((1, D), f32)],
-        hits, node_feats, first, second, out_grad, ln_gain.reshape(1, D),
+        named.T, neighbour_counts.reshape(1, rows), node_feats, first, second, out_grad, ln_gain.reshape(1, D),
+        scratch=[pltpu.VMEM((rows + 2 * rim, rows), bf16)],
     )
     share = gather_sum(share, "y", sizes["y"])
     share, held, gain = together((share, held, gain))

time: 167 us -> 166 us (level)
    pallas_call x6 -> x5, Pallas kernels: 10.2 us -> 10.2 us  [call(): pl.pallas_call(kernel, in_specs=[far if i in away else near for i in rang...]
where the time goes in v8:
time: 166 us; the launch traced here: 165 us
  blocking collectives  122 us (73%)
  starting transfers between devices  25.9 us (16%)
  Pallas kernels  10.2 us (6%)
  waiting for transfers between devices  3.6 us (2%)
    all_to_all x8, blocking collectives, gather(): return lax.all_to_all(copies, axes, 0, 0, tiled=True)  91.3 us
    all_to_all x3, blocking collectives, scatter_sum(): parts = lax.all_to_all(value, axes, 0, 0, tiled=True)  30.7 us
    pallas_call x5, Pallas kernels, call(): pl.pallas_call(kernel, in_specs=[far if i in away else near for i in rang...  10.2 us
    all_to_all x1, starting transfers between devices, scatter_sum(): parts = lax.all_to_all(value, axes, 0, 0, tiled=True)  10.2 us
    all_to_all x1, starting transfers between devices, gather(): return lax.all_to_all(copies, axes, 0, 0, tiled=True)  6.95 us
    ppermute x1, starting transfers between devices, local(): second = lax.ppermute(second, FINE, cross)  6.81 us
    all_to_all x1, waiting for transfers between devices, gather(): return lax.all_to_all(copies, axes, 0, 0, tiled=True)  3.59 us
  transfers between devices with their start and end apart: 4, of which 1 were waited for; matrix products, arithmetic and copies ran while one was open for 0% of the time, Pallas kernels for 2%

profile of v8, /device:TPU:1, one launch (start us, length us, event | category | flops | bytes accessed | tf_op | source)
XLA Modules:
  0.0 165.3 jit_solution(15421181541185442191)
XLA Ops:
  1.3 0.0 copy-start.2
  1.3 2.7 %shard_map.112 = (f32[8,1,1280]{2,1,0:T(1,128)}, bf16[64,256]{1,0:T(8,128)(2,1)}, bf16[64,256]{1,0:T(8,128)(2,1)}) custom-call(s32[1,1]{1,0:T(1,128)} %bitcast.9.count_ref, bf16[512,256]{1,0:T(8,128)(2,1)} %feats_ref.5, bf16[3,256,256]{2,1,0:T(8,128)(2,1)} %w_ref.3, s32[1,2,64]{2,1,0:T(2,128)} %send_hbm.1), custom_call_target="tpu_custom_call" | custom-call | flops 1000000000 | bytes 10000000 | tf_op jit(solution)/shard_map/pallas_call | solution.py:220
  4.0 0.0 copy-start.1
  4.0 10.2 %all-to-all-start = ((f32[8,1,1280]{2,1,0:T(1,128)}), f32[8,1,1280]{2,1,0:T(1,128)S(1)}, u32[]{:S(2)}, u32[]{:S(2)}) async-start(f32[8,1,1280]{2,1,0:T(1,128)} %get-tuple-element.20), calls=%async_computation | async-start | bytes 81920 | tf_op jit(solution)/shard_map/all_to_all | solution.py:232
  14.3 1.9 %collective-permute-start = (bf16[64,256]{1,0:T(8,128)(2,1)}, bf16[64,256]{1,0:T(8,128)(2,1)S(1)}, u32[]{:S(2)}, u32[]{:S(2)}) collective-permute-start(bf16[64,256]{1,0:T(8,128)(2,1)} %get-tuple-element.23), channel_id=1, source_target_pairs={{0,1},{1,0},{2,3},{3,2},{4,5},{5,4},{6,7},{7,6},{8,9},{9,8},{10,11... | collective-permute-start | bytes 98312 | tf_op jit(solution)/shard_map/ppermute | solution.py:278
  16.2 6.8 %collective-permute-start.1 = (bf16[64,256]{1,0:T(8,128)(2,1)}, bf16[64,256]{1,0:T(8,128)(2,1)S(1)}, u32[]{:S(2)}, u32[]{:S(2)}) collective-permute-start(bf16[64,256]{1,0:T(8,128)(2,1)} %get-tuple-element.24), channel_id=1, source_target_pairs={{1,2},{2,1},{3,4},{4,3},{5,6},{6,5},{7,8},{8,7},{9,10},{10,9},{11,... | collective-permute-start | bytes 98312 | tf_op jit(solution)/shard_map/ppermute | solution.py:279
  23.0 0.0 all-to-all-done
  23.1 0.6 reshape.118
  23.7 0.0 copy-start.4
  23.7 7.0 %all-to-all-start.1 = ((f32[8,1,1280]{2,1,0:T(1,128)}), f32[8,1,1280]{2,1,0:T(1,128)S(1)}, u32[]{:S(2)}, u32[]{:S(2)}) async-start(f32[8,1,1280]{2,1,0:T(1,128)} %reshape.118), calls=%async_computation.1 | async-start | bytes 81920 | tf_op jit(solution)/shard_map/all_to_all | solution.py:238
  30.7 0.0 collective-permute-done.first_ref
  30.7 0.0 collective-permute-done.1.second_ref
  30.7 0.0 copy-start.5
  30.7 0.0 copy-start.6
  30.7 0.0 copy-done.2
  30.7 0.0 copy-done.1
  30.7 0.0 copy-done.4
  30.8 0.6 copy-done.5
  31.4 0.0 copy-done.6
  31.4 0.0 copy-start.3
  31.4 2.6 %shard_map.113 = (bf16[2,512,256]{2,1,0:T(8,128)(2,1)S(1)}, f32[1,256]{1,0:T(1,128)S(1)}) custom-call(s32[16,512]{1,0:T(8,128)S(1)} %bitcast.15, s32[1,512]{1,0:T(1,128)S(1)} %bitcast.16, bf16[512,256]{1,0:T(8,128)(2,1)S(1)} %copy-done.2, bf16[64,256]{1,0:T(8,128)(2,1)S(1)} %collective-permute-done.first_ref, ...), custom_call_target="tpu_custom_call" | custom-call | flops 1000000000 | bytes 10000000 | tf_op jit(solution)/shard_map/pallas_call | solution.py:220
  34.1 0.0 copy-start
  34.1 3.6 %all-to-all-done.1 = f32[8,1,1280]{2,1,0:T(1,128)S(1)} async-done(((f32[8,1,1280]{2,1,0:T(1,128)}), f32[8,1,1280]{2,1,0:T(1,128)S(1)}, u32[]{:S(2)}, u32[]{:S(2)}) %all-to-all-start.1) | async-done | bytes 40992 | tf_op jit(solution)/shard_map/all_to_all | solution.py:238
  37.8 10.0 %all_to_all.76 = f32[8,1,1280]{2,1,0:T(1,128)S(1)} all-to-all(f32[8,1,1280]{2,1,0:T(1,128)S(1)} %reshape.121), channel_id=1, replica_groups=mesh['x'=4,'y'=8,'c'=2,'z'=8] {'z'}, dimensions={0} | all-to-all | bytes 81920 | tf_op jit(solution)/shard_map/all_to_all | solution.py:238
  47.8 12.8 %all_to_all.77.packed_ref = f32[8,1,1280]{2,1,0:T(1,128)S(1)} all-to-all(f32[8,1,1280]{2,1,0:T(1,128)S(1)} %reshape.122), channel_id=1, replica_groups=mesh['x'=4,'y'=8,'c'=2,'z'=8] {'x','c'}, dimensions={0} | all-to-all | bytes 81920 | tf_op jit(solution)/shard_map/all_to_all | solution.py:238
  60.6 0.0 copy-done.3
  60.6 0.0 copy-done
  60.6 2.7 %shard_map.114 = (bf16[512,256]{1,0:T(8,128)(2,1)}, f32[512,256]{1,0:T(8,128)S(1)}, f32[8,1,1280]{2,1,0:T(1,128)S(1)}, f32[2,256,256]{2,1,0:T(8,128)S(1)}, f32[1,256]{1,0:T(1,128)S(1)}) custom-call(s32[1,1]{1,0:T(1,128)} %bitcast.10.count_ref, f32[8,1,1280]{2,1,0:T(1,128)S(1)} %all_to_all.77.packed_ref, bf16[512,256]{1,0:T(8,128)(2,1)S(1)} %copy-done.2, ...), custom_call_target="tpu_custom_call" | custom-call | flops 1000000000 | bytes 10000000 | tf_op jit(solution)/shard_map/pallas_call | solution.py:220
  63.3 7.8 %all_to_all.78 = f32[8,1,1280]{2,1,0:T(1,128)S(1)} all-to-all(f32[8,1,1280]{2,1,0:T(1,128)S(1)} %get-tuple-element.31), channel_id=1, replica_groups=mesh['x'=4,'y'=8,'c'=2,'z'=8] {'x','c'}, dimensions={0} | all-to-all | bytes 81920 | tf_op jit(solution)/shard_map/all_to_all | solution.py:232
  71.2 9.4 %all_to_all.79 = f32[8,1,1280]{2,1,0:T(1,128)S(1)} all-to-all(f32[8,1,1280]{2,1,0:T(1,128)S(1)} %reshape.123), channel_id=1, replica_groups=mesh['x'=4,'y'=8,'c'=2,'z'=8] {'y'}, dimensions={0} | all-to-all | bytes 81920 | tf_op jit(solution)/shard_map/all_to_all | solution.py:238
  80.7 9.3 %all_to_all.80 = f32[8,1,1280]{2,1,0:T(1,128)S(1)} all-to-all(f32[8,1,1280]{2,1,0:T(1,128)S(1)} %reshape.124), channel_id=1, replica_groups=mesh['x'=4,'y'=8,'c'=2,'z'=8] {'z'}, dimensions={0} | all-to-all | bytes 81920 | tf_op jit(solution)/shard_map/all_to_all | solution.py:238
  90.1 10.1 %all_to_all.81.packed_ref = f32[8,1,1280]{2,1,0:T(1,128)S(1)} all-to-all(f32[8,1,1280]{2,1,0:T(1,128)S(1)} %reshape.125), channel_id=1, replica_groups=mesh['x'=4,'y'=8,'c'=2,'z'=8] {'x','c'}, dimensions={0} | all-to-all | bytes 81920 | tf_op jit(solution)/shard_map/all_to_all | solution.py:238
  100.2 1.2 shard_map.115
  101.4 4.9 %all_to_all.82 = f32[2,512,256]{2,1,0:T(8,128)S(1)} all-to-all(f32[2,512,256]{2,1,0:T(8,128)S(1)} %bitcast.12), channel_id=1, replica_groups=mesh['x'=4,'y'=8,'c'=2,'z'=8] {'c'}, dimensions={0} | all-to-all | bytes 2097152 | tf_op jit(solution)/shard_map/all_to_all | solution.py:232
  106.3 0.1 reduce_sum.93
  106.4 17.9 %all_to_all.83 = f32[32,16,256]{2,1,0:T(8,128)S(1)} all-to-all(f32[32,16,256]{2,1,0:T(8,128)S(1)} %bitcast.19), channel_id=1, replica_groups=mesh['x'=4,'y'=8,'c'=2,'z'=8] {'x','z'}, dimensions={0} | all-to-all | bytes 1048576 | tf_op jit(solution)/shard_map/all_to_all | solution.py:232
  124.4 10.3 %all_to_all.84 = f32[8,16,256]{2,1,0:T(8,128)S(1)} all-to-all(f32[8,16,256]{2,1,0:T(8,128)S(1)} %broadcast_in_dim.14), channel_id=1, replica_groups=mesh['x'=4,'y'=8,'c'=2,'z'=8] {'y'}, dimensions={0} | all-to-all | bytes 262144 | tf_op jit(solution)/shard_map/all_to_all | solution.py:238
  134.7 0.1 broadcast_in_dim.15
  134.8 20.3 %all_to_all.85 = f32[32,16,256]{2,1,0:T(8,128)S(1)} all-to-all(f32[32,16,256]{2,1,0:T(8,128)S(1)} %broadcast_in_dim.15), channel_id=1, replica_groups=mesh['x'=4,'y'=8,'c'=2,'z'=8] {'x','z'}, dimensions={0} | all-to-all | bytes 1048576 | tf_op jit(solution)/shard_map/all_to_all | solution.py:238
  155.0 0.1 broadcast_in_dim.17
  155.1 9.2 %all_to_all.86 = f32[2,512,256]{2,1,0:T(8,128)S(1)} all-to-all(f32[2,512,256]{2,1,0:T(8,128)S(1)} %broadcast_in_dim.17), channel_id=1, replica_groups=mesh['x'=4,'y'=8,'c'=2,'z'=8] {'c'}, dimensions={0} | all-to-all | bytes 2097152 | tf_op jit(solution)/shard_map/all_to_all | solution.py:238
  164.3 1.0 shard_map.116
  (19 shorter events, 0.5 us)
Async XLA Ops:
  1.3 29.5 %copy-start.2 = (bf16[512,256]{1,0:T(8,128)(2,1)S(1)}, bf16[512,256]{1,0:T(8,128)(2,1)}, u32[]{:S(2)}) copy-start(bf16[512,256]{1,0:T(8,128)(2,1)} %feats_ref.5) | copy-start | bytes 786436
  4.0 26.7 %copy-start.1 = (bf16[512,256]{1,0:T(8,128)(2,1)S(1)}, bf16[512,256]{1,0:T(8,128)(2,1)}, u32[]{:S(2)}) copy-start(bf16[512,256]{1,0:T(8,128)(2,1)} %grad_ref.1) | copy-start | bytes 786436
  4.0 19.0 %all-to-all-start = ((f32[8,1,1280]{2,1,0:T(1,128)}), f32[8,1,1280]{2,1,0:T(1,128)S(1)}, u32[]{:S(2)}, u32[]{:S(2)}) async-start(f32[8,1,1280]{2,1,0:T(1,128)} %get-tuple-element.20), calls=%async_computation | async-start | bytes 81920 | tf_op jit(solution)/shard_map/all_to_all | solution.py:232
  14.3 16.4 %collective-permute-start = (bf16[64,256]{1,0:T(8,128)(2,1)}, bf16[64,256]{1,0:T(8,128)(2,1)S(1)}, u32[]{:S(2)}, u32[]{:S(2)}) collective-permute-start(bf16[64,256]{1,0:T(8,128)(2,1)} %get-tuple-element.23), channel_id=1, source_target_pairs={{0,1},{1,0},{2,3},{3,2},{4,5},{5,4},{6,7},{7,6},{8,9},{9,8},{10,11... | collective-permute-start | bytes 98312 | tf_op jit(solution)/shard_map/ppermute | solution.py:278
  16.2 14.5 %collective-permute-start.1 = (bf16[64,256]{1,0:T(8,128)(2,1)}, bf16[64,256]{1,0:T(8,128)(2,1)S(1)}, u32[]{:S(2)}, u32[]{:S(2)}) collective-permute-start(bf16[64,256]{1,0:T(8,128)(2,1)} %get-tuple-element.24), channel_id=1, source_target_pairs={{1,2},{2,1},{3,4},{4,3},{5,6},{6,5},{7,8},{8,7},{9,10},{10,9},{11,... | collective-permute-start | bytes 98312 | tf_op jit(solution)/shard_map/ppermute | solution.py:279
  23.7 7.0 %copy-start.4 = (s32[512,16]{0,1:T(8,128)S(1)}, s32[512,16]{0,1:T(8,128)}, u32[]{:S(2)}) copy-start(s32[512,16]{0,1:T(8,128)} %param.16) | copy-start | bytes 98308
  23.7 13.9 %all-to-all-start.1 = ((f32[8,1,1280]{2,1,0:T(1,128)}), f32[8,1,1280]{2,1,0:T(1,128)S(1)}, u32[]{:S(2)}, u32[]{:S(2)}) async-start(f32[8,1,1280]{2,1,0:T(1,128)} %reshape.118), calls=%async_computation.1 | async-start | bytes 81920 | tf_op jit(solution)/shard_map/all_to_all | solution.py:238
  30.7 0.7 copy-start.5
  30.7 0.7 copy-start.6
  31.4 29.2 %copy-start.3 = (bf16[256,256]{1,0:T(8,128)(2,1)S(1)}, bf16[256,256]{1,0:T(8,128)(2,1)}, u32[]{:S(2)}) copy-start(bf16[256,256]{1,0:T(8,128)(2,1)} %wg_ref.1) | copy-start | bytes 393220
  34.1 26.5 %copy-start = (bf16[3,256,256]{2,1,0:T(8,128)(2,1)S(1)}, bf16[3,256,256]{2,1,0:T(8,128)(2,1)}, u32[]{:S(2)}) copy-start(bf16[3,256,256]{2,1,0:T(8,128)(2,1)} %w_ref.3) | copy-start | bytes 1179652
